TPU v7x, 512 devices: a whole 4x4x16 slice. The times are simulated.
512 devices in a mesh: leaf: 32 (over z, core), front: 16 (over y, x).
Axes of the slice: x: 4, y: 4, z: 16, core: 2. Of those that a mesh axis runs over, the one named last changes fastest.
Arguments:
- forcing: bfloat16 [32, 10240, 128], P('leaf', 'front'), may hold values from -6 to 6
- live: int32 [2, 32], replicated, may hold values from 40 to 80, as said below
- lower_inv: bfloat16 [32, 10240, 960], P('leaf', 'front'), may hold values from -0.0625 to 0.0625
- lower_upd: bfloat16 [32, 10240, 640], P('leaf', 'front'), may hold values from -0.0625 to 0.0625
- upper_inv: bfloat16 [32, 10240, 960], P('leaf', 'front'), may hold values from -0.0625 to 0.0625
- upper_upd: bfloat16 [32, 10240, 640], P('leaf', 'front'), may hold values from -0.0625 to 0.0625
Outputs:
- solution: bfloat16 [2, 32, 10240, 128], P(None, 'leaf', 'front')
Inputs may be any that keep to these rules, and one draw needn't show every extreme that they name: Entries (l, j) with j at or beyond 2**(1 - l) are not read. The root's separator is live in full.
All inputs are finite; a program needn't handle non-finite values.
Results may differ from a plain program's by a relative error of at most 0.008.
Values may be sent and summed in bfloat16 or wider, within the bound.
No kernel may reach another device: no remote copies, remote signals or barrier semaphores. Data moves between devices by JAX's collectives and lax.ppermute only.
A program may use at most 64 MiB of HBM per device.

v0:
```python
import jax
import jax.numpy as jnp
from jax import lax
from jax.sharding import PartitionSpec as P

BLK = 128
LEV = 2


def from_root(array, axis, root):
    mine = lax.axis_index(axis) == root
    return lax.psum(jnp.where(mine, array, jnp.zeros_like(array)), axis)


def partner(block, axis, bit):
    count = lax.axis_size(axis)
    route = []
    for low in range(count):
        high = low | 1 << bit
        if high != low and high < count:
            route += [(low, high), (high, low)]
    return lax.ppermute(block, axis, route)


def body(forcing, live, lower_inv, lower_upd, upper_inv, upper_upd):
    n_leaf = lax.axis_size("leaf")
    sep_dev = forcing.shape[1]
    n_rhs = forcing.shape[2]
    sep = sep_dev * lax.axis_size("front")
    skip = n_leaf.bit_length() - LEV
    leaf_id = lax.axis_index("leaf")
    front_id = lax.axis_index("front")
    rows = front_id * sep_dev + jnp.arange(sep_dev)
    first = 2 * (sep >> skip)

    def level_mask(level):
        count = live[level][leaf_id >> level + skip]
        return (rows < count * BLK).astype(jnp.float32)[:, None]

    def fetch(block, level, residual_kind):
        depth = level + skip
        width = sep >> depth
        start = (leaf_id & (1 << depth) - 1) * width
        owner = start // sep_dev
        if residual_kind:
            piece = from_root(block, "front", owner)
        else:
            piece = from_root(block, "front", owner)
        return lax.dynamic_slice_in_dim(piece, start % sep_dev, width, 0)

    def subtree_total(partial_value, depth):
        for bit in range(depth):
            partial_value = partial_value + partner(partial_value, "leaf", bit)
        return partial_value

    residual = subtree_total(forcing[0].astype(jnp.float32), skip)
    forward = []
    for level in range(LEV):
        depth = level + skip
        width = sep >> depth
        offset = first - 2 * width
        mask = level_mask(level)
        masked = (mask * residual).astype(jnp.bfloat16)
        picked = fetch(masked, level, True)
        y_term = jnp.dot(
            lower_inv[0, :, offset : offset + width], picked, preferred_element_type=jnp.float32
        )
        if level < LEV - 1:
            c_term = jnp.dot(
                lower_upd[0, :, offset : offset + width], picked, preferred_element_type=jnp.float32
            )
            summed = subtree_total(jnp.concatenate([y_term, -c_term], 0), depth)
            y_sum = summed[:sep_dev]
            loads = summed[sep_dev:]
            residual = loads + partner(loads, "leaf", depth)
        else:
            y_sum = subtree_total(y_term, depth)
        forward.append((mask * y_sum).astype(jnp.bfloat16))
    results = [None] * LEV
    above = None
    for level in reversed(range(LEV)):
        depth = level + skip
        width = sep >> depth
        offset = first - 2 * width
        mask = level_mask(level)
        if above is None:
            picked = fetch(forward[level], level, False)
            term = jnp.dot(
                upper_inv[0, :, offset : offset + width], picked, preferred_element_type=jnp.float32
            )
        else:
            picked = fetch(jnp.concatenate([forward[level], above], 1), level, False)
            term = jnp.dot(
                upper_inv[0, :, offset : offset + width],
                picked[:, :n_rhs],
                preferred_element_type=jnp.float32,
            )
            term = term - jnp.dot(
                upper_upd[0, :, offset : offset + width],
                picked[:, n_rhs:],
                preferred_element_type=jnp.float32,
            )
        solved = (mask * subtree_total(term, depth)).astype(jnp.bfloat16)
        results[level] = solved
        above = solved
    return jnp.stack(results)[:, None]


def solution(mesh):
    return jax.shard_map(
        body,
        mesh=mesh,
        in_specs=(
            P("leaf", "front", None),
            P(),
            P("leaf", "front", None),
            P("leaf", "front", None),
            P("leaf", "front", None),
            P("leaf", "front", None),
        ),
        out_specs=P(None, "leaf", "front", None),
        check_vma=False,
    )
```

profile of v0, /device:TPU:1, one launch (start us, length us, event | category | flops | bytes accessed | tf_op | source)
XLA Modules:
  0.0 972.4 jit_solution(18222243295650057958)
XLA Ops:
  7.7 8.8 collective-permute-start
  17.8 1.9 collective-permute-start.1
  19.7 8.9 collective-permute-done.1
  28.7 2.1 collective-permute-start.2
  30.7 17.4 %collective-permute-done.2 = f32[640,128]{0,1:T(8,128)S(1)} collective-permute-done((f32[640,128]{0,1:T(8,128)S(1)}, f32[640,128]{0,1:T(8,128)S(1)}, u32[]{:S(2)}, u32[]{:S(2)}) %collective-permute-start.2) | collective-permute-done | bytes 327712 | tf_op jit(solution)/shard_map/ppermute | solution.py:22
  48.2 3.5 collective-permute-start.3
  53.1 29.1 %collective-permute-done.3 = f32[640,128]{0,1:T(8,128)S(1)} collective-permute-done((f32[640,128]{0,1:T(8,128)S(1)}, f32[640,128]{0,1:T(8,128)S(1)}, u32[]{:S(2)}, u32[]{:S(2)}) %collective-permute-start.3) | collective-permute-done | bytes 327712 | tf_op jit(solution)/shard_map/ppermute | solution.py:22
  82.9 112.0 %all-reduce.5.cloned.1.call-done = bf16[640,128]{0,1:T(8,128)(2,1)} async-done(((bf16[640,128]{0,1:T(8,128)(2,1)}), bf16[640,128]{0,1:T(8,128)(2,1)}) %all-reduce.5.cloned.1.call-update) | async-done | bytes 163856 | tf_op jit(solution)/shard_map/psum | solution.py:12
  194.9 1.3 convolution_bitcast_fusion.2
  196.7 4.4 collective-permute-start.4
  201.1 1.7 collective-permute-done.4
  202.9 3.2 collective-permute-start.5
  206.1 14.7 %collective-permute-done.5 = f32[1280,128]{0,1:T(8,128)S(1)} collective-permute-done((f32[1280,128]{0,1:T(8,128)S(1)}, f32[1280,128]{0,1:T(8,128)S(1)}, u32[]{:S(2)}, u32[]{:S(2)}) %collective-permute-start.5) | collective-permute-done | bytes 655392 | tf_op jit(solution)/shard_map/ppermute | solution.py:22
  220.8 4.2 collective-permute-start.6
  225.0 28.3 %collective-permute-done.6 = f32[1280,128]{0,1:T(8,128)S(1)} collective-permute-done((f32[1280,128]{0,1:T(8,128)S(1)}, f32[1280,128]{0,1:T(8,128)S(1)}, u32[]{:S(2)}, u32[]{:S(2)}) %collective-permute-start.6) | collective-permute-done | bytes 655392 | tf_op jit(solution)/shard_map/ppermute | solution.py:22
  253.3 7.4 collective-permute-start.7
  260.7 63.4 %collective-permute-done.7 = f32[1280,128]{0,1:T(8,128)S(1)} collective-permute-done((f32[1280,128]{0,1:T(8,128)S(1)}, f32[1280,128]{0,1:T(8,128)S(1)}, u32[]{:S(2)}, u32[]{:S(2)}) %collective-permute-start.7) | collective-permute-done | bytes 655392 | tf_op jit(solution)/shard_map/ppermute | solution.py:22
  324.2 11.1 %collective-permute-start.8 = (f32[640,128]{0,1:T(8,128)S(1)}, f32[640,128]{0,1:T(8,128)S(1)}, u32[]{:S(2)}, u32[]{:S(2)}) collective-permute-start(f32[640,128]{0,1:T(8,128)S(1)} %get-tuple-element.6), channel_id=1, source_target_pairs={{0,256},{256,0},{16,272},{272,16},{32,288},{288,32},{48,304},{304,... | collective-permute-start | bytes 983048 | tf_op jit(solution)/shard_map/ppermute | solution.py:22
  336.0 12.4 %collective-permute-done.8 = f32[640,128]{0,1:T(8,128)S(1)} collective-permute-done((f32[640,128]{0,1:T(8,128)S(1)}, f32[640,128]{0,1:T(8,128)S(1)}, u32[]{:S(2)}, u32[]{:S(2)}) %collective-permute-start.8) | collective-permute-done | bytes 327712 | tf_op jit(solution)/shard_map/ppermute | solution.py:22
  349.2 113.3 %all-reduce.7.cloned.1.call-done = bf16[640,128]{0,1:T(8,128)(2,1)} async-done(((bf16[640,128]{0,1:T(8,128)(2,1)}), bf16[640,128]{0,1:T(8,128)(2,1)}) %all-reduce.7.cloned.1.call-update) | async-done | bytes 163856 | tf_op jit(solution)/shard_map/psum | solution.py:12
  463.7 4.4 collective-permute-start.9
  469.4 3.2 collective-permute-start.10
  472.6 7.6 collective-permute-done.10
  480.3 4.2 collective-permute-start.11
  484.5 14.2 %collective-permute-done.11 = f32[640,128]{0,1:T(8,128)S(1)} collective-permute-done((f32[640,128]{0,1:T(8,128)S(1)}, f32[640,128]{0,1:T(8,128)S(1)}, u32[]{:S(2)}, u32[]{:S(2)}) %collective-permute-start.11) | collective-permute-done | bytes 327712 | tf_op jit(solution)/shard_map/ppermute | solution.py:22
  498.7 7.5 collective-permute-start.12
  506.2 28.2 %collective-permute-done.12 = f32[640,128]{0,1:T(8,128)S(1)} collective-permute-done((f32[640,128]{0,1:T(8,128)S(1)}, f32[640,128]{0,1:T(8,128)S(1)}, u32[]{:S(2)}, u32[]{:S(2)}) %collective-permute-start.12) | collective-permute-done | bytes 327712 | tf_op jit(solution)/shard_map/ppermute | solution.py:22
  534.5 18.2 %collective-permute-start.13 = (f32[640,128]{0,1:T(8,128)S(1)}, f32[640,128]{0,1:T(8,128)S(1)}, u32[]{:S(2)}, u32[]{:S(2)}) collective-permute-start(f32[640,128]{0,1:T(8,128)S(1)} %add.131), channel_id=1, source_target_pairs={{0,256},{256,0},{16,272},{272,16},{32,288},{288,32},{48,304},{304,... | collective-permute-start | bytes 983048 | tf_op jit(solution)/shard_map/ppermute | solution.py:22
  552.7 14.1 %collective-permute-done.13 = f32[640,128]{0,1:T(8,128)S(1)} collective-permute-done((f32[640,128]{0,1:T(8,128)S(1)}, f32[640,128]{0,1:T(8,128)S(1)}, u32[]{:S(2)}, u32[]{:S(2)}) %collective-permute-start.13) | collective-permute-done | bytes 327712 | tf_op jit(solution)/shard_map/ppermute | solution.py:22
  567.6 110.0 %all-reduce.9.cloned.1.call-done = bf16[640,128]{0,1:T(8,128)(2,1)} async-done(((bf16[640,128]{0,1:T(8,128)(2,1)}), bf16[640,128]{0,1:T(8,128)(2,1)}) %all-reduce.9.cloned.1.call-update) | async-done | bytes 163856 | tf_op jit(solution)/shard_map/psum | solution.py:12
  678.8 4.4 collective-permute-start.14
  684.5 3.2 collective-permute-start.15
  687.7 7.6 collective-permute-done.15
  695.3 4.2 collective-permute-start.16
  699.5 14.2 %collective-permute-done.16 = f32[640,128]{0,1:T(8,128)S(1)} collective-permute-done((f32[640,128]{0,1:T(8,128)S(1)}, f32[640,128]{0,1:T(8,128)S(1)}, u32[]{:S(2)}, u32[]{:S(2)}) %collective-permute-start.16) | collective-permute-done | bytes 327712 | tf_op jit(solution)/shard_map/ppermute | solution.py:22
  713.7 7.4 collective-permute-start.17
  721.1 28.2 %collective-permute-done.17 = f32[640,128]{0,1:T(8,128)S(1)} collective-permute-done((f32[640,128]{0,1:T(8,128)S(1)}, f32[640,128]{0,1:T(8,128)S(1)}, u32[]{:S(2)}, u32[]{:S(2)}) %collective-permute-start.17) | collective-permute-done | bytes 327712 | tf_op jit(solution)/shard_map/ppermute | solution.py:22
  749.4 18.2 %collective-permute-start.18 = (f32[640,128]{0,1:T(8,128)S(1)}, f32[640,128]{0,1:T(8,128)S(1)}, u32[]{:S(2)}, u32[]{:S(2)}) collective-permute-start(f32[640,128]{0,1:T(8,128)S(1)} %add.136), channel_id=1, source_target_pairs={{0,256},{256,0},{16,272},{272,16},{32,288},{288,32},{48,304},{304,... | collective-permute-start | bytes 983048 | tf_op jit(solution)/shard_map/ppermute | solution.py:22
  767.6 14.1 %collective-permute-done.18 = f32[640,128]{0,1:T(8,128)S(1)} collective-permute-done((f32[640,128]{0,1:T(8,128)S(1)}, f32[640,128]{0,1:T(8,128)S(1)}, u32[]{:S(2)}, u32[]{:S(2)}) %collective-permute-start.18) | collective-permute-done | bytes 327712 | tf_op jit(solution)/shard_map/ppermute | solution.py:22
  782.6 110.6 %all-reduce.11.cloned.1.call-done = bf16[640,256]{0,1:T(8,128)(2,1)} async-done(((bf16[640,256]{0,1:T(8,128)(2,1)}), bf16[640,256]{0,1:T(8,128)(2,1)}) %all-reduce.11.cloned.1.call-update) | async-done | bytes 327696 | tf_op jit(solution)/shard_map/psum | solution.py:12
  893.2 1.3 fusion.3
  894.9 3.9 collective-permute-start.19
  900.1 3.2 collective-permute-start.20
  903.2 7.6 collective-permute-done.20
  910.9 4.2 collective-permute-start.21
  915.1 14.2 %collective-permute-done.21 = f32[640,128]{0,1:T(8,128)S(1)} collective-permute-done((f32[640,128]{0,1:T(8,128)S(1)}, f32[640,128]{0,1:T(8,128)S(1)}, u32[]{:S(2)}, u32[]{:S(2)}) %collective-permute-start.21) | collective-permute-done | bytes 327712 | tf_op jit(solution)/shard_map/ppermute | solution.py:22
  929.3 7.4 collective-permute-start.22
  936.7 28.2 %collective-permute-done.22 = f32[640,128]{0,1:T(8,128)S(1)} collective-permute-done((f32[640,128]{0,1:T(8,128)S(1)}, f32[640,128]{0,1:T(8,128)S(1)}, u32[]{:S(2)}, u32[]{:S(2)}) %collective-permute-start.22) | collective-permute-done | bytes 327712 | tf_op jit(solution)/shard_map/ppermute | solution.py:22
  (64 shorter events, 16.2 us)
Async XLA Ops:
  6.5 189.7 %copy-start = (bf16[1,640,640]{2,1,0:T(8,128)(2,1)S(1)}, bf16[1,640,640]{2,1,0:T(8,128)(2,1)}, u32[]{:S(2)}) copy-start(bf16[1,640,640]{2,1,0:T(8,128)(2,1)} %param.9) | copy-start | bytes 2457604
  6.5 188.4 %all-reduce.5.cloned.1.call-start = ((), (), s32[]{:S(2)}) async-start(), calls=%async_computation | async-start | bytes 327680 | tf_op jit(solution)/shard_map/psum | solution.py:12
  7.7 44.0 %copy-start.6 = (s32[2,32]{1,0:T(2,128)S(1)}, s32[2,32]{1,0:T(2,128)}, u32[]{:S(2)}) copy-start(s32[2,32]{1,0:T(2,128)} %param.7) | copy-start | bytes 772
  7.7 10.0 %collective-permute-start = (f32[640,128]{0,1:T(8,128)S(1)}, f32[640,128]{0,1:T(8,128)S(1)}, u32[]{:S(2)}, u32[]{:S(2)}) collective-permute-start(f32[640,128]{0,1:T(8,128)S(1)} %bitcast_convert_fusion), channel_id=1, source_target_pairs={{0,16},{16,0},{32,48},{48,32},{64,80},{80,64},{96,112},{112,96},{1... | collective-permute-start | bytes 983048 | tf_op jit(solution)/shard_map/ppermute | solution.py:22
  17.8 10.8 %collective-permute-start.1 = (f32[640,128]{0,1:T(8,128)S(1)}, f32[640,128]{0,1:T(8,128)S(1)}, u32[]{:S(2)}, u32[]{:S(2)}) collective-permute-start(f32[640,128]{0,1:T(8,128)S(1)} %fusion.22), channel_id=1, source_target_pairs={{0,32},{32,0},{16,48},{48,16},{64,96},{96,64},{80,112},{112,80},{1... | collective-permute-start | bytes 983048 | tf_op jit(solution)/shard_map/ppermute | solution.py:22
  28.6 166.3 %copy-start.1 = (bf16[1,640,960]{1,2,0:T(8,128)(2,1)S(1)}, bf16[1,640,960]{1,2,0:T(8,128)(2,1)}, u32[]{:S(2)}) copy-start(bf16[1,640,960]{1,2,0:T(8,128)(2,1)} %param.8) | copy-start | bytes 3686404
  28.7 19.5 %collective-permute-start.2 = (f32[640,128]{0,1:T(8,128)S(1)}, f32[640,128]{0,1:T(8,128)S(1)}, u32[]{:S(2)}, u32[]{:S(2)}) collective-permute-start(f32[640,128]{0,1:T(8,128)S(1)} %add.117), channel_id=1, source_target_pairs={{0,64},{64,0},{16,80},{80,16},{32,96},{96,32},{48,112},{112,48},{1... | collective-permute-start | bytes 983048 | tf_op jit(solution)/shard_map/ppermute | solution.py:22
  48.2 33.9 %collective-permute-start.3 = (f32[640,128]{0,1:T(8,128)S(1)}, f32[640,128]{0,1:T(8,128)S(1)}, u32[]{:S(2)}, u32[]{:S(2)}) collective-permute-start(f32[640,128]{0,1:T(8,128)S(1)} %add.118), channel_id=1, source_target_pairs={{0,128},{128,0},{16,144},{144,16},{32,160},{160,32},{48,176},{176,... | collective-permute-start | bytes 983048 | tf_op jit(solution)/shard_map/ppermute | solution.py:22
  82.9 379.7 %all-reduce.7.cloned.1.call-start = ((), (), s32[]{:S(2)}) async-start(), calls=%async_computation.1 | async-start | bytes 327680 | tf_op jit(solution)/shard_map/psum | solution.py:12
  194.9 1.3 copy-start.4
  196.7 6.1 collective-permute-start.4
  202.9 17.8 %collective-permute-start.5 = (f32[1280,128]{0,1:T(8,128)S(1)}, f32[1280,128]{0,1:T(8,128)S(1)}, u32[]{:S(2)}, u32[]{:S(2)}) collective-permute-start(f32[1280,128]{0,1:T(8,128)S(1)} %fusion.29), channel_id=1, source_target_pairs={{0,32},{32,0},{16,48},{48,16},{64,96},{96,64},{80,112},{112,80},{1... | collective-permute-start | bytes 1966088 | tf_op jit(solution)/shard_map/ppermute | solution.py:22
  220.8 32.4 %collective-permute-start.6 = (f32[1280,128]{0,1:T(8,128)S(1)}, f32[1280,128]{0,1:T(8,128)S(1)}, u32[]{:S(2)}, u32[]{:S(2)}) collective-permute-start(f32[1280,128]{0,1:T(8,128)S(1)} %add.121), channel_id=1, source_target_pairs={{0,64},{64,0},{16,80},{80,16},{32,96},{96,32},{48,112},{112,48},{1... | collective-permute-start | bytes 1966088 | tf_op jit(solution)/shard_map/ppermute | solution.py:22
  253.3 70.8 %collective-permute-start.7 = (f32[1280,128]{0,1:T(8,128)S(1)}, f32[1280,128]{0,1:T(8,128)S(1)}, u32[]{:S(2)}, u32[]{:S(2)}) collective-permute-start(f32[1280,128]{0,1:T(8,128)S(1)} %add.122), channel_id=1, source_target_pairs={{0,128},{128,0},{16,144},{144,16},{32,160},{160,32},{48,176},{176,... | collective-permute-start | bytes 1966088 | tf_op jit(solution)/shard_map/ppermute | solution.py:22
  324.2 24.2 %collective-permute-start.8 = (f32[640,128]{0,1:T(8,128)S(1)}, f32[640,128]{0,1:T(8,128)S(1)}, u32[]{:S(2)}, u32[]{:S(2)}) collective-permute-start(f32[640,128]{0,1:T(8,128)S(1)} %get-tuple-element.6), channel_id=1, source_target_pairs={{0,256},{256,0},{16,272},{272,16},{32,288},{288,32},{48,304},{304,... | collective-permute-start | bytes 983048 | tf_op jit(solution)/shard_map/ppermute | solution.py:22
  349.1 328.4 %all-reduce.9.cloned.1.call-start = ((), (), s32[]{:S(2)}) async-start(), calls=%async_computation.2 | async-start | bytes 327680 | tf_op jit(solution)/shard_map/psum | solution.py:12
  463.7 5.7 collective-permute-start.9
  469.4 10.8 %collective-permute-start.10 = (f32[640,128]{0,1:T(8,128)S(1)}, f32[640,128]{0,1:T(8,128)S(1)}, u32[]{:S(2)}, u32[]{:S(2)}) collective-permute-start(f32[640,128]{0,1:T(8,128)S(1)} %add.128), channel_id=1, source_target_pairs={{0,32},{32,0},{16,48},{48,16},{64,96},{96,64},{80,112},{112,80},{1... | collective-permute-start | bytes 983048 | tf_op jit(solution)/shard_map/ppermute | solution.py:22
  480.3 18.4 %collective-permute-start.11 = (f32[640,128]{0,1:T(8,128)S(1)}, f32[640,128]{0,1:T(8,128)S(1)}, u32[]{:S(2)}, u32[]{:S(2)}) collective-permute-start(f32[640,128]{0,1:T(8,128)S(1)} %add.129), channel_id=1, source_target_pairs={{0,64},{64,0},{16,80},{80,16},{32,96},{96,32},{48,112},{112,48},{1... | collective-permute-start | bytes 983048 | tf_op jit(solution)/shard_map/ppermute | solution.py:22
  498.7 178.9 %copy-start.2 = (bf16[1,640,960]{1,2,0:T(8,128)(2,1)S(1)}, bf16[1,640,960]{1,2,0:T(8,128)(2,1)}, u32[]{:S(2)}) copy-start(bf16[1,640,960]{1,2,0:T(8,128)(2,1)} %param.10) | copy-start | bytes 3686404
  498.7 35.7 %collective-permute-start.12 = (f32[640,128]{0,1:T(8,128)S(1)}, f32[640,128]{0,1:T(8,128)S(1)}, u32[]{:S(2)}, u32[]{:S(2)}) collective-permute-start(f32[640,128]{0,1:T(8,128)S(1)} %add.130), channel_id=1, source_target_pairs={{0,128},{128,0},{16,144},{144,16},{32,160},{160,32},{48,176},{176,... | collective-permute-start | bytes 983048 | tf_op jit(solution)/shard_map/ppermute | solution.py:22
  534.5 32.3 %collective-permute-start.13 = (f32[640,128]{0,1:T(8,128)S(1)}, f32[640,128]{0,1:T(8,128)S(1)}, u32[]{:S(2)}, u32[]{:S(2)}) collective-permute-start(f32[640,128]{0,1:T(8,128)S(1)} %add.131), channel_id=1, source_target_pairs={{0,256},{256,0},{16,272},{272,16},{32,288},{288,32},{48,304},{304,... | collective-permute-start | bytes 983048 | tf_op jit(solution)/shard_map/ppermute | solution.py:22
  567.5 325.7 %all-reduce.11.cloned.1.call-start = ((), (), s32[]{:S(2)}) async-start(), calls=%async_computation.3 | async-start | bytes 655360 | tf_op jit(solution)/shard_map/psum | solution.py:12
  678.8 5.7 collective-permute-start.14
  684.5 10.8 %collective-permute-start.15 = (f32[640,128]{0,1:T(8,128)S(1)}, f32[640,128]{0,1:T(8,128)S(1)}, u32[]{:S(2)}, u32[]{:S(2)}) collective-permute-start(f32[640,128]{0,1:T(8,128)S(1)} %add.133), channel_id=1, source_target_pairs={{0,32},{32,0},{16,48},{48,16},{64,96},{96,64},{80,112},{112,80},{1... | collective-permute-start | bytes 983048 | tf_op jit(solution)/shard_map/ppermute | solution.py:22
  695.3 18.4 %collective-permute-start.16 = (f32[640,128]{0,1:T(8,128)S(1)}, f32[640,128]{0,1:T(8,128)S(1)}, u32[]{:S(2)}, u32[]{:S(2)}) collective-permute-start(f32[640,128]{0,1:T(8,128)S(1)} %add.134), channel_id=1, source_target_pairs={{0,64},{64,0},{16,80},{80,16},{32,96},{96,32},{48,112},{112,48},{1... | collective-permute-start | bytes 983048 | tf_op jit(solution)/shard_map/ppermute | solution.py:22
  713.7 35.6 %collective-permute-start.17 = (f32[640,128]{0,1:T(8,128)S(1)}, f32[640,128]{0,1:T(8,128)S(1)}, u32[]{:S(2)}, u32[]{:S(2)}) collective-permute-start(f32[640,128]{0,1:T(8,128)S(1)} %add.135), channel_id=1, source_target_pairs={{0,128},{128,0},{16,144},{144,16},{32,160},{160,32},{48,176},{176,... | collective-permute-start | bytes 983048 | tf_op jit(solution)/shard_map/ppermute | solution.py:22
  749.4 32.3 %collective-permute-start.18 = (f32[640,128]{0,1:T(8,128)S(1)}, f32[640,128]{0,1:T(8,128)S(1)}, u32[]{:S(2)}, u32[]{:S(2)}) collective-permute-start(f32[640,128]{0,1:T(8,128)S(1)} %add.136), channel_id=1, source_target_pairs={{0,256},{256,0},{16,272},{272,16},{32,288},{288,32},{48,304},{304,... | collective-permute-start | bytes 983048 | tf_op jit(solution)/shard_map/ppermute | solution.py:22
  781.7 112.8 %copy-start.3 = (bf16[1,640,640]{2,1,0:T(8,128)(2,1)S(1)}, bf16[1,640,640]{2,1,0:T(8,128)(2,1)}, u32[]{:S(2)}) copy-start(bf16[1,640,640]{2,1,0:T(8,128)(2,1)} %param.11) | copy-start | bytes 2457604
  893.2 1.3 copy-start.5
  894.9 5.1 collective-permute-start.19
  900.1 10.8 %collective-permute-start.20 = (f32[640,128]{0,1:T(8,128)S(1)}, f32[640,128]{0,1:T(8,128)S(1)}, u32[]{:S(2)}, u32[]{:S(2)}) collective-permute-start(f32[640,128]{0,1:T(8,128)S(1)} %add.138), channel_id=1, source_target_pairs={{0,32},{32,0},{16,48},{48,16},{64,96},{96,64},{80,112},{112,80},{1... | collective-permute-start | bytes 983048 | tf_op jit(solution)/shard_map/ppermute | solution.py:22
  910.9 18.4 %collective-permute-start.21 = (f32[640,128]{0,1:T(8,128)S(1)}, f32[640,128]{0,1:T(8,128)S(1)}, u32[]{:S(2)}, u32[]{:S(2)}) collective-permute-start(f32[640,128]{0,1:T(8,128)S(1)} %add.139), channel_id=1, source_target_pairs={{0,64},{64,0},{16,80},{80,16},{32,96},{96,32},{48,112},{112,48},{1... | collective-permute-start | bytes 983048 | tf_op jit(solution)/shard_map/ppermute | solution.py:22
  929.3 35.6 %collective-permute-start.22 = (f32[640,128]{0,1:T(8,128)S(1)}, f32[640,128]{0,1:T(8,128)S(1)}, u32[]{:S(2)}, u32[]{:S(2)}) collective-permute-start(f32[640,128]{0,1:T(8,128)S(1)} %add.140), channel_id=1, source_target_pairs={{0,128},{128,0},{16,144},{144,16},{32,160},{160,32},{48,176},{176,... | collective-permute-start | bytes 983048 | tf_op jit(solution)/shard_map/ppermute | solution.py:22
Sparse Core Ops, SparseCore 0:
  83.0 111.9 all-reduce.4
  349.3 113.2 all-reduce.6
  567.7 109.8 all-reduce.8
  782.7 110.4 all-reduce.10
where the time goes:
time: 973 us; the launch traced here: 972 us
  waiting for transfers between devices  805 us (83%)
  starting transfers between devices  140 us (14%)
  between operations  13.6 us (1%)
    psum x4, waiting for transfers between devices, from_root(): return lax.psum(jnp.where(mine, array, jnp.zeros_like(array)), axis)  446 us
    ppermute x23, waiting for transfers between devices, partner(): return lax.ppermute(block, axis, route)  359 us
    ppermute x23, starting transfers between devices, partner(): return lax.ppermute(block, axis, route)  140 us
  transfers between devices with their start and end apart: 27, of which 27 were waited for; matrix products, arithmetic and copies ran while one was open for 0% of the time, Pallas kernels for 0%

commit v1 on v0

v1 whole, which is shorter than its diff:
```python
import jax
import jax.numpy as jnp
from jax import lax
from jax.sharding import PartitionSpec as P

BLK = 128
WIN = 24
PIECE = 40
LO = PIECE - WIN


def body(forcing, live, lower_inv, lower_upd, upper_inv, upper_upd):
    n_leaf = lax.axis_size("leaf")
    n_front = lax.axis_size("front")
    n_z = n_leaf // 2
    half = n_z // 2
    sep_dev, n_rhs = forcing.shape[1:]
    w0, w1 = sep_dev, sep_dev // 2
    leaf_id = lax.axis_index("leaf")
    front_id = lax.axis_index("front")
    z, core = leaf_id // 2, leaf_id % 2
    node, z8 = z // half, z % half
    bf, f32 = jnp.bfloat16, jnp.float32

    plane = [[(2 * k + c) * n_front + f for c in range(2) for f in range(n_front)] for k in range(n_z)]
    z_all = [[2 * k + c for k in range(n_z)] for c in range(2)]
    z_half = [[2 * (h * half + k) + c for k in range(half)] for h in range(2) for c in range(2)]
    leaf_half = [list(range(h * n_z, (h + 1) * n_z)) for h in range(2)]

    def a2a_plane(v):
        return lax.all_to_all(v, ("leaf", "front"), 0, 0, axis_index_groups=plane)

    def a2a_leaf(v, groups):
        return lax.all_to_all(v, "leaf", 0, 0, axis_index_groups=groups)

    def spread(v, n):
        return jnp.broadcast_to(v[None], (n,) + v.shape)

    def cut(v):
        v = v.reshape(n_front, PIECE, v.shape[-1])
        return jnp.concatenate([v[:, :WIN], v[:, LO:]], 0)

    def join(v):
        low, high = v[:n_front], v[n_front:, WIN - LO :]
        return jnp.concatenate([low, high], 1).reshape(n_front * PIECE, v.shape[-1])

    def total(v):
        return jnp.sum(v.astype(f32), 0)

    def piece_mask(first_block, n_blocks, count):
        rows = (
            (first_block + jnp.arange(n_blocks)[:, None]) * sep_dev
            + front_id * PIECE
            + core * LO
            + jnp.arange(WIN)[None, :]
        )
        return (rows < count * BLK).astype(f32)[:, :, None]

    def times(mat, vec):
        width = mat.shape[-1]
        m = mat.reshape(2, n_front * WIN, width)
        v = vec.reshape(2, width, n_rhs)
        return (
            jnp.dot(m[0], v[0], preferred_element_type=f32)
            + jnp.dot(m[1], v[1], preferred_element_type=f32)
        ).reshape(n_front, WIN, n_rhs)

    mask0 = piece_mask(2 * z8, 2, live[0][node])
    mask1 = piece_mask(z, 1, live[1][0])
    rows = front_id * sep_dev + jnp.arange(sep_dev)
    rows_mask = (rows < live[0][node] * BLK).astype(f32)[:, None]

    got = a2a_plane(cut(forcing[0]))
    low0 = a2a_plane(cut(jnp.concatenate([lower_upd[0], lower_inv[0]], 1)))
    up1 = a2a_plane(cut(upper_inv[0, :, w0:]))
    g0, linv0, linv1 = low0[:, :, :w0], low0[:, :, w0 : 2 * w0], low0[:, :, 2 * w0 :]

    pair = got[:n_front].astype(f32) + got[n_front:].astype(f32)
    pair = pair.astype(bf).reshape(half, 2 * WIN, n_rhs)
    r0 = total(a2a_leaf(pair, z_half)).reshape(2, WIN, n_rhs)
    rm0 = (mask0 * r0).astype(bf)

    def gather_two(v):
        got = a2a_plane(spread(v, 2 * n_front))
        return jnp.concatenate([join(got[:, 0]), join(got[:, 1])], 0)

    rm0 = gather_two(rm0)
    c_part = times(g0, rm0).astype(bf)
    y_part = times(linv0, rm0).astype(bf).reshape(half, 2 * WIN, n_rhs)
    zero = jnp.zeros_like(y_part)
    first = node == 0
    y_part = jnp.concatenate([jnp.where(first, y_part, zero), jnp.where(first, zero, y_part)], 0)
    got = total(a2a_leaf(jnp.concatenate([c_part, y_part], 1), z_all))
    r1 = (mask1[0] * -got[:WIN]).astype(bf)
    y0 = (mask0 * got[WIN:].reshape(2, WIN, n_rhs)).astype(bf)
    got = a2a_plane(spread(jnp.concatenate([r1[None], y0], 0), 2 * n_front))
    r1 = join(got[:, 0])
    y0 = jnp.concatenate([join(got[:, 1]), join(got[:, 2])], 0)

    y1 = total(a2a_leaf(times(linv1, r1).astype(bf), z_all))
    y1 = (mask1[0] * y1).astype(bf)
    y1 = join(a2a_plane(spread(y1, 2 * n_front)))

    x_part = times(up1, y1).astype(bf).reshape(half, 2 * WIN, n_rhs)
    x1 = total(a2a_leaf(jnp.concatenate([x_part, x_part], 0), z_all)).reshape(2, WIN, n_rhs)
    x1 = (piece_mask(2 * z8, 2, live[1][0]) * x1).astype(bf)
    x1_all = a2a_leaf(spread(x1, half), z_half).reshape(n_front, WIN, n_rhs)
    x1_out = join(a2a_plane(jnp.concatenate([x1_all, x1_all], 0)))
    x1 = gather_two(x1)

    y0 = lax.dynamic_slice_in_dim(y0, core * w0, w0, 0)
    x1 = lax.dynamic_slice_in_dim(x1, core * w0, w0, 0)
    term = jnp.dot(upper_inv[0, :, :w0], y0, preferred_element_type=f32) - jnp.dot(
        upper_upd[0], x1, preferred_element_type=f32
    )
    term = total(a2a_leaf(term.astype(bf).reshape(n_z, sep_dev // n_z, n_rhs), leaf_half))
    x0 = a2a_leaf(spread(term.astype(bf), n_z), leaf_half).reshape(sep_dev, n_rhs)
    x0 = (rows_mask * x0).astype(bf)
    return jnp.stack([x0, x1_out])[:, None]


def solution(mesh):
    return jax.shard_map(
        body,
        mesh=mesh,
        in_specs=(
            P("leaf", "front", None),
            P(),
            P("leaf", "front", None),
            P("leaf", "front", None),
            P("leaf", "front", None),
            P("leaf", "front", None),
        ),
        out_specs=P(None, "leaf", "front", None),
        check_vma=False,
    )
```

time: 973 us -> 305 us (0.31)
  waiting for transfers between devices: 805 us -> 155 us
  starting transfers between devices: 140 us -> 89.5 us
  local copies, waits for them, and re-layouts: 2.09 us -> 22.6 us
  blocking collectives: 0 us -> 17.8 us
  between operations: 13.6 us -> 1.09 us
    psum x4 -> x0, waiting for transfers between devices: 446 us -> none  [from_root(): return lax.psum(jnp.where(mine, array, jnp.zeros_like(array)), axis)]
    ppermute x23 -> x0, waiting for transfers between devices: 359 us -> none  [partner(): return lax.ppermute(block, axis, route)]
    all_to_all x0 -> x14, waiting for transfers between devices: none -> 155 us  [the longest x7 81.2 us: a2a_plane(): return lax.all_to_all(v, ('leaf', 'front'), 0, 0, axis_index_groups=plane)]
    ppermute x23 -> x0, starting transfers between devices: 140 us -> none  [partner(): return lax.ppermute(block, axis, route)]
    all_to_all x0 -> x14, starting transfers between devices: none -> 89.5 us  [the longest x7 46.4 us: a2a_plane(): return lax.all_to_all(v, ('leaf', 'front'), 0, 0, axis_index_groups=plane)]
    all_to_all x0 -> x1, blocking collectives: none -> 17.8 us  [a2a_plane(): return lax.all_to_all(v, ('leaf', 'front'), 0, 0, axis_index_groups=plane)]
  transfers between devices with their start and end apart: 27 -> 14, of which waited for: 27 -> 14; matrix products, arithmetic and copies ran while one was open for 0% -> 7% of each run, Pallas kernels for 0% -> 0%
where the time goes in v1:
time: 305 us; the launch traced here: 303 us
  waiting for transfers between devices  155 us (51%)
  starting transfers between devices  89.5 us (29%)
  local copies, waits for them, and re-layouts  22.6 us (7%)
  blocking collectives  17.8 us (6%)
  other arithmetic  11.5 us (4%)
  matrix products  5.4 us (2%)
    all_to_all x7, waiting for transfers between devices, a2a_plane(): return lax.all_to_all(v, ('leaf', 'front'), 0, 0, axis_index_groups=plane)  81.2 us
    all_to_all x7, waiting for transfers between devices, a2a_leaf(): return lax.all_to_all(v, 'leaf', 0, 0, axis_index_groups=groups)  74.2 us
    all_to_all x7, starting transfers between devices, a2a_plane(): return lax.all_to_all(v, ('leaf', 'front'), 0, 0, axis_index_groups=plane)  46.4 us
    all_to_all x7, starting transfers between devices, a2a_leaf(): return lax.all_to_all(v, 'leaf', 0, 0, axis_index_groups=groups)  43 us
    all_to_all x1, blocking collectives, a2a_plane(): return lax.all_to_all(v, ('leaf', 'front'), 0, 0, axis_index_groups=plane)  17.8 us
  transfers between devices with their start and end apart: 14, of which 14 were waited for; matrix products, arithmetic and copies ran while one was open for 7% of the time, Pallas kernels for 0%

profile of v1, /device:TPU:1, one launch (start us, length us, event | category | flops | bytes accessed | tf_op | source)
XLA Modules:
  0.0 303.2 jit_solution(9122547772528711569)
XLA Ops:
  0.0 1.0 fusion.31
  1.1 17.8 %all_to_all.75 = bf16[32,24,128]{2,1,0:T(8,128)(2,1)S(1)} all-to-all(bf16[32,24,128]{2,1,0:T(8,128)(2,1)S(1)} %pad_maximum_fusion.2), channel_id=1, replica_groups={{0,1,2,3,4,5,6,7,8,9,10,11,12,13,14,15,16,17,18,19,20,21,22,23,24,25,26..., dimensions={0} | all-to-all | bytes 393216 | tf_op jit(solution)/shard_map/all_to_all | solution.py:31
  19.6 11.0 %all-to-all-start.2 = ((bf16[8,48,128]{2,1,0:T(8,128)(2,1)}), bf16[8,48,128]{2,1,0:T(8,128)(2,1)S(1)}, u32[]{:S(2)}, u32[]{:S(2)}) async-start(bf16[8,48,128]{2,1,0:T(8,128)(2,1)} %bitcast.6), calls=%async_computation.2 | async-start | bytes 196608 | tf_op jit(solution)/shard_map/all_to_all | solution.py:34
  30.6 1.2 slice.215
  31.8 1.6 copy.8
  34.7 1.3 compare_convert_fusion
  36.0 4.6 %all-to-all-done.2 = bf16[8,48,128]{2,1,0:T(8,128)(2,1)S(1)} async-done(((bf16[8,48,128]{2,1,0:T(8,128)(2,1)}), bf16[8,48,128]{2,1,0:T(8,128)(2,1)S(1)}, u32[]{:S(2)}, u32[]{:S(2)}) %all-to-all-start.2) | async-done | bytes 98336 | tf_op jit(solution)/shard_map/all_to_all | solution.py:34
  41.6 5.7 %all-to-all-start.3 = ((bf16[32,2,24,128]{3,2,1,0:T(8,128)(2,1)}), bf16[32,2,24,128]{3,2,1,0:T(8,128)(2,1)S(1)}, u32[]{:S(2)}, u32[]{:S(2)}) async-start(bf16[32,2,24,128]{3,2,1,0:T(8,128)(2,1)} %broadcast_in_dim.18), calls=%async_computation.3 | async-start | bytes 786432 | tf_op jit(solution)/shard_map/all_to_all | solution.py:31
  47.4 1.7 fusion
  49.1 7.8 %all-to-all-done.3 = bf16[32,2,24,128]{3,2,1,0:T(8,128)(2,1)S(1)} async-done(((bf16[32,2,24,128]{3,2,1,0:T(8,128)(2,1)}), bf16[32,2,24,128]{3,2,1,0:T(8,128)(2,1)S(1)}, u32[]{:S(2)}, u32[]{:S(2)}) %all-to-all-start.3) | async-done | bytes 393248 | tf_op jit(solution)/shard_map/all_to_all | solution.py:31
  57.7 5.0 %all-to-all-start = ((bf16[32,24,1600]{2,1,0:T(8,128)(2,1)}), bf16[32,24,1600]{2,1,0:T(8,128)(2,1)S(1)}, u32[]{:S(2)}, u32[]{:S(2)}) async-start(bf16[32,24,1600]{2,1,0:T(8,128)(2,1)} %fusion), calls=%async_computation | async-start | bytes 5111808 | tf_op jit(solution)/shard_map/all_to_all | solution.py:31
  62.7 1.1 slice_bitcast_fusion.5
  63.8 1.0 slice_bitcast_fusion.12
  65.5 30.8 %all-to-all-done = bf16[32,24,1600]{2,1,0:T(8,128)(2,1)S(1)} async-done(((bf16[32,24,1600]{2,1,0:T(8,128)(2,1)}), bf16[32,24,1600]{2,1,0:T(8,128)(2,1)S(1)}, u32[]{:S(2)}, u32[]{:S(2)}) %all-to-all-start) | async-done | bytes 2457632 | tf_op jit(solution)/shard_map/all_to_all | solution.py:31
  98.5 7.5 %all-to-all-start.4 = ((bf16[16,72,128]{2,1,0:T(8,128)(2,1)}), bf16[16,72,128]{2,1,0:T(8,128)(2,1)}, u32[]{:S(2)}, u32[]{:S(2)}) async-start(bf16[16,72,128]{2,1,0:T(8,128)(2,1)} %maximum_maximum_fusion), calls=%async_computation.4 | async-start | bytes 589824 | tf_op jit(solution)/shard_map/all_to_all | solution.py:34
  106.0 13.2 %all-to-all-done.4 = bf16[16,72,128]{2,1,0:T(8,128)(2,1)} async-done(((bf16[16,72,128]{2,1,0:T(8,128)(2,1)}), bf16[16,72,128]{2,1,0:T(8,128)(2,1)}, u32[]{:S(2)}, u32[]{:S(2)}) %all-to-all-start.4) | async-done | bytes 294944 | tf_op jit(solution)/shard_map/all_to_all | solution.py:34
  119.2 1.0 convert_reduce_fusion
  120.4 0.9 broadcast_in_dim.21
  121.3 12.0 %all-to-all-start.5 = ((bf16[32,3,24,128]{3,2,1,0:T(8,128)(2,1)}), bf16[32,3,24,128]{3,2,1,0:T(8,128)(2,1)}, u32[]{:S(2)}, u32[]{:S(2)}) async-start(bf16[32,3,24,128]{3,2,1,0:T(8,128)(2,1)} %broadcast_in_dim.21), calls=%async_computation.5 | async-start | bytes 1179648 | tf_op jit(solution)/shard_map/all_to_all | solution.py:31
  133.4 1.8 slice.245
  135.2 2.0 copy.11
  137.2 0.9 fusion.27
  138.1 7.1 %all-to-all-done.5 = bf16[32,3,24,128]{3,2,1,0:T(8,128)(2,1)} async-done(((bf16[32,3,24,128]{3,2,1,0:T(8,128)(2,1)}), bf16[32,3,24,128]{3,2,1,0:T(8,128)(2,1)}, u32[]{:S(2)}, u32[]{:S(2)}) %all-to-all-start.5) | async-done | bytes 589856 | tf_op jit(solution)/shard_map/all_to_all | solution.py:31
  145.2 1.9 slice_bitcast_fusion.3
  147.1 1.7 slice_bitcast_fusion.10
  148.8 1.2 fusion.35
  150.0 0.9 fusion.6
  150.9 5.2 %all-to-all-start.7 = ((bf16[16,24,128]{2,1,0:T(8,128)(2,1)}), bf16[16,24,128]{2,1,0:T(8,128)(2,1)S(1)}, u32[]{:S(2)}, u32[]{:S(2)}) async-start(bf16[16,24,128]{2,1,0:T(8,128)(2,1)} %bitcast.37), calls=%async_computation.7 | async-start | bytes 196608 | tf_op jit(solution)/shard_map/all_to_all | solution.py:34
  156.3 0.9 pad_maximum_fusion.1
  157.2 10.8 %all-to-all-done.7 = bf16[16,24,128]{2,1,0:T(8,128)(2,1)S(1)} async-done(((bf16[16,24,128]{2,1,0:T(8,128)(2,1)}), bf16[16,24,128]{2,1,0:T(8,128)(2,1)S(1)}, u32[]{:S(2)}, u32[]{:S(2)}) %all-to-all-start.7) | async-done | bytes 98336 | tf_op jit(solution)/shard_map/all_to_all | solution.py:34
  168.0 6.5 %all-to-all-start.6 = ((bf16[32,24,320]{2,1,0:T(8,128)(2,1)}), bf16[32,24,320]{2,1,0:T(8,128)(2,1)S(1)}, u32[]{:S(2)}, u32[]{:S(2)}) async-start(bf16[32,24,320]{2,1,0:T(8,128)(2,1)} %pad_maximum_fusion.1), calls=%async_computation.6 | async-start | bytes 1179648 | tf_op jit(solution)/shard_map/all_to_all | solution.py:31
  174.6 11.6 %all-to-all-done.6 = bf16[32,24,320]{2,1,0:T(8,128)(2,1)S(1)} async-done(((bf16[32,24,320]{2,1,0:T(8,128)(2,1)}), bf16[32,24,320]{2,1,0:T(8,128)(2,1)S(1)}, u32[]{:S(2)}, u32[]{:S(2)}) %all-to-all-start.6) | async-done | bytes 491552 | tf_op jit(solution)/shard_map/all_to_all | solution.py:31
  186.9 4.8 %all-to-all-start.8 = ((bf16[32,24,128]{2,1,0:T(8,128)(2,1)}), bf16[32,24,128]{2,1,0:T(8,128)(2,1)S(1)}, u32[]{:S(2)}, u32[]{:S(2)}) async-start(bf16[32,24,128]{2,1,0:T(8,128)(2,1)} %broadcast_in_dim.22), calls=%async_computation.8 | async-start | bytes 393216 | tf_op jit(solution)/shard_map/all_to_all | solution.py:31
  191.8 8.0 %all-to-all-done.8 = bf16[32,24,128]{2,1,0:T(8,128)(2,1)S(1)} async-done(((bf16[32,24,128]{2,1,0:T(8,128)(2,1)}), bf16[32,24,128]{2,1,0:T(8,128)(2,1)S(1)}, u32[]{:S(2)}, u32[]{:S(2)}) %all-to-all-start.8) | async-done | bytes 196640 | tf_op jit(solution)/shard_map/all_to_all | solution.py:31
  201.0 3.5 %all-to-all-start.9 = ((bf16[16,48,128]{2,1,0:T(8,128)(2,1)}), bf16[16,48,128]{2,1,0:T(8,128)(2,1)S(1)}, u32[]{:S(2)}, u32[]{:S(2)}) async-start(bf16[16,48,128]{2,1,0:T(8,128)(2,1)} %pad_maximum_fusion.3), calls=%async_computation.9 | async-start | bytes 393216 | tf_op jit(solution)/shard_map/all_to_all | solution.py:34
  204.6 0.8 slice.295
  205.4 11.7 %all-to-all-done.9 = bf16[16,48,128]{2,1,0:T(8,128)(2,1)S(1)} async-done(((bf16[16,48,128]{2,1,0:T(8,128)(2,1)}), bf16[16,48,128]{2,1,0:T(8,128)(2,1)S(1)}, u32[]{:S(2)}, u32[]{:S(2)}) %all-to-all-start.9) | async-done | bytes 196640 | tf_op jit(solution)/shard_map/all_to_all | solution.py:34
  218.0 8.4 %all-to-all-start.10 = ((bf16[32,2,24,128]{3,2,1,0:T(8,128)(2,1)}), bf16[32,2,24,128]{3,2,1,0:T(8,128)(2,1)S(1)}, u32[]{:S(2)}, u32[]{:S(2)}) async-start(bf16[32,2,24,128]{3,2,1,0:T(8,128)(2,1)} %broadcast_in_dim.23), calls=%async_computation.10 | async-start | bytes 786432 | tf_op jit(solution)/shard_map/all_to_all | solution.py:31
  228.2 7.9 %all-to-all-done.10 = bf16[32,2,24,128]{3,2,1,0:T(8,128)(2,1)S(1)} async-done(((bf16[32,2,24,128]{3,2,1,0:T(8,128)(2,1)}), bf16[32,2,24,128]{3,2,1,0:T(8,128)(2,1)S(1)}, u32[]{:S(2)}, u32[]{:S(2)}) %all-to-all-start.10) | async-done | bytes 393248 | tf_op jit(solution)/shard_map/all_to_all | solution.py:31
  236.7 4.5 %all-to-all-start.13 = ((bf16[8,2,24,128]{3,2,1,0:T(8,128)(2,1)}), bf16[8,2,24,128]{3,2,1,0:T(8,128)(2,1)S(1)}, u32[]{:S(2)}, u32[]{:S(2)}) async-start(bf16[8,2,24,128]{3,2,1,0:T(8,128)(2,1)} %broadcast_in_dim.25), calls=%async_computation.13 | async-start | bytes 196608 | tf_op jit(solution)/shard_map/all_to_all | solution.py:34
  241.4 0.9 fusion.3
  243.1 8.2 %all-to-all-done.13 = bf16[8,2,24,128]{3,2,1,0:T(8,128)(2,1)S(1)} async-done(((bf16[8,2,24,128]{3,2,1,0:T(8,128)(2,1)}), bf16[8,2,24,128]{3,2,1,0:T(8,128)(2,1)S(1)}, u32[]{:S(2)}, u32[]{:S(2)}) %all-to-all-start.13) | async-done | bytes 98336 | tf_op jit(solution)/shard_map/all_to_all | solution.py:34
  251.3 6.0 %all-to-all-start.11 = ((bf16[16,40,128]{2,1,0:T(8,128)(2,1)}), bf16[16,40,128]{2,1,0:T(8,128)(2,1)S(1)}, u32[]{:S(2)}, u32[]{:S(2)}) async-start(bf16[16,40,128]{2,1,0:T(8,128)(2,1)} %bitcast.51), calls=%async_computation.11 | async-start | bytes 327680 | tf_op jit(solution)/shard_map/all_to_all | solution.py:34
  257.9 12.9 %all-to-all-done.11 = bf16[16,40,128]{2,1,0:T(8,128)(2,1)S(1)} async-done(((bf16[16,40,128]{2,1,0:T(8,128)(2,1)}), bf16[16,40,128]{2,1,0:T(8,128)(2,1)S(1)}, u32[]{:S(2)}, u32[]{:S(2)}) %all-to-all-start.11) | async-done | bytes 163872 | tf_op jit(solution)/shard_map/all_to_all | solution.py:34
  270.8 3.9 %all-to-all-start.14 = ((bf16[32,24,128]{2,1,0:T(8,128)(2,1)}), bf16[32,24,128]{2,1,0:T(8,128)(2,1)S(1)}, u32[]{:S(2)}, u32[]{:S(2)}) async-start(bf16[32,24,128]{2,1,0:T(8,128)(2,1)} %pad_maximum_fusion.4), calls=%async_computation.14 | async-start | bytes 393216 | tf_op jit(solution)/shard_map/all_to_all | solution.py:31
  274.8 8.1 %all-to-all-done.14 = bf16[32,24,128]{2,1,0:T(8,128)(2,1)S(1)} async-done(((bf16[32,24,128]{2,1,0:T(8,128)(2,1)}), bf16[32,24,128]{2,1,0:T(8,128)(2,1)S(1)}, u32[]{:S(2)}, u32[]{:S(2)}) %all-to-all-start.14) | async-done | bytes 196640 | tf_op jit(solution)/shard_map/all_to_all | solution.py:31
  283.5 5.3 %all-to-all-start.12 = ((bf16[16,40,128]{2,1,0:T(8,128)(2,1)}), bf16[16,40,128]{2,1,0:T(8,128)(2,1)S(1)}, u32[]{:S(2)}, u32[]{:S(2)}) async-start(bf16[16,40,128]{2,1,0:T(8,128)(2,1)} %broadcast_in_dim.24), calls=%async_computation.12 | async-start | bytes 327680 | tf_op jit(solution)/shard_map/all_to_all | solution.py:34
  289.5 12.7 %all-to-all-done.12 = bf16[16,40,128]{2,1,0:T(8,128)(2,1)S(1)} async-done(((bf16[16,40,128]{2,1,0:T(8,128)(2,1)}), bf16[16,40,128]{2,1,0:T(8,128)(2,1)S(1)}, u32[]{:S(2)}, u32[]{:S(2)}) %all-to-all-start.12) | async-done | bytes 163872 | tf_op jit(solution)/shard_map/all_to_all | solution.py:34
  (81 shorter events, 15.6 us)
Async XLA Ops:
  0.0 241.4 %copy-start = (bf16[1,640,640]{2,1,0:T(8,128)(2,1)S(1)}, bf16[1,640,640]{2,1,0:T(8,128)(2,1)}, u32[]{:S(2)}) copy-start(bf16[1,640,640]{2,1,0:T(8,128)(2,1)} %param.11) | copy-start | bytes 2457604
  0.0 33.4 %slice-start = ((s32[2,32]{1,0:T(2,128)}), s32[1,32]{1,0:T(1,128)S(1)}, s32[]{:S(2)}) async-start(s32[2,32]{1,0:T(2,128)} %param.7), calls=%async_computation.15 | async-start | bytes 1024 | tf_op jit(solution)/shard_map/slice | solution.py:71
  1.0 46.3 %copy-start.1 = (bf16[1,640,640]{2,1,0:T(8,128)(2,1)S(1)}, bf16[1,640,640]{2,1,0:T(8,128)(2,1)}, u32[]{:S(2)}) copy-start(bf16[1,640,640]{2,1,0:T(8,128)(2,1)} %param.9) | copy-start | bytes 2457604
  19.6 21.1 %all-to-all-start.2 = ((bf16[8,48,128]{2,1,0:T(8,128)(2,1)}), bf16[8,48,128]{2,1,0:T(8,128)(2,1)S(1)}, u32[]{:S(2)}, u32[]{:S(2)}) async-start(bf16[8,48,128]{2,1,0:T(8,128)(2,1)} %bitcast.6), calls=%async_computation.2 | async-start | bytes 196608 | tf_op jit(solution)/shard_map/all_to_all | solution.py:34
  41.6 15.3 %all-to-all-start.3 = ((bf16[32,2,24,128]{3,2,1,0:T(8,128)(2,1)}), bf16[32,2,24,128]{3,2,1,0:T(8,128)(2,1)S(1)}, u32[]{:S(2)}, u32[]{:S(2)}) async-start(bf16[32,2,24,128]{3,2,1,0:T(8,128)(2,1)} %broadcast_in_dim.18), calls=%async_computation.3 | async-start | bytes 786432 | tf_op jit(solution)/shard_map/all_to_all | solution.py:31
  56.9 0.7 copy-start.2
  57.7 38.6 %all-to-all-start = ((bf16[32,24,1600]{2,1,0:T(8,128)(2,1)}), bf16[32,24,1600]{2,1,0:T(8,128)(2,1)S(1)}, u32[]{:S(2)}, u32[]{:S(2)}) async-start(bf16[32,24,1600]{2,1,0:T(8,128)(2,1)} %fusion), calls=%async_computation | async-start | bytes 5111808 | tf_op jit(solution)/shard_map/all_to_all | solution.py:31
  96.2 0.9 copy-start.4
  98.5 20.7 %all-to-all-start.4 = ((bf16[16,72,128]{2,1,0:T(8,128)(2,1)}), bf16[16,72,128]{2,1,0:T(8,128)(2,1)}, u32[]{:S(2)}, u32[]{:S(2)}) async-start(bf16[16,72,128]{2,1,0:T(8,128)(2,1)} %maximum_maximum_fusion), calls=%async_computation.4 | async-start | bytes 589824 | tf_op jit(solution)/shard_map/all_to_all | solution.py:34
  121.3 23.8 %all-to-all-start.5 = ((bf16[32,3,24,128]{3,2,1,0:T(8,128)(2,1)}), bf16[32,3,24,128]{3,2,1,0:T(8,128)(2,1)}, u32[]{:S(2)}, u32[]{:S(2)}) async-start(bf16[32,3,24,128]{3,2,1,0:T(8,128)(2,1)} %broadcast_in_dim.21), calls=%async_computation.5 | async-start | bytes 1179648 | tf_op jit(solution)/shard_map/all_to_all | solution.py:31
  138.1 12.0 %copy-start.6 = (bf16[16,24,320]{2,1,0:T(8,128)(2,1)S(1)}, bf16[16,24,320]{2,1,0:T(8,128)(2,1)}, u32[]{:S(2)}) copy-start(bf16[16,24,320]{2,1,0:T(8,128)(2,1)} %get-tuple-element.5) | copy-start | bytes 737284
  138.1 18.1 %copy-start.3 = (bf16[1,640,320]{2,1,0:T(8,128)(2,1)S(1)}, bf16[1,640,320]{2,1,0:T(8,128)(2,1)}, u32[]{:S(2)}) copy-start(bf16[1,640,320]{2,1,0:T(8,128)(2,1)} %copy.11) | copy-start | bytes 1228804
  150.9 17.1 %all-to-all-start.7 = ((bf16[16,24,128]{2,1,0:T(8,128)(2,1)}), bf16[16,24,128]{2,1,0:T(8,128)(2,1)S(1)}, u32[]{:S(2)}, u32[]{:S(2)}) async-start(bf16[16,24,128]{2,1,0:T(8,128)(2,1)} %bitcast.37), calls=%async_computation.7 | async-start | bytes 196608 | tf_op jit(solution)/shard_map/all_to_all | solution.py:34
  168.0 18.2 %all-to-all-start.6 = ((bf16[32,24,320]{2,1,0:T(8,128)(2,1)}), bf16[32,24,320]{2,1,0:T(8,128)(2,1)S(1)}, u32[]{:S(2)}, u32[]{:S(2)}) async-start(bf16[32,24,320]{2,1,0:T(8,128)(2,1)} %pad_maximum_fusion.1), calls=%async_computation.6 | async-start | bytes 1179648 | tf_op jit(solution)/shard_map/all_to_all | solution.py:31
  174.5 42.6 %copy-start.9 = (f32[2,24]{1,0:T(2,128)S(1)}, f32[2,24]{1,0:T(2,128)}, u32[]{:S(2)}) copy-start(f32[2,24]{1,0:T(2,128)} %get-tuple-element.37) | copy-start | bytes 580
  186.9 12.9 %all-to-all-start.8 = ((bf16[32,24,128]{2,1,0:T(8,128)(2,1)}), bf16[32,24,128]{2,1,0:T(8,128)(2,1)S(1)}, u32[]{:S(2)}, u32[]{:S(2)}) async-start(bf16[32,24,128]{2,1,0:T(8,128)(2,1)} %broadcast_in_dim.22), calls=%async_computation.8 | async-start | bytes 393216 | tf_op jit(solution)/shard_map/all_to_all | solution.py:31
  191.7 34.8 %copy-start.8 = (bf16[16,24,128]{2,1,0:T(8,128)(2,1)S(1)}, bf16[16,24,128]{2,1,0:T(8,128)(2,1)}, u32[]{:S(2)}) copy-start(bf16[16,24,128]{2,1,0:T(8,128)(2,1)} %get-tuple-element.11) | copy-start | bytes 294916
  191.8 35.6 %copy-start.7 = (bf16[16,24,128]{2,1,0:T(8,128)(2,1)S(1)}, bf16[16,24,128]{2,1,0:T(8,128)(2,1)}, u32[]{:S(2)}) copy-start(bf16[16,24,128]{2,1,0:T(8,128)(2,1)} %get-tuple-element.13) | copy-start | bytes 294916
  191.8 35.6 %copy-start.5 = (bf16[1,640,960]{1,2,0:T(8,128)(2,1)S(1)}, bf16[1,640,960]{1,2,0:T(8,128)(2,1)}, u32[]{:S(2)}) copy-start(bf16[1,640,960]{1,2,0:T(8,128)(2,1)} %param.10) | copy-start | bytes 3686404
  201.0 16.1 %all-to-all-start.9 = ((bf16[16,48,128]{2,1,0:T(8,128)(2,1)}), bf16[16,48,128]{2,1,0:T(8,128)(2,1)S(1)}, u32[]{:S(2)}, u32[]{:S(2)}) async-start(bf16[16,48,128]{2,1,0:T(8,128)(2,1)} %pad_maximum_fusion.3), calls=%async_computation.9 | async-start | bytes 393216 | tf_op jit(solution)/shard_map/all_to_all | solution.py:34
  218.0 18.1 %all-to-all-start.10 = ((bf16[32,2,24,128]{3,2,1,0:T(8,128)(2,1)}), bf16[32,2,24,128]{3,2,1,0:T(8,128)(2,1)S(1)}, u32[]{:S(2)}, u32[]{:S(2)}) async-start(bf16[32,2,24,128]{3,2,1,0:T(8,128)(2,1)} %broadcast_in_dim.23), calls=%async_computation.10 | async-start | bytes 786432 | tf_op jit(solution)/shard_map/all_to_all | solution.py:31
  236.7 14.5 %all-to-all-start.13 = ((bf16[8,2,24,128]{3,2,1,0:T(8,128)(2,1)}), bf16[8,2,24,128]{3,2,1,0:T(8,128)(2,1)S(1)}, u32[]{:S(2)}, u32[]{:S(2)}) async-start(bf16[8,2,24,128]{3,2,1,0:T(8,128)(2,1)} %broadcast_in_dim.25), calls=%async_computation.13 | async-start | bytes 196608 | tf_op jit(solution)/shard_map/all_to_all | solution.py:34
  251.3 19.5 %all-to-all-start.11 = ((bf16[16,40,128]{2,1,0:T(8,128)(2,1)}), bf16[16,40,128]{2,1,0:T(8,128)(2,1)S(1)}, u32[]{:S(2)}, u32[]{:S(2)}) async-start(bf16[16,40,128]{2,1,0:T(8,128)(2,1)} %bitcast.51), calls=%async_computation.11 | async-start | bytes 327680 | tf_op jit(solution)/shard_map/all_to_all | solution.py:34
  270.8 12.0 %all-to-all-start.14 = ((bf16[32,24,128]{2,1,0:T(8,128)(2,1)}), bf16[32,24,128]{2,1,0:T(8,128)(2,1)S(1)}, u32[]{:S(2)}, u32[]{:S(2)}) async-start(bf16[32,24,128]{2,1,0:T(8,128)(2,1)} %pad_maximum_fusion.4), calls=%async_computation.14 | async-start | bytes 393216 | tf_op jit(solution)/shard_map/all_to_all | solution.py:31
  283.5 18.8 %all-to-all-start.12 = ((bf16[16,40,128]{2,1,0:T(8,128)(2,1)}), bf16[16,40,128]{2,1,0:T(8,128)(2,1)S(1)}, u32[]{:S(2)}, u32[]{:S(2)}) async-start(bf16[16,40,128]{2,1,0:T(8,128)(2,1)} %broadcast_in_dim.24), calls=%async_computation.12 | async-start | bytes 327680 | tf_op jit(solution)/shard_map/all_to_all | solution.py:34

commit v2 on v1

--- a/solution.py
+++ b/solution.py
@@ -25,7 +25,6 @@
     plane = [[(2 * k + c) * n_front + f for c in range(2) for f in range(n_front)] for k in range(n_z)]
     z_all = [[2 * k + c for k in range(n_z)] for c in range(2)]
     z_half = [[2 * (h * half + k) + c for k in range(half)] for h in range(2) for c in range(2)]
-    leaf_half = [list(range(h * n_z, (h + 1) * n_z)) for h in range(2)]
 
     def a2a_plane(v):
         return lax.all_to_all(v, ("leaf", "front"), 0, 0, axis_index_groups=plane)
@@ -65,57 +64,66 @@
             + jnp.dot(m[1], v[1], preferred_element_type=f32)
         ).reshape(n_front, WIN, n_rhs)
 
+    def fold(v):
+        return v[:n_front].astype(f32) + v[n_front:].astype(f32)
+
+    def by_core(v):
+        return jnp.broadcast_to(v[:, None], (2, n_front) + v.shape[1:]).reshape((2 * n_front,) + v.shape[1:])
+
+    swap = [(k, k ^ 1) for k in range(n_leaf)]
     mask0 = piece_mask(2 * z8, 2, live[0][node])
     mask1 = piece_mask(z, 1, live[1][0])
-    rows = front_id * sep_dev + jnp.arange(sep_dev)
-    rows_mask = (rows < live[0][node] * BLK).astype(f32)[:, None]
 
     got = a2a_plane(cut(forcing[0]))
-    low0 = a2a_plane(cut(jnp.concatenate([lower_upd[0], lower_inv[0]], 1)))
-    up1 = a2a_plane(cut(upper_inv[0, :, w0:]))
-    g0, linv0, linv1 = low0[:, :, :w0], low0[:, :, w0 : 2 * w0], low0[:, :, 2 * w0 :]
+    pair = fold(got).astype(bf).reshape(half, 2 * WIN, n_rhs)
+    r0 = total(a2a_leaf(pair, z_half)).reshape(2, WIN, n_rhs)
+    rm0 = join(a2a_plane(by_core((mask0 * r0).astype(bf))))
 
-    pair = got[:n_front].astype(f32) + got[n_front:].astype(f32)
-    pair = pair.astype(bf).reshape(half, 2 * WIN, n_rhs)
-    r0 = total(a2a_leaf(pair, z_half)).reshape(2, WIN, n_rhs)
-    rm0 = (mask0 * r0).astype(bf)
+    c_part = jnp.dot(lower_upd[0], rm0, preferred_element_type=f32).astype(bf)
+    y_part = jnp.dot(lower_inv[0, :, :w0], rm0, preferred_element_type=f32).astype(bf)
+    root = cut(jnp.concatenate([lower_inv[0, :, w0:], upper_inv[0, :, w0:]], 1))
+    got = a2a_plane(jnp.concatenate([cut(jnp.concatenate([c_part, y_part], 1)), root], 2))
+    parts = fold(got[:, :, : 2 * n_rhs]).astype(bf)
+    linv1 = got[:, :, 2 * n_rhs : 2 * n_rhs + w1]
+    uinv1 = got[:, :, 2 * n_rhs + w1 :]
 
-    def gather_two(v):
-        got = a2a_plane(spread(v, 2 * n_front))
-        return jnp.concatenate([join(got[:, 0]), join(got[:, 1])], 0)
-
-    rm0 = gather_two(rm0)
-    c_part = times(g0, rm0).astype(bf)
-    y_part = times(linv0, rm0).astype(bf).reshape(half, 2 * WIN, n_rhs)
+    c_part = parts[:, :, :n_rhs]
+    y_part = parts[:, :, n_rhs:].reshape(half, 2 * WIN, n_rhs)
     zero = jnp.zeros_like(y_part)
     first = node == 0
     y_part = jnp.concatenate([jnp.where(first, y_part, zero), jnp.where(first, zero, y_part)], 0)
     got = total(a2a_leaf(jnp.concatenate([c_part, y_part], 1), z_all))
     r1 = (mask1[0] * -got[:WIN]).astype(bf)
     y0 = (mask0 * got[WIN:].reshape(2, WIN, n_rhs)).astype(bf)
-    got = a2a_plane(spread(jnp.concatenate([r1[None], y0], 0), 2 * n_front))
-    r1 = join(got[:, 0])
-    y0 = jnp.concatenate([join(got[:, 1]), join(got[:, 2])], 0)
+    got = a2a_plane(by_core(jnp.concatenate([jnp.stack([r1, r1]), y0], 1)))
+    r1 = join(got[:, :WIN])
+    y0 = join(got[:, WIN:])
 
     y1 = total(a2a_leaf(times(linv1, r1).astype(bf), z_all))
     y1 = (mask1[0] * y1).astype(bf)
     y1 = join(a2a_plane(spread(y1, 2 * n_front)))
 
-    x_part = times(up1, y1).astype(bf).reshape(half, 2 * WIN, n_rhs)
+    x_part = times(uinv1, y1).astype(bf).reshape(half, 2 * WIN, n_rhs)
     x1 = total(a2a_leaf(jnp.concatenate([x_part, x_part], 0), z_all)).reshape(2, WIN, n_rhs)
     x1 = (piece_mask(2 * z8, 2, live[1][0]) * x1).astype(bf)
-    x1_all = a2a_leaf(spread(x1, half), z_half).reshape(n_front, WIN, n_rhs)
-    x1_out = join(a2a_plane(jnp.concatenate([x1_all, x1_all], 0)))
-    x1 = gather_two(x1)
+    x1c = join(a2a_plane(by_core(x1)))
 
-    y0 = lax.dynamic_slice_in_dim(y0, core * w0, w0, 0)
-    x1 = lax.dynamic_slice_in_dim(x1, core * w0, w0, 0)
     term = jnp.dot(upper_inv[0, :, :w0], y0, preferred_element_type=f32) - jnp.dot(
-        upper_upd[0], x1, preferred_element_type=f32
+        upper_upd[0], x1c, preferred_element_type=f32
     )
-    term = total(a2a_leaf(term.astype(bf).reshape(n_z, sep_dev // n_z, n_rhs), leaf_half))
-    x0 = a2a_leaf(spread(term.astype(bf), n_z), leaf_half).reshape(sep_dev, n_rhs)
-    x0 = (rows_mask * x0).astype(bf)
+    term = term.reshape(2, half, PIECE, n_rhs)
+    away = lax.dynamic_index_in_dim(term, 1 - core, 0, False).astype(bf)
+    keep = lax.dynamic_index_in_dim(term, core, 0, False)
+    term = (keep + lax.ppermute(away, "leaf", swap).astype(f32)).astype(bf)
+    got = a2a_leaf(jnp.concatenate([term, spread(x1.reshape(2 * WIN, n_rhs), half)], 1), z_half)
+    x1_out = got[:, PIECE:].reshape(n_front, WIN, n_rhs)
+    x1_out = join(a2a_plane(jnp.concatenate([x1_out, x1_out], 0)))
+
+    rows = front_id * sep_dev + (core * half + z8) * PIECE + jnp.arange(PIECE)
+    x0 = total(got[:, :PIECE]) * (rows < live[0][node] * BLK).astype(f32)[:, None]
+    x0 = a2a_leaf(spread(x0.astype(bf), half), z_half).reshape(half * PIECE, n_rhs)
+    other = lax.ppermute(x0, "leaf", swap)
+    x0 = jnp.where(core == 0, jnp.concatenate([x0, other], 0), jnp.concatenate([other, x0], 0))
     return jnp.stack([x0, x1_out])[:, None]
 
 

time: 305 us -> 255 us (0.84)
  waiting for transfers between devices: 155 us -> 107 us
  blocking collectives: 17.8 us -> 49.7 us
  starting transfers between devices: 89.5 us -> 74.3 us
  local copies, waits for them, and re-layouts: 22.6 us -> 10.2 us
    all_to_all x7 -> x5, waiting for transfers between devices: 81.2 us -> 52.4 us  [a2a_plane(): return lax.all_to_all(v, ('leaf', 'front'), 0, 0, axis_index_groups=plane)]
    all_to_all x7 -> x5, waiting for transfers between devices: 74.2 us -> 53 us  [a2a_leaf(): return lax.all_to_all(v, 'leaf', 0, 0, axis_index_groups=groups)]
    all_to_all x0 -> x1, blocking collectives: none -> 17.4 us  [a2a_leaf(): return lax.all_to_all(v, 'leaf', 0, 0, axis_index_groups=groups)]
    all_to_all x1 -> x2, blocking collectives: 17.8 us -> 32.3 us  [a2a_plane(): return lax.all_to_all(v, ('leaf', 'front'), 0, 0, axis_index_groups=plane)]
    all_to_all x7 -> x5, starting transfers between devices: 43 us -> 31.7 us  [a2a_leaf(): return lax.all_to_all(v, 'leaf', 0, 0, axis_index_groups=groups)]
    all_to_all x7 -> x5, starting transfers between devices: 46.4 us -> 36.3 us  [a2a_plane(): return lax.all_to_all(v, ('leaf', 'front'), 0, 0, axis_index_groups=plane)]
    ppermute x0 -> x2, starting transfers between devices: none -> 6.42 us  [the longest x1 3.91 us: body(): other = lax.ppermute(x0, 'leaf', swap)]
    unnamed x22 -> x26, local copies, waits for them, and re-layouts: 4.52 us -> 0.58 us
  transfers between devices with their start and end apart: 14 -> 12, of which waited for: 14 -> 12; matrix products, arithmetic and copies ran while one was open for 7% -> 2% of each run, Pallas kernels for 0% -> 0%
where the time goes in v2:
time: 255 us; the launch traced here: 254 us
  waiting for transfers between devices  107 us (42%)
  starting transfers between devices  74.3 us (29%)
  blocking collectives  49.7 us (19%)
  local copies, waits for them, and re-layouts  10.2 us (4%)
  other arithmetic  9.25 us (4%)
    all_to_all x5, waiting for transfers between devices, a2a_leaf(): return lax.all_to_all(v, 'leaf', 0, 0, axis_index_groups=groups)  53 us
    all_to_all x5, waiting for transfers between devices, a2a_plane(): return lax.all_to_all(v, ('leaf', 'front'), 0, 0, axis_index_groups=plane)  52.4 us
    all_to_all x5, starting transfers between devices, a2a_plane(): return lax.all_to_all(v, ('leaf', 'front'), 0, 0, axis_index_groups=plane)  36.3 us
    all_to_all x2, blocking collectives, a2a_plane(): return lax.all_to_all(v, ('leaf', 'front'), 0, 0, axis_index_groups=plane)  32.3 us
    all_to_all x5, starting transfers between devices, a2a_leaf(): return lax.all_to_all(v, 'leaf', 0, 0, axis_index_groups=groups)  31.7 us
    all_to_all x1, blocking collectives, a2a_leaf(): return lax.all_to_all(v, 'leaf', 0, 0, axis_index_groups=groups)  17.4 us
  transfers between devices with their start and end apart: 12, of which 12 were waited for; matrix products, arithmetic and copies ran while one was open for 2% of the time, Pallas kernels for 0%

profile of v2, /device:TPU:1, one launch (start us, length us, event | category | flops | bytes accessed | tf_op | source)
XLA Modules:
  0.0 254.2 jit_solution(15107336428991252127)
XLA Ops:
  0.0 1.0 fusion.27
  1.1 17.8 %all_to_all.65 = bf16[32,24,128]{2,1,0:T(8,128)(2,1)S(1)} all-to-all(bf16[32,24,128]{2,1,0:T(8,128)(2,1)S(1)} %pad_maximum_fusion.2), channel_id=1, replica_groups={{0,1,2,3,4,5,6,7,8,9,10,11,12,13,14,15,16,17,18,19,20,21,22,23,24,25,26..., dimensions={0} | all-to-all | bytes 393216 | tf_op jit(solution)/shard_map/all_to_all | solution.py:30
  18.9 0.7 add_convert_fusion.1
  19.6 11.0 %all-to-all-start.1 = ((bf16[8,48,128]{2,1,0:T(8,128)(2,1)}), bf16[8,48,128]{2,1,0:T(8,128)(2,1)S(1)}, u32[]{:S(2)}, u32[]{:S(2)}) async-start(bf16[8,48,128]{2,1,0:T(8,128)(2,1)} %bitcast.3), calls=%async_computation.1 | async-start | bytes 196608 | tf_op jit(solution)/shard_map/all_to_all | solution.py:33
  31.9 0.6 fusion.28
  32.5 0.7 compare_convert_fusion.1
  33.2 7.5 %all-to-all-done.1 = bf16[8,48,128]{2,1,0:T(8,128)(2,1)S(1)} async-done(((bf16[8,48,128]{2,1,0:T(8,128)(2,1)}), bf16[8,48,128]{2,1,0:T(8,128)(2,1)S(1)}, u32[]{:S(2)}, u32[]{:S(2)}) %all-to-all-start.1) | async-done | bytes 98336 | tf_op jit(solution)/shard_map/all_to_all | solution.py:33
  40.8 0.7 broadcast_in_dim.16
  41.5 6.5 %all-to-all-start.2 = ((bf16[32,24,128]{2,1,0:T(8,128)(2,1)}), bf16[32,24,128]{2,1,0:T(8,128)(2,1)}, u32[]{:S(2)}, u32[]{:S(2)}) async-start(bf16[32,24,128]{2,1,0:T(8,128)(2,1)} %bitcast.5), calls=%async_computation.2 | async-start | bytes 393216 | tf_op jit(solution)/shard_map/all_to_all | solution.py:30
  48.7 7.4 %all-to-all-done.2 = bf16[32,24,128]{2,1,0:T(8,128)(2,1)} async-done(((bf16[32,24,128]{2,1,0:T(8,128)(2,1)}), bf16[32,24,128]{2,1,0:T(8,128)(2,1)}, u32[]{:S(2)}, u32[]{:S(2)}) %all-to-all-start.2) | async-done | bytes 196640 | tf_op jit(solution)/shard_map/all_to_all | solution.py:30
  56.1 0.8 slice.202
  57.0 0.9 slice.201
  59.0 1.3 fusion.1
  60.2 4.3 %all-to-all-start.3 = ((bf16[32,24,896]{2,1,0:T(8,128)(2,1)}), bf16[32,24,896]{2,1,0:T(8,128)(2,1)S(1)}, u32[]{:S(2)}, u32[]{:S(2)}) async-start(bf16[32,24,896]{2,1,0:T(8,128)(2,1)} %fusion.1), calls=%async_computation.3 | async-start | bytes 2752512 | tf_op jit(solution)/shard_map/all_to_all | solution.py:30
  64.6 20.6 %all-to-all-done.3 = bf16[32,24,896]{2,1,0:T(8,128)(2,1)S(1)} async-done(((bf16[32,24,896]{2,1,0:T(8,128)(2,1)}), bf16[32,24,896]{2,1,0:T(8,128)(2,1)S(1)}, u32[]{:S(2)}, u32[]{:S(2)}) %all-to-all-start.3) | async-done | bytes 1376288 | tf_op jit(solution)/shard_map/all_to_all | solution.py:30
  85.2 0.7 maximum_maximum_fusion
  86.0 7.4 %all-to-all-start.4 = ((bf16[16,72,128]{2,1,0:T(8,128)(2,1)}), bf16[16,72,128]{2,1,0:T(8,128)(2,1)S(1)}, u32[]{:S(2)}, u32[]{:S(2)}) async-start(bf16[16,72,128]{2,1,0:T(8,128)(2,1)} %maximum_maximum_fusion), calls=%async_computation.4 | async-start | bytes 589824 | tf_op jit(solution)/shard_map/all_to_all | solution.py:33
  93.4 13.5 %all-to-all-done.4 = bf16[16,72,128]{2,1,0:T(8,128)(2,1)S(1)} async-done(((bf16[16,72,128]{2,1,0:T(8,128)(2,1)}), bf16[16,72,128]{2,1,0:T(8,128)(2,1)S(1)}, u32[]{:S(2)}, u32[]{:S(2)}) %all-to-all-start.4) | async-done | bytes 294944 | tf_op jit(solution)/shard_map/all_to_all | solution.py:33
  107.1 0.8 broadcast_in_dim.18
  107.9 10.6 %all-to-all-start.5 = ((bf16[32,48,128]{2,1,0:T(8,128)(2,1)}), bf16[32,48,128]{2,1,0:T(8,128)(2,1)S(1)}, u32[]{:S(2)}, u32[]{:S(2)}) async-start(bf16[32,48,128]{2,1,0:T(8,128)(2,1)} %bitcast.18), calls=%async_computation.5 | async-start | bytes 786432 | tf_op jit(solution)/shard_map/all_to_all | solution.py:30
  118.5 1.0 fusion.22
  119.5 8.6 %all-to-all-done.5 = bf16[32,48,128]{2,1,0:T(8,128)(2,1)S(1)} async-done(((bf16[32,48,128]{2,1,0:T(8,128)(2,1)}), bf16[32,48,128]{2,1,0:T(8,128)(2,1)S(1)}, u32[]{:S(2)}, u32[]{:S(2)}) %all-to-all-start.5) | async-done | bytes 393248 | tf_op jit(solution)/shard_map/all_to_all | solution.py:30
  128.1 0.6 fusion.24
  128.8 0.7 fusion.23
  129.9 17.4 %all_to_all.66 = bf16[16,24,128]{2,1,0:T(8,128)(2,1)S(1)} all-to-all(bf16[16,24,128]{2,1,0:T(8,128)(2,1)S(1)} %bitcast.93), channel_id=1, replica_groups={{0,32,64,96,128,160,192,224,256,288,320,352,384,416,448,480},{16,48,80,..., dimensions={0} | all-to-all | bytes 196608 | tf_op jit(solution)/shard_map/all_to_all | solution.py:33
  147.5 14.5 %all_to_all.67 = bf16[32,24,128]{2,1,0:T(8,128)(2,1)S(1)} all-to-all(bf16[32,24,128]{2,1,0:T(8,128)(2,1)S(1)} %broadcast_in_dim.19), channel_id=1, replica_groups={{0,1,2,3,4,5,6,7,8,9,10,11,12,13,14,15,16,17,18,19,20,21,22,23,24,25,26..., dimensions={0} | all-to-all | bytes 393216 | tf_op jit(solution)/shard_map/all_to_all | solution.py:30
  162.5 0.7 pad_maximum_fusion.3
  163.2 3.5 %all-to-all-start.8 = ((bf16[16,48,128]{2,1,0:T(8,128)(2,1)}), bf16[16,48,128]{2,1,0:T(8,128)(2,1)S(1)}, u32[]{:S(2)}, u32[]{:S(2)}) async-start(bf16[16,48,128]{2,1,0:T(8,128)(2,1)} %pad_maximum_fusion.3), calls=%async_computation.8 | async-start | bytes 393216 | tf_op jit(solution)/shard_map/all_to_all | solution.py:33
  167.4 11.8 %all-to-all-done.8 = bf16[16,48,128]{2,1,0:T(8,128)(2,1)S(1)} async-done(((bf16[16,48,128]{2,1,0:T(8,128)(2,1)}), bf16[16,48,128]{2,1,0:T(8,128)(2,1)S(1)}, u32[]{:S(2)}, u32[]{:S(2)}) %all-to-all-start.8) | async-done | bytes 196640 | tf_op jit(solution)/shard_map/all_to_all | solution.py:33
  179.2 0.8 multiply_convert_fusion.1
  180.0 0.7 broadcast_in_dim.20
  180.7 7.9 %all-to-all-start.9 = ((bf16[32,24,128]{2,1,0:T(8,128)(2,1)}), bf16[32,24,128]{2,1,0:T(8,128)(2,1)S(1)}, u32[]{:S(2)}, u32[]{:S(2)}) async-start(bf16[32,24,128]{2,1,0:T(8,128)(2,1)} %bitcast.32), calls=%async_computation.9 | async-start | bytes 393216 | tf_op jit(solution)/shard_map/all_to_all | solution.py:30
  189.0 7.7 %all-to-all-done.9 = bf16[32,24,128]{2,1,0:T(8,128)(2,1)S(1)} async-done(((bf16[32,24,128]{2,1,0:T(8,128)(2,1)}), bf16[32,24,128]{2,1,0:T(8,128)(2,1)S(1)}, u32[]{:S(2)}, u32[]{:S(2)}) %all-to-all-start.9) | async-done | bytes 196640 | tf_op jit(solution)/shard_map/all_to_all | solution.py:30
  197.4 2.5 collective-permute-start
  200.0 0.8 collective-permute-done
  200.9 0.7 pad_maximum_fusion.5
  201.6 5.1 %all-to-all-start.10 = ((bf16[8,88,128]{2,1,0:T(8,128)(2,1)}), bf16[8,88,128]{2,1,0:T(8,128)(2,1)S(1)}, u32[]{:S(2)}, u32[]{:S(2)}) async-start(bf16[8,88,128]{2,1,0:T(8,128)(2,1)} %pad_maximum_fusion.5), calls=%async_computation.10 | async-start | bytes 360448 | tf_op jit(solution)/shard_map/all_to_all | solution.py:33
  206.6 0.6 compare_convert_fusion
  207.3 10.4 %all-to-all-done.10 = bf16[8,88,128]{2,1,0:T(8,128)(2,1)S(1)} async-done(((bf16[8,88,128]{2,1,0:T(8,128)(2,1)}), bf16[8,88,128]{2,1,0:T(8,128)(2,1)S(1)}, u32[]{:S(2)}, u32[]{:S(2)}) %all-to-all-start.10) | async-done | bytes 180256 | tf_op jit(solution)/shard_map/all_to_all | solution.py:33
  217.7 0.7 pad_maximum_fusion.4
  218.4 6.9 %all-to-all-start.12 = ((bf16[32,24,128]{2,1,0:T(8,128)(2,1)}), bf16[32,24,128]{2,1,0:T(8,128)(2,1)S(1)}, u32[]{:S(2)}, u32[]{:S(2)}) async-start(bf16[32,24,128]{2,1,0:T(8,128)(2,1)} %pad_maximum_fusion.4), calls=%async_computation.12 | async-start | bytes 393216 | tf_op jit(solution)/shard_map/all_to_all | solution.py:30
  225.4 8.0 %all-to-all-done.12 = bf16[32,24,128]{2,1,0:T(8,128)(2,1)S(1)} async-done(((bf16[32,24,128]{2,1,0:T(8,128)(2,1)}), bf16[32,24,128]{2,1,0:T(8,128)(2,1)S(1)}, u32[]{:S(2)}, u32[]{:S(2)}) %all-to-all-start.12) | async-done | bytes 196640 | tf_op jit(solution)/shard_map/all_to_all | solution.py:30
  233.4 0.6 broadcast_in_dim.22
  234.0 4.6 %all-to-all-start.11 = ((bf16[8,40,128]{2,1,0:T(8,128)(2,1)}), bf16[8,40,128]{2,1,0:T(8,128)(2,1)S(1)}, u32[]{:S(2)}, u32[]{:S(2)}) async-start(bf16[8,40,128]{2,1,0:T(8,128)(2,1)} %broadcast_in_dim.22), calls=%async_computation.11 | async-start | bytes 163840 | tf_op jit(solution)/shard_map/all_to_all | solution.py:33
  238.7 9.9 %all-to-all-done.11 = bf16[8,40,128]{2,1,0:T(8,128)(2,1)S(1)} async-done(((bf16[8,40,128]{2,1,0:T(8,128)(2,1)}), bf16[8,40,128]{2,1,0:T(8,128)(2,1)S(1)}, u32[]{:S(2)}, u32[]{:S(2)}) %all-to-all-start.11) | async-done | bytes 81952 | tf_op jit(solution)/shard_map/all_to_all | solution.py:33
  248.6 3.9 %collective-permute-start.1 = (bf16[320,128]{1,0:T(8,128)(2,1)S(1)}, bf16[320,128]{1,0:T(8,128)(2,1)S(1)}, u32[]{:S(2)}, u32[]{:S(2)}) collective-permute-start(bf16[320,128]{1,0:T(8,128)(2,1)S(1)} %bitcast.97), channel_id=1, source_target_pairs={{0,16},{16,0},{32,48},{48,32},{64,80},{80,64},{96,112},{112,96},{1... | collective-permute-start | bytes 245768 | tf_op jit(solution)/shard_map/ppermute | solution.py:125
  252.5 0.9 collective-permute-done.1
  253.4 0.8 maximum_bitcast_fusion
  (83 shorter events, 5.7 us)
Async XLA Ops:
  0.0 58.3 %copy-start = (bf16[1,640,640]{2,1,0:T(8,128)(2,1)S(1)}, bf16[1,640,640]{2,1,0:T(8,128)(2,1)}, u32[]{:S(2)}) copy-start(bf16[1,640,640]{2,1,0:T(8,128)(2,1)} %param.9) | copy-start | bytes 2457604
  0.0 30.6 %copy-start.11 = (s32[2,32]{1,0:T(2,128)S(1)}, s32[2,32]{1,0:T(2,128)}, u32[]{:S(2)}) copy-start(s32[2,32]{1,0:T(2,128)} %param.7) | copy-start | bytes 772
  0.0 31.8 %slice-start.2 = ((s32[2,32]{1,0:T(2,128)}), s32[1,32]{1,0:T(1,128)S(1)}, s32[]{:S(2)}) async-start(s32[2,32]{1,0:T(2,128)} %param.7), calls=%async_computation.15 | async-start | bytes 1024 | tf_op jit(solution)/shard_map/slice | solution.py:74
  1.1 46.9 %slice-start = ((bf16[1,640,960]{1,2,0:T(8,128)(2,1)}), bf16[1,640,320]{1,2,0:T(8,128)(2,1)S(1)}, s32[]{:S(2)}) async-start(bf16[1,640,960]{1,2,0:T(8,128)(2,1)} %param.8), calls=%async_computation.13 | async-start | bytes 819200 | tf_op jit(solution)/shard_map/slice | solution.py:84
  19.6 21.1 %all-to-all-start.1 = ((bf16[8,48,128]{2,1,0:T(8,128)(2,1)}), bf16[8,48,128]{2,1,0:T(8,128)(2,1)S(1)}, u32[]{:S(2)}, u32[]{:S(2)}) async-start(bf16[8,48,128]{2,1,0:T(8,128)(2,1)} %bitcast.3), calls=%async_computation.1 | async-start | bytes 196608 | tf_op jit(solution)/shard_map/all_to_all | solution.py:33
  33.2 133.6 %copy-start.9 = (f32[2,24]{1,0:T(2,128)}, f32[2,24]{1,0:T(2,128)S(1)}, u32[]{:S(2)}) copy-start(f32[2,24]{1,0:T(2,128)S(1)} %get-tuple-element.24) | copy-start | bytes 580
  41.5 6.8 %slice-start.1 = ((bf16[1,640,960]{1,2,0:T(8,128)(2,1)}), bf16[1,640,320]{1,2,0:T(8,128)(2,1)S(1)}, s32[]{:S(2)}) async-start(bf16[1,640,960]{1,2,0:T(8,128)(2,1)} %param.10), calls=%async_computation.14 | async-start | bytes 819200 | tf_op jit(solution)/shard_map/slice | solution.py:84
  41.5 14.6 %all-to-all-start.2 = ((bf16[32,24,128]{2,1,0:T(8,128)(2,1)}), bf16[32,24,128]{2,1,0:T(8,128)(2,1)}, u32[]{:S(2)}, u32[]{:S(2)}) async-start(bf16[32,24,128]{2,1,0:T(8,128)(2,1)} %bitcast.5), calls=%async_computation.2 | async-start | bytes 393216 | tf_op jit(solution)/shard_map/all_to_all | solution.py:30
  48.3 9.6 %copy-start.1 = (bf16[1,640,960]{1,2,0:T(8,128)(2,1)S(1)}, bf16[1,640,960]{1,2,0:T(8,128)(2,1)}, u32[]{:S(2)}) copy-start(bf16[1,640,960]{1,2,0:T(8,128)(2,1)} %param.8) | copy-start | bytes 3686404
  60.2 24.9 %all-to-all-start.3 = ((bf16[32,24,896]{2,1,0:T(8,128)(2,1)}), bf16[32,24,896]{2,1,0:T(8,128)(2,1)S(1)}, u32[]{:S(2)}, u32[]{:S(2)}) async-start(bf16[32,24,896]{2,1,0:T(8,128)(2,1)} %fusion.1), calls=%async_computation.3 | async-start | bytes 2752512 | tf_op jit(solution)/shard_map/all_to_all | solution.py:30
  86.0 20.9 %all-to-all-start.4 = ((bf16[16,72,128]{2,1,0:T(8,128)(2,1)}), bf16[16,72,128]{2,1,0:T(8,128)(2,1)S(1)}, u32[]{:S(2)}, u32[]{:S(2)}) async-start(bf16[16,72,128]{2,1,0:T(8,128)(2,1)} %maximum_maximum_fusion), calls=%async_computation.4 | async-start | bytes 589824 | tf_op jit(solution)/shard_map/all_to_all | solution.py:33
  107.9 20.2 %all-to-all-start.5 = ((bf16[32,48,128]{2,1,0:T(8,128)(2,1)}), bf16[32,48,128]{2,1,0:T(8,128)(2,1)S(1)}, u32[]{:S(2)}, u32[]{:S(2)}) async-start(bf16[32,48,128]{2,1,0:T(8,128)(2,1)} %bitcast.18), calls=%async_computation.5 | async-start | bytes 786432 | tf_op jit(solution)/shard_map/all_to_all | solution.py:30
  119.5 10.2 %copy-start.3 = (bf16[16,24,320]{2,1,0:T(8,128)(2,1)S(1)}, bf16[16,24,320]{2,1,0:T(8,128)(2,1)}, u32[]{:S(2)}) copy-start(bf16[16,24,320]{2,1,0:T(8,128)(2,1)} %get-tuple-element.6) | copy-start | bytes 737284
  162.0 5.4 %copy-start.5 = (bf16[16,24,128]{2,1,0:T(8,128)(2,1)S(1)}, bf16[16,24,128]{2,1,0:T(8,128)(2,1)}, u32[]{:S(2)}) copy-start(bf16[16,24,128]{2,1,0:T(8,128)(2,1)} %get-tuple-element.9) | copy-start | bytes 294916
  162.0 5.4 %copy-start.6 = (bf16[16,16,128]{2,1,0:T(8,128)(2,1)S(1)}, bf16[16,16,128]{2,1,0:T(8,128)(2,1)}, u32[]{:S(2)}) copy-start(bf16[16,16,128]{2,1,0:T(8,128)(2,1)} %get-tuple-element.11) | copy-start | bytes 196612
  162.3 26.4 %copy-start.2 = (bf16[1,640,960]{1,2,0:T(8,128)(2,1)S(1)}, bf16[1,640,960]{1,2,0:T(8,128)(2,1)}, u32[]{:S(2)}) copy-start(bf16[1,640,960]{1,2,0:T(8,128)(2,1)} %param.10) | copy-start | bytes 3686404
  163.2 16.0 %all-to-all-start.8 = ((bf16[16,48,128]{2,1,0:T(8,128)(2,1)}), bf16[16,48,128]{2,1,0:T(8,128)(2,1)S(1)}, u32[]{:S(2)}, u32[]{:S(2)}) async-start(bf16[16,48,128]{2,1,0:T(8,128)(2,1)} %pad_maximum_fusion.3), calls=%async_computation.8 | async-start | bytes 393216 | tf_op jit(solution)/shard_map/all_to_all | solution.py:33
  167.4 29.4 %copy-start.4 = (bf16[1,640,640]{2,1,0:T(8,128)(2,1)S(1)}, bf16[1,640,640]{2,1,0:T(8,128)(2,1)}, u32[]{:S(2)}) copy-start(bf16[1,640,640]{2,1,0:T(8,128)(2,1)} %param.11) | copy-start | bytes 2457604
  179.2 9.4 %copy-start.7 = (f32[48,128]{1,0:T(8,128)}, f32[48,128]{1,0:T(8,128)S(1)}, u32[]{:S(2)}) copy-start(f32[48,128]{1,0:T(8,128)S(1)} %convert_reduce_fusion.1) | copy-start | bytes 73732
  180.7 16.1 %all-to-all-start.9 = ((bf16[32,24,128]{2,1,0:T(8,128)(2,1)}), bf16[32,24,128]{2,1,0:T(8,128)(2,1)S(1)}, u32[]{:S(2)}, u32[]{:S(2)}) async-start(bf16[32,24,128]{2,1,0:T(8,128)(2,1)} %bitcast.32), calls=%async_computation.9 | async-start | bytes 393216 | tf_op jit(solution)/shard_map/all_to_all | solution.py:30
  196.8 3.2 %copy-start.8 = (f32[48,128]{1,0:T(8,128)S(1)}, f32[48,128]{1,0:T(8,128)}, u32[]{:S(2)}) copy-start(f32[48,128]{1,0:T(8,128)} %copy-done.7) | copy-start | bytes 73732
  196.8 3.2 %copy-start.10 = (f32[48]{0:T(128)S(1)}, f32[48]{0:T(128)}, u32[]{:S(2)}) copy-start(f32[48]{0:T(128)} %reshape.297) | copy-start | bytes 580
  197.4 3.4 %collective-permute-start = (bf16[8,40,128]{2,1,0:T(8,128)(2,1)S(1)}, bf16[8,40,128]{2,1,0:T(8,128)(2,1)S(1)}, u32[]{:S(2)}, u32[]{:S(2)}) collective-permute-start(bf16[8,40,128]{2,1,0:T(8,128)(2,1)S(1)} %fusion.16), channel_id=1, source_target_pairs={{0,16},{16,0},{32,48},{48,32},{64,80},{80,64},{96,112},{112,96},{1... | collective-permute-start | bytes 245768 | tf_op jit(solution)/shard_map/ppermute | solution.py:117
  201.6 16.1 %all-to-all-start.10 = ((bf16[8,88,128]{2,1,0:T(8,128)(2,1)}), bf16[8,88,128]{2,1,0:T(8,128)(2,1)S(1)}, u32[]{:S(2)}, u32[]{:S(2)}) async-start(bf16[8,88,128]{2,1,0:T(8,128)(2,1)} %pad_maximum_fusion.5), calls=%async_computation.10 | async-start | bytes 360448 | tf_op jit(solution)/shard_map/all_to_all | solution.py:33
  218.4 15.0 %all-to-all-start.12 = ((bf16[32,24,128]{2,1,0:T(8,128)(2,1)}), bf16[32,24,128]{2,1,0:T(8,128)(2,1)S(1)}, u32[]{:S(2)}, u32[]{:S(2)}) async-start(bf16[32,24,128]{2,1,0:T(8,128)(2,1)} %pad_maximum_fusion.4), calls=%async_computation.12 | async-start | bytes 393216 | tf_op jit(solution)/shard_map/all_to_all | solution.py:30
  234.0 14.5 %all-to-all-start.11 = ((bf16[8,40,128]{2,1,0:T(8,128)(2,1)}), bf16[8,40,128]{2,1,0:T(8,128)(2,1)S(1)}, u32[]{:S(2)}, u32[]{:S(2)}) async-start(bf16[8,40,128]{2,1,0:T(8,128)(2,1)} %broadcast_in_dim.22), calls=%async_computation.11 | async-start | bytes 163840 | tf_op jit(solution)/shard_map/all_to_all | solution.py:33
  248.6 4.8 %collective-permute-start.1 = (bf16[320,128]{1,0:T(8,128)(2,1)S(1)}, bf16[320,128]{1,0:T(8,128)(2,1)S(1)}, u32[]{:S(2)}, u32[]{:S(2)}) collective-permute-start(bf16[320,128]{1,0:T(8,128)(2,1)S(1)} %bitcast.97), channel_id=1, source_target_pairs={{0,16},{16,0},{32,48},{48,32},{64,80},{80,64},{96,112},{112,96},{1... | collective-permute-start | bytes 245768 | tf_op jit(solution)/shard_map/ppermute | solution.py:125

commit v3 on v2

--- a/solution.py
+++ b/solution.py
@@ -106,7 +106,10 @@
     x_part = times(uinv1, y1).astype(bf).reshape(half, 2 * WIN, n_rhs)
     x1 = total(a2a_leaf(jnp.concatenate([x_part, x_part], 0), z_all)).reshape(2, WIN, n_rhs)
     x1 = (piece_mask(2 * z8, 2, live[1][0]) * x1).astype(bf)
-    x1c = join(a2a_plane(by_core(x1)))
+    own = jnp.broadcast_to(x1[None, None], (2, n_front // 2) + x1.shape).reshape(2 * n_front, WIN, n_rhs)
+    got = a2a_plane(jnp.concatenate([by_core(x1), own], 1))
+    x1c = join(got[:, :WIN])
+    own = join(got[:, WIN:])
 
     term = jnp.dot(upper_inv[0, :, :w0], y0, preferred_element_type=f32) - jnp.dot(
         upper_upd[0], x1c, preferred_element_type=f32
@@ -115,16 +118,17 @@
     away = lax.dynamic_index_in_dim(term, 1 - core, 0, False).astype(bf)
     keep = lax.dynamic_index_in_dim(term, core, 0, False)
     term = (keep + lax.ppermute(away, "leaf", swap).astype(f32)).astype(bf)
-    got = a2a_leaf(jnp.concatenate([term, spread(x1.reshape(2 * WIN, n_rhs), half)], 1), z_half)
-    x1_out = got[:, PIECE:].reshape(n_front, WIN, n_rhs)
-    x1_out = join(a2a_plane(jnp.concatenate([x1_out, x1_out], 0)))
+    own = lax.dynamic_index_in_dim(own.reshape(2, half, PIECE, n_rhs), core, 0, False)
+    got = a2a_leaf(jnp.concatenate([term, own], 1), z_half)
 
     rows = front_id * sep_dev + (core * half + z8) * PIECE + jnp.arange(PIECE)
     x0 = total(got[:, :PIECE]) * (rows < live[0][node] * BLK).astype(f32)[:, None]
-    x0 = a2a_leaf(spread(x0.astype(bf), half), z_half).reshape(half * PIECE, n_rhs)
-    other = lax.ppermute(x0, "leaf", swap)
-    x0 = jnp.where(core == 0, jnp.concatenate([x0, other], 0), jnp.concatenate([other, x0], 0))
-    return jnp.stack([x0, x1_out])[:, None]
+    x1 = lax.dynamic_index_in_dim(got[:, PIECE:], front_id // 2, 0, False)
+    both = a2a_leaf(spread(jnp.stack([x0.astype(bf), x1]), half), z_half)
+    both = jnp.swapaxes(both, 0, 1).reshape(2, half * PIECE, n_rhs)
+    other = lax.ppermute(both, "leaf", swap)
+    both = jnp.where(core == 0, jnp.concatenate([both, other], 1), jnp.concatenate([other, both], 1))
+    return both[:, None]
 
 
 def solution(mesh):

time: 255 us -> 244 us (0.957)
  blocking collectives: 49.7 us -> 83 us
  waiting for transfers between devices: 107 us -> 78.8 us
  starting transfers between devices: 74.3 us -> 61.1 us
  local copies, waits for them, and re-layouts: 10.2 us -> 7.64 us
    all_to_all x1 -> x3, blocking collectives: 17.4 us -> 50.6 us  [a2a_leaf(): return lax.all_to_all(v, 'leaf', 0, 0, axis_index_groups=groups)]
    all_to_all x5 -> x3, waiting for transfers between devices: 53 us -> 31 us  [a2a_leaf(): return lax.all_to_all(v, 'leaf', 0, 0, axis_index_groups=groups)]
    all_to_all x5 -> x3, starting transfers between devices: 31.7 us -> 23 us  [a2a_leaf(): return lax.all_to_all(v, 'leaf', 0, 0, axis_index_groups=groups)]
    all_to_all x5 -> x4, waiting for transfers between devices: 52.4 us -> 45.8 us  [a2a_plane(): return lax.all_to_all(v, ('leaf', 'front'), 0, 0, axis_index_groups=plane)]
    all_to_all x5 -> x4, starting transfers between devices: 36.3 us -> 29.8 us  [a2a_plane(): return lax.all_to_all(v, ('leaf', 'front'), 0, 0, axis_index_groups=plane)]
  transfers between devices with their start and end apart: 12 -> 9, of which waited for: 12 -> 9; matrix products, arithmetic and copies ran while one was open for 2% -> 2% of each run, Pallas kernels for 0% -> 0%
where the time goes in v3:
time: 244 us; the launch traced here: 243 us
  blocking collectives  83 us (34%)
  waiting for transfers between devices  78.8 us (32%)
  starting transfers between devices  61.1 us (25%)
  other arithmetic  8.11 us (3%)
  local copies, waits for them, and re-layouts  7.64 us (3%)
  matrix products  3.58 us (1%)
    all_to_all x3, blocking collectives, a2a_leaf(): return lax.all_to_all(v, 'leaf', 0, 0, axis_index_groups=groups)  50.6 us
    all_to_all x4, waiting for transfers between devices, a2a_plane(): return lax.all_to_all(v, ('leaf', 'front'), 0, 0, axis_index_groups=plane)  45.8 us
    all_to_all x2, blocking collectives, a2a_plane(): return lax.all_to_all(v, ('leaf', 'front'), 0, 0, axis_index_groups=plane)  32.3 us
    all_to_all x3, waiting for transfers between devices, a2a_leaf(): return lax.all_to_all(v, 'leaf', 0, 0, axis_index_groups=groups)  31 us
    all_to_all x4, starting transfers between devices, a2a_plane(): return lax.all_to_all(v, ('leaf', 'front'), 0, 0, axis_index_groups=plane)  29.8 us
    all_to_all x3, starting transfers between devices, a2a_leaf(): return lax.all_to_all(v, 'leaf', 0, 0, axis_index_groups=groups)  23 us
    ppermute x1, starting transfers between devices, body(): other = lax.ppermute(both, 'leaf', swap)  5.11 us
  transfers between devices with their start and end apart: 9, of which 9 were waited for; matrix products, arithmetic and copies ran while one was open for 2% of the time, Pallas kernels for 0%

profile of v3, /device:TPU:1, one launch (start us, length us, event | category | flops | bytes accessed | tf_op | source)
XLA Modules:
  0.0 243.2 jit_solution(1458180195920661219)
XLA Ops:
  0.0 1.0 fusion.31
  1.1 17.8 %all_to_all.60 = bf16[32,24,128]{2,1,0:T(8,128)(2,1)S(1)} all-to-all(bf16[32,24,128]{2,1,0:T(8,128)(2,1)S(1)} %pad_maximum_fusion.3), channel_id=1, replica_groups={{0,1,2,3,4,5,6,7,8,9,10,11,12,13,14,15,16,17,18,19,20,21,22,23,24,25,26..., dimensions={0} | all-to-all | bytes 393216 | tf_op jit(solution)/shard_map/all_to_all | solution.py:30
  18.9 0.7 add_convert_fusion.1
  19.6 11.0 %all-to-all-start.1 = ((bf16[8,48,128]{2,1,0:T(8,128)(2,1)}), bf16[8,48,128]{2,1,0:T(8,128)(2,1)S(1)}, u32[]{:S(2)}, u32[]{:S(2)}) async-start(bf16[8,48,128]{2,1,0:T(8,128)(2,1)} %bitcast.3), calls=%async_computation.1 | async-start | bytes 196608 | tf_op jit(solution)/shard_map/all_to_all | solution.py:33
  30.6 0.5 slice.161
  31.7 0.7 fusion.32
  32.4 0.8 compare_convert_fusion.1
  33.2 7.5 %all-to-all-done.1 = bf16[8,48,128]{2,1,0:T(8,128)(2,1)S(1)} async-done(((bf16[8,48,128]{2,1,0:T(8,128)(2,1)}), bf16[8,48,128]{2,1,0:T(8,128)(2,1)S(1)}, u32[]{:S(2)}, u32[]{:S(2)}) %all-to-all-start.1) | async-done | bytes 98336 | tf_op jit(solution)/shard_map/all_to_all | solution.py:33
  40.8 0.7 broadcast_in_dim.14
  41.5 6.5 %all-to-all-start.2 = ((bf16[32,24,128]{2,1,0:T(8,128)(2,1)}), bf16[32,24,128]{2,1,0:T(8,128)(2,1)}, u32[]{:S(2)}, u32[]{:S(2)}) async-start(bf16[32,24,128]{2,1,0:T(8,128)(2,1)} %bitcast.5), calls=%async_computation.2 | async-start | bytes 393216 | tf_op jit(solution)/shard_map/all_to_all | solution.py:30
  48.0 0.3 copy.22
  48.3 0.3 copy.23
  48.7 7.4 %all-to-all-done.2 = bf16[32,24,128]{2,1,0:T(8,128)(2,1)} async-done(((bf16[32,24,128]{2,1,0:T(8,128)(2,1)}), bf16[32,24,128]{2,1,0:T(8,128)(2,1)}, u32[]{:S(2)}, u32[]{:S(2)}) %all-to-all-start.2) | async-done | bytes 196640 | tf_op jit(solution)/shard_map/all_to_all | solution.py:30
  56.1 0.8 slice.208
  57.0 0.9 slice.207
  57.9 0.4 fusion.4
  58.3 0.4 fusion.3
  59.0 1.3 fusion.1
  60.3 4.3 %all-to-all-start.3 = ((bf16[32,24,896]{2,1,0:T(8,128)(2,1)}), bf16[32,24,896]{2,1,0:T(8,128)(2,1)S(1)}, u32[]{:S(2)}, u32[]{:S(2)}) async-start(bf16[32,24,896]{2,1,0:T(8,128)(2,1)} %fusion.1), calls=%async_computation.3 | async-start | bytes 2752512 | tf_op jit(solution)/shard_map/all_to_all | solution.py:30
  64.6 20.6 %all-to-all-done.3 = bf16[32,24,896]{2,1,0:T(8,128)(2,1)S(1)} async-done(((bf16[32,24,896]{2,1,0:T(8,128)(2,1)}), bf16[32,24,896]{2,1,0:T(8,128)(2,1)S(1)}, u32[]{:S(2)}, u32[]{:S(2)}) %all-to-all-start.3) | async-done | bytes 1376288 | tf_op jit(solution)/shard_map/all_to_all | solution.py:30
  85.2 0.7 maximum_maximum_fusion
  86.0 7.4 %all-to-all-start.4 = ((bf16[16,72,128]{2,1,0:T(8,128)(2,1)}), bf16[16,72,128]{2,1,0:T(8,128)(2,1)S(1)}, u32[]{:S(2)}, u32[]{:S(2)}) async-start(bf16[16,72,128]{2,1,0:T(8,128)(2,1)} %maximum_maximum_fusion), calls=%async_computation.4 | async-start | bytes 589824 | tf_op jit(solution)/shard_map/all_to_all | solution.py:33
  93.4 13.5 %all-to-all-done.4 = bf16[16,72,128]{2,1,0:T(8,128)(2,1)S(1)} async-done(((bf16[16,72,128]{2,1,0:T(8,128)(2,1)}), bf16[16,72,128]{2,1,0:T(8,128)(2,1)S(1)}, u32[]{:S(2)}, u32[]{:S(2)}) %all-to-all-start.4) | async-done | bytes 294944 | tf_op jit(solution)/shard_map/all_to_all | solution.py:33
  107.1 0.8 broadcast_in_dim.16
  107.9 10.6 %all-to-all-start.5 = ((bf16[32,48,128]{2,1,0:T(8,128)(2,1)}), bf16[32,48,128]{2,1,0:T(8,128)(2,1)S(1)}, u32[]{:S(2)}, u32[]{:S(2)}) async-start(bf16[32,48,128]{2,1,0:T(8,128)(2,1)} %bitcast.18), calls=%async_computation.5 | async-start | bytes 786432 | tf_op jit(solution)/shard_map/all_to_all | solution.py:30
  118.5 1.0 fusion.24
  119.5 8.6 %all-to-all-done.5 = bf16[32,48,128]{2,1,0:T(8,128)(2,1)S(1)} async-done(((bf16[32,48,128]{2,1,0:T(8,128)(2,1)}), bf16[32,48,128]{2,1,0:T(8,128)(2,1)S(1)}, u32[]{:S(2)}, u32[]{:S(2)}) %all-to-all-start.5) | async-done | bytes 393248 | tf_op jit(solution)/shard_map/all_to_all | solution.py:30
  128.2 0.7 fusion.27
  129.1 0.2 fusion.5
  129.3 17.4 %all_to_all.61 = bf16[16,24,128]{2,1,0:T(8,128)(2,1)S(1)} all-to-all(bf16[16,24,128]{2,1,0:T(8,128)(2,1)S(1)} %bitcast.104), channel_id=1, replica_groups={{0,32,64,96,128,160,192,224,256,288,320,352,384,416,448,480},{16,48,80,..., dimensions={0} | all-to-all | bytes 196608 | tf_op jit(solution)/shard_map/all_to_all | solution.py:33
  146.9 14.5 %all_to_all.62 = bf16[32,24,128]{2,1,0:T(8,128)(2,1)S(1)} all-to-all(bf16[32,24,128]{2,1,0:T(8,128)(2,1)S(1)} %broadcast_in_dim.17), channel_id=1, replica_groups={{0,1,2,3,4,5,6,7,8,9,10,11,12,13,14,15,16,17,18,19,20,21,22,23,24,25,26..., dimensions={0} | all-to-all | bytes 393216 | tf_op jit(solution)/shard_map/all_to_all | solution.py:30
  161.7 0.2 fusion.6
  161.9 15.8 %all_to_all.63 = bf16[16,48,128]{2,1,0:T(8,128)(2,1)S(1)} all-to-all(bf16[16,48,128]{2,1,0:T(8,128)(2,1)S(1)} %pad_maximum_fusion.4), channel_id=1, replica_groups={{0,32,64,96,128,160,192,224,256,288,320,352,384,416,448,480},{16,48,80,..., dimensions={0} | all-to-all | bytes 393216 | tf_op jit(solution)/shard_map/all_to_all | solution.py:33
  178.0 0.8 pad_maximum_fusion.1
  178.7 8.4 %all-to-all-start.9 = ((bf16[32,48,128]{2,1,0:T(8,128)(2,1)}), bf16[32,48,128]{2,1,0:T(8,128)(2,1)S(1)}, u32[]{:S(2)}, u32[]{:S(2)}) async-start(bf16[32,48,128]{2,1,0:T(8,128)(2,1)} %pad_maximum_fusion.1), calls=%async_computation.9 | async-start | bytes 786432 | tf_op jit(solution)/shard_map/all_to_all | solution.py:30
  187.2 0.3 fusion.8
  187.6 9.2 %all-to-all-done.9 = bf16[32,48,128]{2,1,0:T(8,128)(2,1)S(1)} async-done(((bf16[32,48,128]{2,1,0:T(8,128)(2,1)}), bf16[32,48,128]{2,1,0:T(8,128)(2,1)S(1)}, u32[]{:S(2)}, u32[]{:S(2)}) %all-to-all-start.9) | async-done | bytes 393248 | tf_op jit(solution)/shard_map/all_to_all | solution.py:30
  196.9 1.5 fusion.2
  198.6 3.1 %collective-permute-start = (bf16[8,40,128]{2,1,0:T(8,128)(2,1)S(1)}, bf16[8,40,128]{2,1,0:T(8,128)(2,1)S(1)}, u32[]{:S(2)}, u32[]{:S(2)}) collective-permute-start(bf16[8,40,128]{2,1,0:T(8,128)(2,1)S(1)} %fusion.17), channel_id=1, source_target_pairs={{0,16},{16,0},{32,48},{48,32},{64,80},{80,64},{96,112},{112,96},{1... | collective-permute-start | bytes 245768 | tf_op jit(solution)/shard_map/ppermute | solution.py:120
  201.8 0.9 collective-permute-done
  202.7 0.7 pad_maximum_fusion.9
  203.4 4.5 %all-to-all-start.10 = ((bf16[8,80,128]{2,1,0:T(8,128)(2,1)}), bf16[8,80,128]{2,1,0:T(8,128)(2,1)S(1)}, u32[]{:S(2)}, u32[]{:S(2)}) async-start(bf16[8,80,128]{2,1,0:T(8,128)(2,1)} %pad_maximum_fusion.9), calls=%async_computation.10 | async-start | bytes 327680 | tf_op jit(solution)/shard_map/all_to_all | solution.py:33
  207.9 0.7 compare_convert_fusion
  208.6 10.1 %all-to-all-done.10 = bf16[8,80,128]{2,1,0:T(8,128)(2,1)S(1)} async-done(((bf16[8,80,128]{2,1,0:T(8,128)(2,1)}), bf16[8,80,128]{2,1,0:T(8,128)(2,1)S(1)}, u32[]{:S(2)}, u32[]{:S(2)}) %all-to-all-start.10) | async-done | bytes 163872 | tf_op jit(solution)/shard_map/all_to_all | solution.py:33
  218.8 17.4 %all_to_all.64 = bf16[8,2,40,128]{3,2,1,0:T(8,128)(2,1)S(1)} all-to-all(bf16[8,2,40,128]{3,2,1,0:T(8,128)(2,1)S(1)} %broadcast_in_dim.20), channel_id=1, replica_groups={{0,32,64,96,128,160,192,224},{16,48,80,112,144,176,208,240},{256,288,32..., dimensions={0} | all-to-all | bytes 327680 | tf_op jit(solution)/shard_map/all_to_all | solution.py:33
  236.2 5.1 %collective-permute-start.1 = (bf16[2,320,128]{2,1,0:T(8,128)(2,1)S(1)}, bf16[2,320,128]{2,1,0:T(8,128)(2,1)S(1)}, u32[]{:S(2)}, u32[]{:S(2)}) collective-permute-start(bf16[2,320,128]{2,1,0:T(8,128)(2,1)S(1)} %bitcast.100), channel_id=1, source_target_pairs={{0,16},{16,0},{32,48},{48,32},{64,80},{80,64},{96,112},{112,96},{1... | collective-permute-start | bytes 491528 | tf_op jit(solution)/shard_map/ppermute | solution.py:129
  241.4 1.0 collective-permute-done.1
  242.4 0.8 fusion.15
  (65 shorter events, 2.1 us)
Async XLA Ops:
  0.0 58.3 %copy-start = (bf16[1,640,640]{2,1,0:T(8,128)(2,1)S(1)}, bf16[1,640,640]{2,1,0:T(8,128)(2,1)}, u32[]{:S(2)}) copy-start(bf16[1,640,640]{2,1,0:T(8,128)(2,1)} %param.9) | copy-start | bytes 2457604
  0.0 30.6 %copy-start.5 = (s32[2,32]{1,0:T(2,128)S(1)}, s32[2,32]{1,0:T(2,128)}, u32[]{:S(2)}) copy-start(s32[2,32]{1,0:T(2,128)} %param.7) | copy-start | bytes 772
  0.0 31.7 %slice-start.2 = ((s32[2,32]{1,0:T(2,128)}), s32[1,32]{1,0:T(1,128)S(1)}, s32[]{:S(2)}) async-start(s32[2,32]{1,0:T(2,128)} %param.7), calls=%async_computation.14 | async-start | bytes 1024 | tf_op jit(solution)/shard_map/slice | solution.py:74
  1.1 46.9 %slice-start = ((bf16[1,640,960]{1,2,0:T(8,128)(2,1)}), bf16[1,640,320]{1,2,0:T(8,128)(2,1)S(1)}, s32[]{:S(2)}) async-start(bf16[1,640,960]{1,2,0:T(8,128)(2,1)} %param.8), calls=%async_computation.12 | async-start | bytes 819200 | tf_op jit(solution)/shard_map/slice | solution.py:84
  19.6 21.1 %all-to-all-start.1 = ((bf16[8,48,128]{2,1,0:T(8,128)(2,1)}), bf16[8,48,128]{2,1,0:T(8,128)(2,1)S(1)}, u32[]{:S(2)}, u32[]{:S(2)}) async-start(bf16[8,48,128]{2,1,0:T(8,128)(2,1)} %bitcast.3), calls=%async_computation.1 | async-start | bytes 196608 | tf_op jit(solution)/shard_map/all_to_all | solution.py:33
  41.5 6.8 %slice-start.1 = ((bf16[1,640,960]{1,2,0:T(8,128)(2,1)}), bf16[1,640,320]{1,2,0:T(8,128)(2,1)S(1)}, s32[]{:S(2)}) async-start(bf16[1,640,960]{1,2,0:T(8,128)(2,1)} %param.10), calls=%async_computation.13 | async-start | bytes 819200 | tf_op jit(solution)/shard_map/slice | solution.py:84
  41.5 14.6 %all-to-all-start.2 = ((bf16[32,24,128]{2,1,0:T(8,128)(2,1)}), bf16[32,24,128]{2,1,0:T(8,128)(2,1)}, u32[]{:S(2)}, u32[]{:S(2)}) async-start(bf16[32,24,128]{2,1,0:T(8,128)(2,1)} %bitcast.5), calls=%async_computation.2 | async-start | bytes 393216 | tf_op jit(solution)/shard_map/all_to_all | solution.py:30
  48.3 9.6 %copy-start.1 = (bf16[1,640,960]{1,2,0:T(8,128)(2,1)S(1)}, bf16[1,640,960]{1,2,0:T(8,128)(2,1)}, u32[]{:S(2)}) copy-start(bf16[1,640,960]{1,2,0:T(8,128)(2,1)} %param.8) | copy-start | bytes 3686404
  60.3 24.9 %all-to-all-start.3 = ((bf16[32,24,896]{2,1,0:T(8,128)(2,1)}), bf16[32,24,896]{2,1,0:T(8,128)(2,1)S(1)}, u32[]{:S(2)}, u32[]{:S(2)}) async-start(bf16[32,24,896]{2,1,0:T(8,128)(2,1)} %fusion.1), calls=%async_computation.3 | async-start | bytes 2752512 | tf_op jit(solution)/shard_map/all_to_all | solution.py:30
  86.0 20.9 %all-to-all-start.4 = ((bf16[16,72,128]{2,1,0:T(8,128)(2,1)}), bf16[16,72,128]{2,1,0:T(8,128)(2,1)S(1)}, u32[]{:S(2)}, u32[]{:S(2)}) async-start(bf16[16,72,128]{2,1,0:T(8,128)(2,1)} %maximum_maximum_fusion), calls=%async_computation.4 | async-start | bytes 589824 | tf_op jit(solution)/shard_map/all_to_all | solution.py:33
  107.9 20.2 %all-to-all-start.5 = ((bf16[32,48,128]{2,1,0:T(8,128)(2,1)}), bf16[32,48,128]{2,1,0:T(8,128)(2,1)S(1)}, u32[]{:S(2)}, u32[]{:S(2)}) async-start(bf16[32,48,128]{2,1,0:T(8,128)(2,1)} %bitcast.18), calls=%async_computation.5 | async-start | bytes 786432 | tf_op jit(solution)/shard_map/all_to_all | solution.py:30
  119.5 9.6 %copy-start.3 = (bf16[16,24,320]{2,1,0:T(8,128)(2,1)S(1)}, bf16[16,24,320]{2,1,0:T(8,128)(2,1)}, u32[]{:S(2)}) copy-start(bf16[16,24,320]{2,1,0:T(8,128)(2,1)} %get-tuple-element.6) | copy-start | bytes 737284
  161.9 25.3 %copy-start.4 = (bf16[16,24,128]{2,1,0:T(8,128)(2,1)S(1)}, bf16[16,24,128]{2,1,0:T(8,128)(2,1)}, u32[]{:S(2)}) copy-start(bf16[16,24,128]{2,1,0:T(8,128)(2,1)} %get-tuple-element.13) | copy-start | bytes 294916
  177.8 9.5 %copy-start.2 = (bf16[1,640,960]{1,2,0:T(8,128)(2,1)S(1)}, bf16[1,640,960]{1,2,0:T(8,128)(2,1)}, u32[]{:S(2)}) copy-start(bf16[1,640,960]{1,2,0:T(8,128)(2,1)} %param.10) | copy-start | bytes 3686404
  178.7 18.1 %all-to-all-start.9 = ((bf16[32,48,128]{2,1,0:T(8,128)(2,1)}), bf16[32,48,128]{2,1,0:T(8,128)(2,1)S(1)}, u32[]{:S(2)}, u32[]{:S(2)}) async-start(bf16[32,48,128]{2,1,0:T(8,128)(2,1)} %pad_maximum_fusion.1), calls=%async_computation.9 | async-start | bytes 786432 | tf_op jit(solution)/shard_map/all_to_all | solution.py:30
  198.6 4.0 %collective-permute-start = (bf16[8,40,128]{2,1,0:T(8,128)(2,1)S(1)}, bf16[8,40,128]{2,1,0:T(8,128)(2,1)S(1)}, u32[]{:S(2)}, u32[]{:S(2)}) collective-permute-start(bf16[8,40,128]{2,1,0:T(8,128)(2,1)S(1)} %fusion.17), channel_id=1, source_target_pairs={{0,16},{16,0},{32,48},{48,32},{64,80},{80,64},{96,112},{112,96},{1... | collective-permute-start | bytes 245768 | tf_op jit(solution)/shard_map/ppermute | solution.py:120
  203.4 15.3 %all-to-all-start.10 = ((bf16[8,80,128]{2,1,0:T(8,128)(2,1)}), bf16[8,80,128]{2,1,0:T(8,128)(2,1)S(1)}, u32[]{:S(2)}, u32[]{:S(2)}) async-start(bf16[8,80,128]{2,1,0:T(8,128)(2,1)} %pad_maximum_fusion.9), calls=%async_computation.10 | async-start | bytes 327680 | tf_op jit(solution)/shard_map/all_to_all | solution.py:33
  236.2 6.1 %collective-permute-start.1 = (bf16[2,320,128]{2,1,0:T(8,128)(2,1)S(1)}, bf16[2,320,128]{2,1,0:T(8,128)(2,1)S(1)}, u32[]{:S(2)}, u32[]{:S(2)}) collective-permute-start(bf16[2,320,128]{2,1,0:T(8,128)(2,1)S(1)} %bitcast.100), channel_id=1, source_target_pairs={{0,16},{16,0},{32,48},{48,32},{64,80},{80,64},{96,112},{112,96},{1... | collective-permute-start | bytes 491528 | tf_op jit(solution)/shard_map/ppermute | solution.py:129

commit v4 on v3

--- a/solution.py
+++ b/solution.py
@@ -56,12 +56,12 @@
         return (rows < count * BLK).astype(f32)[:, :, None]
 
     def times(mat, vec):
-        width = mat.shape[-1]
-        m = mat.reshape(2, n_front * WIN, width)
-        v = vec.reshape(2, width, n_rhs)
+        height = n_front * WIN
+        m = mat.reshape(2 * height, mat.shape[-1])
+        v = vec.reshape(2, vec.shape[0] // 2, n_rhs)
         return (
-            jnp.dot(m[0], v[0], preferred_element_type=f32)
-            + jnp.dot(m[1], v[1], preferred_element_type=f32)
+            jnp.dot(m[:height, n_rhs:], v[0], preferred_element_type=f32)
+            + jnp.dot(m[height:, n_rhs:], v[1], preferred_element_type=f32)
         ).reshape(n_front, WIN, n_rhs)
 
     def fold(v):
@@ -71,21 +71,26 @@
         return jnp.broadcast_to(v[:, None], (2, n_front) + v.shape[1:]).reshape((2 * n_front,) + v.shape[1:])
 
     swap = [(k, k ^ 1) for k in range(n_leaf)]
+    rows = front_id * sep_dev + (core * half + z8) * PIECE + jnp.arange(PIECE)
     mask0 = piece_mask(2 * z8, 2, live[0][node])
-    mask1 = piece_mask(z, 1, live[1][0])
+    mask1 = piece_mask(z, 1, live[1][0])[0]
+    mask2 = piece_mask(2 * z8, 2, live[1][0])
+    mask3 = (rows < live[0][node] * BLK).astype(f32)[:, None]
 
     got = a2a_plane(cut(forcing[0]))
+    linv1, uinv1 = cut(lower_inv[0, :, w0:]), cut(upper_inv[0, :, w0:])
+    got, linv1, uinv1, mask0, mask1, mask2, mask3 = lax.optimization_barrier(
+        (got, linv1, uinv1, mask0, mask1, mask2, mask3)
+    )
     pair = fold(got).astype(bf).reshape(half, 2 * WIN, n_rhs)
     r0 = total(a2a_leaf(pair, z_half)).reshape(2, WIN, n_rhs)
-    rm0 = join(a2a_plane(by_core((mask0 * r0).astype(bf))))
+    got = a2a_plane(jnp.concatenate([by_core((mask0 * r0).astype(bf)), linv1], 2))
+    rm0 = join(got[:, :, :n_rhs])
+    linv1 = got
 
     c_part = jnp.dot(lower_upd[0], rm0, preferred_element_type=f32).astype(bf)
     y_part = jnp.dot(lower_inv[0, :, :w0], rm0, preferred_element_type=f32).astype(bf)
-    root = cut(jnp.concatenate([lower_inv[0, :, w0:], upper_inv[0, :, w0:]], 1))
-    got = a2a_plane(jnp.concatenate([cut(jnp.concatenate([c_part, y_part], 1)), root], 2))
-    parts = fold(got[:, :, : 2 * n_rhs]).astype(bf)
-    linv1 = got[:, :, 2 * n_rhs : 2 * n_rhs + w1]
-    uinv1 = got[:, :, 2 * n_rhs + w1 :]
+    parts = fold(a2a_plane(cut(jnp.concatenate([c_part, y_part], 1)))).astype(bf)
 
     c_part = parts[:, :, :n_rhs]
     y_part = parts[:, :, n_rhs:].reshape(half, 2 * WIN, n_rhs)
@@ -93,21 +98,23 @@
     first = node == 0
     y_part = jnp.concatenate([jnp.where(first, y_part, zero), jnp.where(first, zero, y_part)], 0)
     got = total(a2a_leaf(jnp.concatenate([c_part, y_part], 1), z_all))
-    r1 = (mask1[0] * -got[:WIN]).astype(bf)
+    r1 = (mask1 * -got[:WIN]).astype(bf)
     y0 = (mask0 * got[WIN:].reshape(2, WIN, n_rhs)).astype(bf)
     got = a2a_plane(by_core(jnp.concatenate([jnp.stack([r1, r1]), y0], 1)))
     r1 = join(got[:, :WIN])
     y0 = join(got[:, WIN:])
 
     y1 = total(a2a_leaf(times(linv1, r1).astype(bf), z_all))
-    y1 = (mask1[0] * y1).astype(bf)
-    y1 = join(a2a_plane(spread(y1, 2 * n_front)))
+    y1 = (mask1 * y1).astype(bf)
+    got = a2a_plane(jnp.concatenate([spread(y1, 2 * n_front), uinv1], 2))
+    y1 = join(got[:, :, :n_rhs])
 
-    x_part = times(uinv1, y1).astype(bf).reshape(half, 2 * WIN, n_rhs)
+    x_part = times(got, y1).astype(bf).reshape(half, 2 * WIN, n_rhs)
     x1 = total(a2a_leaf(jnp.concatenate([x_part, x_part], 0), z_all)).reshape(2, WIN, n_rhs)
-    x1 = (piece_mask(2 * z8, 2, live[1][0]) * x1).astype(bf)
+    x1 = (mask2 * x1).astype(bf)
     own = jnp.broadcast_to(x1[None, None], (2, n_front // 2) + x1.shape).reshape(2 * n_front, WIN, n_rhs)
     got = a2a_plane(jnp.concatenate([by_core(x1), own], 1))
+    got, y0 = lax.optimization_barrier((got, y0))
     x1c = join(got[:, :WIN])
     own = join(got[:, WIN:])
 
@@ -121,8 +128,7 @@
     own = lax.dynamic_index_in_dim(own.reshape(2, half, PIECE, n_rhs), core, 0, False)
     got = a2a_leaf(jnp.concatenate([term, own], 1), z_half)
 
-    rows = front_id * sep_dev + (core * half + z8) * PIECE + jnp.arange(PIECE)
-    x0 = total(got[:, :PIECE]) * (rows < live[0][node] * BLK).astype(f32)[:, None]
+    x0 = total(got[:, :PIECE]) * mask3
     x1 = lax.dynamic_index_in_dim(got[:, PIECE:], front_id // 2, 0, False)
     both = a2a_leaf(spread(jnp.stack([x0.astype(bf), x1]), half), z_half)
     both = jnp.swapaxes(both, 0, 1).reshape(2, half * PIECE, n_rhs)

time: 244 us -> 241 us (0.988)
  blocking collectives: 83 us -> 153 us
  waiting for transfers between devices: 78.8 us -> 33.6 us
  starting transfers between devices: 61.1 us -> 37 us
  local copies, waits for them, and re-layouts: 7.64 us -> 5.1 us
    all_to_all x3 -> x5, blocking collectives: 50.6 us -> 91 us  [a2a_leaf(): return lax.all_to_all(v, 'leaf', 0, 0, axis_index_groups=groups)]
    all_to_all x2 -> x3, blocking collectives: 32.3 us -> 61.8 us  [a2a_plane(): return lax.all_to_all(v, ('leaf', 'front'), 0, 0, axis_index_groups=plane)]
    all_to_all x4 -> x3, waiting for transfers between devices: 45.8 us -> 21 us  [a2a_plane(): return lax.all_to_all(v, ('leaf', 'front'), 0, 0, axis_index_groups=plane)]
    all_to_all x3 -> x1, waiting for transfers between devices: 31 us -> 10.8 us  [a2a_leaf(): return lax.all_to_all(v, 'leaf', 0, 0, axis_index_groups=groups)]
    all_to_all x3 -> x1, starting transfers between devices: 23 us -> 4.67 us  [a2a_leaf(): return lax.all_to_all(v, 'leaf', 0, 0, axis_index_groups=groups)]
    all_to_all x4 -> x3, starting transfers between devices: 29.8 us -> 24 us  [a2a_plane(): return lax.all_to_all(v, ('leaf', 'front'), 0, 0, axis_index_groups=plane)]
    concatenate x1 -> x3, other arithmetic: 0.02 us -> 2.65 us  [cut(): return jnp.concatenate([v[:, :WIN], v[:, LO:]], 0)]
  transfers between devices with their start and end apart: 9 -> 6, of which waited for: 9 -> 6; matrix products, arithmetic and copies ran while one was open for 2% -> 2% of each run, Pallas kernels for 0% -> 0%
where the time goes in v4:
time: 241 us; the launch traced here: 240 us
  blocking collectives  153 us (63%)
  starting transfers between devices  37 us (15%)
  waiting for transfers between devices  33.6 us (14%)
  other arithmetic  7.82 us (3%)
  local copies, waits for them, and re-layouts  5.1 us (2%)
  matrix products  2.41 us (1%)
    all_to_all x5, blocking collectives, a2a_leaf(): return lax.all_to_all(v, 'leaf', 0, 0, axis_index_groups=groups)  91 us
    all_to_all x3, blocking collectives, a2a_plane(): return lax.all_to_all(v, ('leaf', 'front'), 0, 0, axis_index_groups=plane)  61.8 us
    all_to_all x3, starting transfers between devices, a2a_plane(): return lax.all_to_all(v, ('leaf', 'front'), 0, 0, axis_index_groups=plane)  24 us
    all_to_all x3, waiting for transfers between devices, a2a_plane(): return lax.all_to_all(v, ('leaf', 'front'), 0, 0, axis_index_groups=plane)  21 us
    all_to_all x1, waiting for transfers between devices, a2a_leaf(): return lax.all_to_all(v, 'leaf', 0, 0, axis_index_groups=groups)  10.8 us
    ppermute x1, starting transfers between devices, body(): other = lax.ppermute(both, 'leaf', swap)  5.11 us
  transfers between devices with their start and end apart: 6, of which 6 were waited for; matrix products, arithmetic and copies ran while one was open for 2% of the time, Pallas kernels for 0%

profile of v4, /device:TPU:1, one launch (start us, length us, event | category | flops | bytes accessed | tf_op | source)
XLA Modules:
  0.0 239.9 jit_solution(3246649360916448005)
XLA Ops:
  0.0 1.1 fusion.35
  1.1 0.7 pad_maximum_fusion.7
  1.8 10.5 %all-to-all-start = ((bf16[32,24,128]{2,1,0:T(8,128)(2,1)}), bf16[32,24,128]{2,1,0:T(8,128)(2,1)S(1)}, u32[]{:S(2)}, u32[]{:S(2)}) async-start(bf16[32,24,128]{2,1,0:T(8,128)(2,1)} %pad_maximum_fusion.7), calls=%async_computation | async-start | bytes 393216 | tf_op jit(solution)/shard_map/all_to_all | solution.py:30
  12.3 0.6 slice.169
  12.9 0.3 copy.25
  13.2 0.7 slice-done.1
  13.9 0.3 copy.24
  14.2 0.8 fusion.28
  14.9 0.6 fusion.36
  15.5 0.6 compare_convert_fusion
  16.8 1.2 pad_maximum_fusion.2
  17.9 0.6 compare_convert_fusion.1
  18.6 1.8 all-to-all-done
  20.4 20.2 %all_to_all.60 = bf16[8,48,128]{2,1,0:T(8,128)(2,1)S(1)} all-to-all(bf16[8,48,128]{2,1,0:T(8,128)(2,1)S(1)} %bitcast.102), channel_id=1, replica_groups={{0,32,64,96,128,160,192,224},{16,48,80,112,144,176,208,240},{256,288,32..., dimensions={0} | all-to-all | bytes 196608 | tf_op jit(solution)/shard_map/all_to_all | solution.py:33
  40.7 0.1 pad_maximum_fusion
  40.8 21.1 %all_to_all.61 = bf16[32,24,448]{2,1,0:T(8,128)(2,1)S(1)} all-to-all(bf16[32,24,448]{2,1,0:T(8,128)(2,1)S(1)} %pad_maximum_fusion), channel_id=1, replica_groups={{0,1,2,3,4,5,6,7,8,9,10,11,12,13,14,15,16,17,18,19,20,21,22,23,24,25,26..., dimensions={0} | all-to-all | bytes 1376256 | tf_op jit(solution)/shard_map/all_to_all | solution.py:30
  62.0 0.3 fusion.2
  62.3 0.4 fusion.1
  62.8 0.2 copy.20
  63.0 0.8 pad_maximum_fusion.4
  63.8 4.8 %all-to-all-start.3 = ((bf16[32,24,256]{2,1,0:T(8,128)(2,1)}), bf16[32,24,256]{2,1,0:T(8,128)(2,1)S(1)}, u32[]{:S(2)}, u32[]{:S(2)}) async-start(bf16[32,24,256]{2,1,0:T(8,128)(2,1)} %pad_maximum_fusion.4), calls=%async_computation.3 | async-start | bytes 786432 | tf_op jit(solution)/shard_map/all_to_all | solution.py:30
  68.6 9.6 %all-to-all-done.3 = bf16[32,24,256]{2,1,0:T(8,128)(2,1)S(1)} async-done(((bf16[32,24,256]{2,1,0:T(8,128)(2,1)}), bf16[32,24,256]{2,1,0:T(8,128)(2,1)S(1)}, u32[]{:S(2)}, u32[]{:S(2)}) %all-to-all-start.3) | async-done | bytes 393248 | tf_op jit(solution)/shard_map/all_to_all | solution.py:30
  78.3 20.6 %all_to_all.62 = bf16[16,72,128]{2,1,0:T(8,128)(2,1)S(1)} all-to-all(bf16[16,72,128]{2,1,0:T(8,128)(2,1)S(1)} %maximum_maximum_fusion), channel_id=1, replica_groups={{0,32,64,96,128,160,192,224,256,288,320,352,384,416,448,480},{16,48,80,..., dimensions={0} | all-to-all | bytes 589824 | tf_op jit(solution)/shard_map/all_to_all | solution.py:33
  99.2 20.5 %all_to_all.63 = bf16[32,48,128]{2,1,0:T(8,128)(2,1)S(1)} all-to-all(bf16[32,48,128]{2,1,0:T(8,128)(2,1)S(1)} %bitcast.88), channel_id=1, replica_groups={{0,1,2,3,4,5,6,7,8,9,10,11,12,13,14,15,16,17,18,19,20,21,22,23,24,25,26..., dimensions={0} | all-to-all | bytes 786432 | tf_op jit(solution)/shard_map/all_to_all | solution.py:30
  119.8 0.2 fusion.17
  120.0 0.2 fusion.3
  120.3 17.4 %all_to_all.64 = bf16[16,24,128]{2,1,0:T(8,128)(2,1)S(1)} all-to-all(bf16[16,24,128]{2,1,0:T(8,128)(2,1)S(1)} %bitcast.103), channel_id=1, replica_groups={{0,32,64,96,128,160,192,224,256,288,320,352,384,416,448,480},{16,48,80,..., dimensions={0} | all-to-all | bytes 196608 | tf_op jit(solution)/shard_map/all_to_all | solution.py:33
  137.7 0.1 pad_maximum_fusion.1
  137.9 20.3 %all_to_all.65 = bf16[32,24,448]{2,1,0:T(8,128)(2,1)S(1)} all-to-all(bf16[32,24,448]{2,1,0:T(8,128)(2,1)S(1)} %pad_maximum_fusion.1), channel_id=1, replica_groups={{0,1,2,3,4,5,6,7,8,9,10,11,12,13,14,15,16,17,18,19,20,21,22,23,24,25,26..., dimensions={0} | all-to-all | bytes 1376256 | tf_op jit(solution)/shard_map/all_to_all | solution.py:30
  158.2 0.2 fusion.14
  158.4 0.2 fusion.4
  158.7 15.5 %all_to_all.66 = bf16[16,48,128]{2,1,0:T(8,128)(2,1)S(1)} all-to-all(bf16[16,48,128]{2,1,0:T(8,128)(2,1)S(1)} %pad_maximum_fusion.8), channel_id=1, replica_groups={{0,32,64,96,128,160,192,224,256,288,320,352,384,416,448,480},{16,48,80,..., dimensions={0} | all-to-all | bytes 393216 | tf_op jit(solution)/shard_map/all_to_all | solution.py:33
  174.4 0.8 pad_maximum_fusion.5
  175.2 8.7 %all-to-all-start.9 = ((bf16[32,48,128]{2,1,0:T(8,128)(2,1)}), bf16[32,48,128]{2,1,0:T(8,128)(2,1)S(1)}, u32[]{:S(2)}, u32[]{:S(2)}) async-start(bf16[32,48,128]{2,1,0:T(8,128)(2,1)} %pad_maximum_fusion.5), calls=%async_computation.9 | async-start | bytes 786432 | tf_op jit(solution)/shard_map/all_to_all | solution.py:30
  184.0 9.6 %all-to-all-done.9 = bf16[32,48,128]{2,1,0:T(8,128)(2,1)S(1)} async-done(((bf16[32,48,128]{2,1,0:T(8,128)(2,1)}), bf16[32,48,128]{2,1,0:T(8,128)(2,1)S(1)}, u32[]{:S(2)}, u32[]{:S(2)}) %all-to-all-start.9) | async-done | bytes 393248 | tf_op jit(solution)/shard_map/all_to_all | solution.py:30
  193.6 0.6 fusion.30
  194.2 0.3 fusion.6
  194.6 0.4 fusion
  195.0 0.2 copy.21
  195.2 3.1 %collective-permute-start = (bf16[8,40,128]{2,1,0:T(8,128)(2,1)S(1)}, bf16[8,40,128]{2,1,0:T(8,128)(2,1)S(1)}, u32[]{:S(2)}, u32[]{:S(2)}) collective-permute-start(bf16[8,40,128]{2,1,0:T(8,128)(2,1)S(1)} %fusion.20), channel_id=1, source_target_pairs={{0,16},{16,0},{32,48},{48,32},{64,80},{80,64},{96,112},{112,96},{1... | collective-permute-start | bytes 245768 | tf_op jit(solution)/shard_map/ppermute | solution.py:127
  198.4 0.8 collective-permute-done
  199.3 0.7 pad_maximum_fusion.13
  200.0 4.7 %all-to-all-start.10 = ((bf16[8,80,128]{2,1,0:T(8,128)(2,1)}), bf16[8,80,128]{2,1,0:T(8,128)(2,1)S(1)}, u32[]{:S(2)}, u32[]{:S(2)}) async-start(bf16[8,80,128]{2,1,0:T(8,128)(2,1)} %pad_maximum_fusion.13), calls=%async_computation.10 | async-start | bytes 327680 | tf_op jit(solution)/shard_map/all_to_all | solution.py:33
  204.6 10.8 %all-to-all-done.10 = bf16[8,80,128]{2,1,0:T(8,128)(2,1)S(1)} async-done(((bf16[8,80,128]{2,1,0:T(8,128)(2,1)}), bf16[8,80,128]{2,1,0:T(8,128)(2,1)S(1)}, u32[]{:S(2)}, u32[]{:S(2)}) %all-to-all-start.10) | async-done | bytes 163872 | tf_op jit(solution)/shard_map/all_to_all | solution.py:33
  215.5 17.4 %all_to_all.67 = bf16[8,2,40,128]{3,2,1,0:T(8,128)(2,1)S(1)} all-to-all(bf16[8,2,40,128]{3,2,1,0:T(8,128)(2,1)S(1)} %broadcast_in_dim.20), channel_id=1, replica_groups={{0,32,64,96,128,160,192,224},{16,48,80,112,144,176,208,240},{256,288,32..., dimensions={0} | all-to-all | bytes 327680 | tf_op jit(solution)/shard_map/all_to_all | solution.py:33
  232.9 5.1 %collective-permute-start.1 = (bf16[2,320,128]{2,1,0:T(8,128)(2,1)S(1)}, bf16[2,320,128]{2,1,0:T(8,128)(2,1)S(1)}, u32[]{:S(2)}, u32[]{:S(2)}) collective-permute-start(bf16[2,320,128]{2,1,0:T(8,128)(2,1)S(1)} %bitcast.98), channel_id=1, source_target_pairs={{0,16},{16,0},{32,48},{48,32},{64,80},{80,64},{96,112},{112,96},{1... | collective-permute-start | bytes 491528 | tf_op jit(solution)/shard_map/ppermute | solution.py:135
  238.1 1.0 collective-permute-done.1
  239.1 0.8 fusion.12
  (66 shorter events, 1.4 us)
Async XLA Ops:
  0.0 62.3 %copy-start = (bf16[1,640,640]{2,1,0:T(8,128)(2,1)S(1)}, bf16[1,640,640]{2,1,0:T(8,128)(2,1)}, u32[]{:S(2)}) copy-start(bf16[1,640,640]{2,1,0:T(8,128)(2,1)} %param.9) | copy-start | bytes 2457604
  0.0 12.3 %copy-start.5 = (s32[2,32]{1,0:T(2,128)S(1)}, s32[2,32]{1,0:T(2,128)}, u32[]{:S(2)}) copy-start(s32[2,32]{1,0:T(2,128)} %param.7) | copy-start | bytes 772
  0.0 12.9 %slice-start = ((bf16[1,640,960]{1,2,0:T(8,128)(2,1)}), bf16[1,640,320]{1,2,0:T(8,128)(2,1)S(1)}, s32[]{:S(2)}) async-start(bf16[1,640,960]{1,2,0:T(8,128)(2,1)} %param.10), calls=%async_computation.12 | async-start | bytes 819200 | tf_op jit(solution)/shard_map/slice | solution.py:81
  1.8 18.6 %all-to-all-start = ((bf16[32,24,128]{2,1,0:T(8,128)(2,1)}), bf16[32,24,128]{2,1,0:T(8,128)(2,1)S(1)}, u32[]{:S(2)}, u32[]{:S(2)}) async-start(bf16[32,24,128]{2,1,0:T(8,128)(2,1)} %pad_maximum_fusion.7), calls=%async_computation | async-start | bytes 393216 | tf_op jit(solution)/shard_map/all_to_all | solution.py:30
  12.9 1.0 slice-start.1
  13.9 1.0 slice-start.2
  40.8 21.1 %copy-start.2 = (bf16[1,640,960]{1,2,0:T(8,128)(2,1)S(1)}, bf16[1,640,960]{1,2,0:T(8,128)(2,1)}, u32[]{:S(2)}) copy-start(bf16[1,640,960]{1,2,0:T(8,128)(2,1)} %param.8) | copy-start | bytes 3686404
  63.8 14.4 %all-to-all-start.3 = ((bf16[32,24,256]{2,1,0:T(8,128)(2,1)}), bf16[32,24,256]{2,1,0:T(8,128)(2,1)S(1)}, u32[]{:S(2)}, u32[]{:S(2)}) async-start(bf16[32,24,256]{2,1,0:T(8,128)(2,1)} %pad_maximum_fusion.4), calls=%async_computation.3 | async-start | bytes 786432 | tf_op jit(solution)/shard_map/all_to_all | solution.py:30
  174.4 19.8 %copy-start.1 = (bf16[1,640,960]{1,2,0:T(8,128)(2,1)S(1)}, bf16[1,640,960]{1,2,0:T(8,128)(2,1)}, u32[]{:S(2)}) copy-start(bf16[1,640,960]{1,2,0:T(8,128)(2,1)} %param.10) | copy-start | bytes 3686404
  175.2 18.4 %all-to-all-start.9 = ((bf16[32,48,128]{2,1,0:T(8,128)(2,1)}), bf16[32,48,128]{2,1,0:T(8,128)(2,1)S(1)}, u32[]{:S(2)}, u32[]{:S(2)}) async-start(bf16[32,48,128]{2,1,0:T(8,128)(2,1)} %pad_maximum_fusion.5), calls=%async_computation.9 | async-start | bytes 786432 | tf_op jit(solution)/shard_map/all_to_all | solution.py:30
  184.0 10.6 %copy-start.3 = (bf16[1,640,640]{2,1,0:T(8,128)(2,1)S(1)}, bf16[1,640,640]{2,1,0:T(8,128)(2,1)}, u32[]{:S(2)}) copy-start(bf16[1,640,640]{2,1,0:T(8,128)(2,1)} %param.11) | copy-start | bytes 2457604
  194.6 3.8 %copy-start.4 = (bf16[16,16,128]{2,1,0:T(8,128)(2,1)S(1)}, bf16[16,16,128]{2,1,0:T(8,128)(2,1)}, u32[]{:S(2)}) copy-start(bf16[16,16,128]{2,1,0:T(8,128)(2,1)} %get-tuple-element.30) | copy-start | bytes 196612
  195.2 4.0 %collective-permute-start = (bf16[8,40,128]{2,1,0:T(8,128)(2,1)S(1)}, bf16[8,40,128]{2,1,0:T(8,128)(2,1)S(1)}, u32[]{:S(2)}, u32[]{:S(2)}) collective-permute-start(bf16[8,40,128]{2,1,0:T(8,128)(2,1)S(1)} %fusion.20), channel_id=1, source_target_pairs={{0,16},{16,0},{32,48},{48,32},{64,80},{80,64},{96,112},{112,96},{1... | collective-permute-start | bytes 245768 | tf_op jit(solution)/shard_map/ppermute | solution.py:127
  200.0 15.4 %all-to-all-start.10 = ((bf16[8,80,128]{2,1,0:T(8,128)(2,1)}), bf16[8,80,128]{2,1,0:T(8,128)(2,1)S(1)}, u32[]{:S(2)}, u32[]{:S(2)}) async-start(bf16[8,80,128]{2,1,0:T(8,128)(2,1)} %pad_maximum_fusion.13), calls=%async_computation.10 | async-start | bytes 327680 | tf_op jit(solution)/shard_map/all_to_all | solution.py:33
  232.9 6.1 %collective-permute-start.1 = (bf16[2,320,128]{2,1,0:T(8,128)(2,1)S(1)}, bf16[2,320,128]{2,1,0:T(8,128)(2,1)S(1)}, u32[]{:S(2)}, u32[]{:S(2)}) collective-permute-start(bf16[2,320,128]{2,1,0:T(8,128)(2,1)S(1)} %bitcast.98), channel_id=1, source_target_pairs={{0,16},{16,0},{32,48},{48,32},{64,80},{80,64},{96,112},{112,96},{1... | collective-permute-start | bytes 491528 | tf_op jit(solution)/shard_map/ppermute | solution.py:135

commit v5 on v4

--- a/solution.py
+++ b/solution.py
@@ -75,12 +75,13 @@
     mask0 = piece_mask(2 * z8, 2, live[0][node])
     mask1 = piece_mask(z, 1, live[1][0])[0]
     mask2 = piece_mask(2 * z8, 2, live[1][0])
+    mask4 = jnp.stack([piece_mask(z, 1, live[0][0]), piece_mask(z, 1, live[0][1])])[:, 0]
     mask3 = (rows < live[0][node] * BLK).astype(f32)[:, None]
 
     got = a2a_plane(cut(forcing[0]))
     linv1, uinv1 = cut(lower_inv[0, :, w0:]), cut(upper_inv[0, :, w0:])
-    got, linv1, uinv1, mask0, mask1, mask2, mask3 = lax.optimization_barrier(
-        (got, linv1, uinv1, mask0, mask1, mask2, mask3)
+    got, linv1, uinv1, mask0, mask1, mask2, mask3, mask4 = lax.optimization_barrier(
+        (got, linv1, uinv1, mask0, mask1, mask2, mask3, mask4)
     )
     pair = fold(got).astype(bf).reshape(half, 2 * WIN, n_rhs)
     r0 = total(a2a_leaf(pair, z_half)).reshape(2, WIN, n_rhs)
@@ -92,20 +93,16 @@
     y_part = jnp.dot(lower_inv[0, :, :w0], rm0, preferred_element_type=f32).astype(bf)
     parts = fold(a2a_plane(cut(jnp.concatenate([c_part, y_part], 1)))).astype(bf)
 
-    c_part = parts[:, :, :n_rhs]
-    y_part = parts[:, :, n_rhs:].reshape(half, 2 * WIN, n_rhs)
-    zero = jnp.zeros_like(y_part)
-    first = node == 0
-    y_part = jnp.concatenate([jnp.where(first, y_part, zero), jnp.where(first, zero, y_part)], 0)
-    got = total(a2a_leaf(jnp.concatenate([c_part, y_part], 1), z_all))
-    r1 = (mask1 * -got[:WIN]).astype(bf)
-    y0 = (mask0 * got[WIN:].reshape(2, WIN, n_rhs)).astype(bf)
-    got = a2a_plane(by_core(jnp.concatenate([jnp.stack([r1, r1]), y0], 1)))
-    r1 = join(got[:, :WIN])
-    y0 = join(got[:, WIN:])
+    got = a2a_leaf(jnp.concatenate([parts[:, :, :n_rhs], parts[:, :, n_rhs:]], 1), z_all)
+    r1 = (mask1 * -total(got[:, :WIN])).astype(bf)
+    y0 = got[:, WIN:].reshape(2, half, WIN, n_rhs)
+    y0 = (mask4 * jnp.sum(y0.astype(f32), 1)).astype(bf)
+    r1 = join(a2a_plane(spread(r1, 2 * n_front)))
 
-    y1 = total(a2a_leaf(times(linv1, r1).astype(bf), z_all))
-    y1 = (mask1 * y1).astype(bf)
+    y0 = jnp.broadcast_to(y0[:, None], (2, half, WIN, n_rhs)).reshape(n_z, WIN, n_rhs)
+    got = a2a_leaf(jnp.concatenate([times(linv1, r1).astype(bf), y0], 1), z_all)
+    y1 = (mask1 * total(got[:, :WIN])).astype(bf)
+    y0 = lax.dynamic_slice_in_dim(got[:, WIN:], 2 * z8, 2, 0)
     got = a2a_plane(jnp.concatenate([spread(y1, 2 * n_front), uinv1], 2))
     y1 = join(got[:, :, :n_rhs])
 
@@ -113,10 +110,10 @@
     x1 = total(a2a_leaf(jnp.concatenate([x_part, x_part], 0), z_all)).reshape(2, WIN, n_rhs)
     x1 = (mask2 * x1).astype(bf)
     own = jnp.broadcast_to(x1[None, None], (2, n_front // 2) + x1.shape).reshape(2 * n_front, WIN, n_rhs)
-    got = a2a_plane(jnp.concatenate([by_core(x1), own], 1))
-    got, y0 = lax.optimization_barrier((got, y0))
+    got = a2a_plane(jnp.concatenate([by_core(x1), own, by_core(y0)], 1))
     x1c = join(got[:, :WIN])
-    own = join(got[:, WIN:])
+    own = join(got[:, WIN : 2 * WIN])
+    y0 = join(got[:, 2 * WIN :])
 
     term = jnp.dot(upper_inv[0, :, :w0], y0, preferred_element_type=f32) - jnp.dot(
         upper_upd[0], x1c, preferred_element_type=f32

time: 241 us -> 243 us (level)
  blocking collectives: 153 us -> 132 us
  waiting for transfers between devices: 33.6 us -> 44.7 us
  starting transfers between devices: 37 us -> 46.2 us
    all_to_all x5 -> x4, blocking collectives: 91 us -> 74.5 us  [a2a_leaf(): return lax.all_to_all(v, 'leaf', 0, 0, axis_index_groups=groups)]
    all_to_all x1 -> x2, waiting for transfers between devices: 10.8 us -> 23.1 us  [a2a_leaf(): return lax.all_to_all(v, 'leaf', 0, 0, axis_index_groups=groups)]
    all_to_all x1 -> x2, starting transfers between devices: 4.67 us -> 9.88 us  [a2a_leaf(): return lax.all_to_all(v, 'leaf', 0, 0, axis_index_groups=groups)]
    all_to_all x3, starting transfers between devices: 24 us -> 28.1 us  [a2a_plane(): return lax.all_to_all(v, ('leaf', 'front'), 0, 0, axis_index_groups=plane)]
    all_to_all x3, blocking collectives: 61.8 us -> 57.8 us  [a2a_plane(): return lax.all_to_all(v, ('leaf', 'front'), 0, 0, axis_index_groups=plane)]
  transfers between devices with their start and end apart: 6 -> 7, of which waited for: 6 -> 7; matrix products, arithmetic and copies ran while one was open for 2% -> 2% of each run, Pallas kernels for 0% -> 0%
where the time goes in v5:
time: 243 us; the launch traced here: 242 us
  blocking collectives  132 us (54%)
  starting transfers between devices  46.2 us (19%)
  waiting for transfers between devices  44.7 us (18%)
  other arithmetic  8.2 us (3%)
  local copies, waits for them, and re-layouts  6 us (2%)
  between operations  2.52 us (1%)
    all_to_all x4, blocking collectives, a2a_leaf(): return lax.all_to_all(v, 'leaf', 0, 0, axis_index_groups=groups)  74.5 us
    all_to_all x3, blocking collectives, a2a_plane(): return lax.all_to_all(v, ('leaf', 'front'), 0, 0, axis_index_groups=plane)  57.8 us
    all_to_all x3, starting transfers between devices, a2a_plane(): return lax.all_to_all(v, ('leaf', 'front'), 0, 0, axis_index_groups=plane)  28.1 us
    all_to_all x2, waiting for transfers between devices, a2a_leaf(): return lax.all_to_all(v, 'leaf', 0, 0, axis_index_groups=groups)  23.1 us
    all_to_all x3, waiting for transfers between devices, a2a_plane(): return lax.all_to_all(v, ('leaf', 'front'), 0, 0, axis_index_groups=plane)  19.8 us
    all_to_all x2, starting transfers between devices, a2a_leaf(): return lax.all_to_all(v, 'leaf', 0, 0, axis_index_groups=groups)  9.88 us
    ppermute x1, starting transfers between devices, body(): other = lax.ppermute(both, 'leaf', swap)  5.11 us
  transfers between devices with their start and end apart: 7, of which 7 were waited for; matrix products, arithmetic and copies ran while one was open for 2% of the time, Pallas kernels for 0%

profile of v5, /device:TPU:1, one launch (start us, length us, event | category | flops | bytes accessed | tf_op | source)
XLA Modules:
  0.0 242.4 jit_solution(2028782735184132087)
XLA Ops:
  0.0 1.1 fusion.33
  1.1 0.7 pad_maximum_fusion.7
  1.8 10.5 %all-to-all-start = ((bf16[32,24,128]{2,1,0:T(8,128)(2,1)}), bf16[32,24,128]{2,1,0:T(8,128)(2,1)S(1)}, u32[]{:S(2)}, u32[]{:S(2)}) async-start(bf16[32,24,128]{2,1,0:T(8,128)(2,1)} %pad_maximum_fusion.7), calls=%async_computation | async-start | bytes 393216 | tf_op jit(solution)/shard_map/all_to_all | solution.py:30
  12.3 0.7 fusion.34
  14.9 0.3 copy.24
  15.3 0.7 slice-done.1
  15.9 0.3 copy.23
  16.2 0.8 fusion.30
  17.0 0.7 fusion.35
  17.6 0.7 compare_convert_fusion
  18.4 1.2 pad_maximum_fusion.2
  19.6 0.8 compare_convert_fusion.1
  20.4 20.2 %all_to_all.60 = bf16[8,48,128]{2,1,0:T(8,128)(2,1)S(1)} all-to-all(bf16[8,48,128]{2,1,0:T(8,128)(2,1)S(1)} %bitcast.105), channel_id=1, replica_groups={{0,32,64,96,128,160,192,224},{16,48,80,112,144,176,208,240},{256,288,32..., dimensions={0} | all-to-all | bytes 196608 | tf_op jit(solution)/shard_map/all_to_all | solution.py:33
  40.7 0.1 pad_maximum_fusion
  40.9 22.8 %all_to_all.61 = bf16[32,24,448]{2,1,0:T(8,128)(2,1)S(1)} all-to-all(bf16[32,24,448]{2,1,0:T(8,128)(2,1)S(1)} %pad_maximum_fusion), channel_id=1, replica_groups={{0,1,2,3,4,5,6,7,8,9,10,11,12,13,14,15,16,17,18,19,20,21,22,23,24,25,26..., dimensions={0} | all-to-all | bytes 1376256 | tf_op jit(solution)/shard_map/all_to_all | solution.py:30
  63.7 0.3 fusion.2
  64.1 0.4 fusion.1
  64.5 0.2 copy.19
  64.8 13.6 %all_to_all.62 = bf16[32,24,256]{2,1,0:T(8,128)(2,1)S(1)} all-to-all(bf16[32,24,256]{2,1,0:T(8,128)(2,1)S(1)} %pad_maximum_fusion.5), channel_id=1, replica_groups={{0,1,2,3,4,5,6,7,8,9,10,11,12,13,14,15,16,17,18,19,20,21,22,23,24,25,26..., dimensions={0} | all-to-all | bytes 786432 | tf_op jit(solution)/shard_map/all_to_all | solution.py:30
  78.6 19.6 %all_to_all.63 = bf16[16,48,128]{2,1,0:T(8,128)(2,1)S(1)} all-to-all(bf16[16,48,128]{2,1,0:T(8,128)(2,1)S(1)} %pad_maximum_fusion.8), channel_id=1, replica_groups={{0,32,64,96,128,160,192,224,256,288,320,352,384,416,448,480},{16,48,80,..., dimensions={0} | all-to-all | bytes 393216 | tf_op jit(solution)/shard_map/all_to_all | solution.py:33
  98.2 0.7 broadcast_in_dim.17
  98.9 8.7 %all-to-all-start.5 = ((bf16[32,24,128]{2,1,0:T(8,128)(2,1)}), bf16[32,24,128]{2,1,0:T(8,128)(2,1)S(1)}, u32[]{:S(2)}, u32[]{:S(2)}) async-start(bf16[32,24,128]{2,1,0:T(8,128)(2,1)} %broadcast_in_dim.17), calls=%async_computation.5 | async-start | bytes 393216 | tf_op jit(solution)/shard_map/all_to_all | solution.py:30
  107.8 8.0 %all-to-all-done.5 = bf16[32,24,128]{2,1,0:T(8,128)(2,1)S(1)} async-done(((bf16[32,24,128]{2,1,0:T(8,128)(2,1)}), bf16[32,24,128]{2,1,0:T(8,128)(2,1)S(1)}, u32[]{:S(2)}, u32[]{:S(2)}) %all-to-all-start.5) | async-done | bytes 196640 | tf_op jit(solution)/shard_map/all_to_all | solution.py:30
  115.8 0.2 fusion.17
  116.1 0.2 fusion.3
  116.4 17.4 %all_to_all.64 = bf16[16,48,128]{2,1,0:T(8,128)(2,1)S(1)} all-to-all(bf16[16,48,128]{2,1,0:T(8,128)(2,1)S(1)} %pad_maximum_fusion.9), channel_id=1, replica_groups={{0,32,64,96,128,160,192,224,256,288,320,352,384,416,448,480},{16,48,80,..., dimensions={0} | all-to-all | bytes 393216 | tf_op jit(solution)/shard_map/all_to_all | solution.py:33
  134.0 21.4 %all_to_all.65 = bf16[32,24,448]{2,1,0:T(8,128)(2,1)S(1)} all-to-all(bf16[32,24,448]{2,1,0:T(8,128)(2,1)S(1)} %pad_maximum_fusion.1), channel_id=1, replica_groups={{0,1,2,3,4,5,6,7,8,9,10,11,12,13,14,15,16,17,18,19,20,21,22,23,24,25,26..., dimensions={0} | all-to-all | bytes 1376256 | tf_op jit(solution)/shard_map/all_to_all | solution.py:30
  155.5 0.2 fusion.14
  155.7 0.2 fusion.4
  156.0 0.7 pad_maximum_fusion.10
  156.7 5.2 %all-to-all-start.8 = ((bf16[16,48,128]{2,1,0:T(8,128)(2,1)}), bf16[16,48,128]{2,1,0:T(8,128)(2,1)S(1)}, u32[]{:S(2)}, u32[]{:S(2)}) async-start(bf16[16,48,128]{2,1,0:T(8,128)(2,1)} %pad_maximum_fusion.10), calls=%async_computation.8 | async-start | bytes 393216 | tf_op jit(solution)/shard_map/all_to_all | solution.py:33
  161.9 12.3 %all-to-all-done.8 = bf16[16,48,128]{2,1,0:T(8,128)(2,1)S(1)} async-done(((bf16[16,48,128]{2,1,0:T(8,128)(2,1)}), bf16[16,48,128]{2,1,0:T(8,128)(2,1)S(1)}, u32[]{:S(2)}, u32[]{:S(2)}) %all-to-all-start.8) | async-done | bytes 196640 | tf_op jit(solution)/shard_map/all_to_all | solution.py:33
  174.4 0.9 pad_maximum_fusion.4
  175.3 8.9 %all-to-all-start.9 = ((bf16[32,72,128]{2,1,0:T(8,128)(2,1)}), bf16[32,72,128]{2,1,0:T(8,128)(2,1)S(1)}, u32[]{:S(2)}, u32[]{:S(2)}) async-start(bf16[32,72,128]{2,1,0:T(8,128)(2,1)} %pad_maximum_fusion.4), calls=%async_computation.9 | async-start | bytes 1179648 | tf_op jit(solution)/shard_map/all_to_all | solution.py:30
  184.2 11.7 %all-to-all-done.9 = bf16[32,72,128]{2,1,0:T(8,128)(2,1)S(1)} async-done(((bf16[32,72,128]{2,1,0:T(8,128)(2,1)}), bf16[32,72,128]{2,1,0:T(8,128)(2,1)S(1)}, u32[]{:S(2)}, u32[]{:S(2)}) %all-to-all-start.9) | async-done | bytes 589856 | tf_op jit(solution)/shard_map/all_to_all | solution.py:30
  196.0 0.3 fusion.6
  196.4 0.7 copy-done.3
  197.1 0.4 fusion
  197.5 0.2 copy.20
  197.7 3.1 %collective-permute-start = (bf16[8,40,128]{2,1,0:T(8,128)(2,1)S(1)}, bf16[8,40,128]{2,1,0:T(8,128)(2,1)S(1)}, u32[]{:S(2)}, u32[]{:S(2)}) collective-permute-start(bf16[8,40,128]{2,1,0:T(8,128)(2,1)S(1)} %fusion.20), channel_id=1, source_target_pairs={{0,16},{16,0},{32,48},{48,32},{64,80},{80,64},{96,112},{112,96},{1... | collective-permute-start | bytes 245768 | tf_op jit(solution)/shard_map/ppermute | solution.py:124
  200.8 0.9 collective-permute-done
  201.7 0.7 pad_maximum_fusion.15
  202.4 4.7 %all-to-all-start.10 = ((bf16[8,80,128]{2,1,0:T(8,128)(2,1)}), bf16[8,80,128]{2,1,0:T(8,128)(2,1)S(1)}, u32[]{:S(2)}, u32[]{:S(2)}) async-start(bf16[8,80,128]{2,1,0:T(8,128)(2,1)} %pad_maximum_fusion.15), calls=%async_computation.10 | async-start | bytes 327680 | tf_op jit(solution)/shard_map/all_to_all | solution.py:33
  207.1 10.8 %all-to-all-done.10 = bf16[8,80,128]{2,1,0:T(8,128)(2,1)S(1)} async-done(((bf16[8,80,128]{2,1,0:T(8,128)(2,1)}), bf16[8,80,128]{2,1,0:T(8,128)(2,1)S(1)}, u32[]{:S(2)}, u32[]{:S(2)}) %all-to-all-start.10) | async-done | bytes 163872 | tf_op jit(solution)/shard_map/all_to_all | solution.py:33
  218.0 17.4 %all_to_all.66 = bf16[8,2,40,128]{3,2,1,0:T(8,128)(2,1)S(1)} all-to-all(bf16[8,2,40,128]{3,2,1,0:T(8,128)(2,1)S(1)} %broadcast_in_dim.23), channel_id=1, replica_groups={{0,32,64,96,128,160,192,224},{16,48,80,112,144,176,208,240},{256,288,32..., dimensions={0} | all-to-all | bytes 327680 | tf_op jit(solution)/shard_map/all_to_all | solution.py:33
  235.4 5.1 %collective-permute-start.1 = (bf16[2,320,128]{2,1,0:T(8,128)(2,1)S(1)}, bf16[2,320,128]{2,1,0:T(8,128)(2,1)S(1)}, u32[]{:S(2)}, u32[]{:S(2)}) collective-permute-start(bf16[2,320,128]{2,1,0:T(8,128)(2,1)S(1)} %bitcast.102), channel_id=1, source_target_pairs={{0,16},{16,0},{32,48},{48,32},{64,80},{80,64},{96,112},{112,96},{1... | collective-permute-start | bytes 491528 | tf_op jit(solution)/shard_map/ppermute | solution.py:132
  240.5 1.0 collective-permute-done.1
  241.5 0.8 fusion.12
  (71 shorter events, 1.6 us)
Async XLA Ops:
  0.0 64.1 %copy-start = (bf16[1,640,640]{2,1,0:T(8,128)(2,1)S(1)}, bf16[1,640,640]{2,1,0:T(8,128)(2,1)}, u32[]{:S(2)}) copy-start(bf16[1,640,640]{2,1,0:T(8,128)(2,1)} %param.9) | copy-start | bytes 2457604
  0.0 12.3 %copy-start.4 = (s32[2,32]{1,0:T(2,128)S(1)}, s32[2,32]{1,0:T(2,128)}, u32[]{:S(2)}) copy-start(s32[2,32]{1,0:T(2,128)} %param.7) | copy-start | bytes 772
  0.0 14.9 %slice-start = ((bf16[1,640,960]{1,2,0:T(8,128)(2,1)}), bf16[1,640,320]{1,2,0:T(8,128)(2,1)S(1)}, s32[]{:S(2)}) async-start(bf16[1,640,960]{1,2,0:T(8,128)(2,1)} %param.10), calls=%async_computation.12 | async-start | bytes 819200 | tf_op jit(solution)/shard_map/slice | solution.py:82
  1.8 18.6 %all-to-all-start = ((bf16[32,24,128]{2,1,0:T(8,128)(2,1)}), bf16[32,24,128]{2,1,0:T(8,128)(2,1)S(1)}, u32[]{:S(2)}, u32[]{:S(2)}) async-start(bf16[32,24,128]{2,1,0:T(8,128)(2,1)} %pad_maximum_fusion.7), calls=%async_computation | async-start | bytes 393216 | tf_op jit(solution)/shard_map/all_to_all | solution.py:30
  14.9 1.0 slice-start.1
  15.9 1.0 slice-start.2
  40.9 22.9 %copy-start.2 = (bf16[1,640,960]{1,2,0:T(8,128)(2,1)S(1)}, bf16[1,640,960]{1,2,0:T(8,128)(2,1)}, u32[]{:S(2)}) copy-start(bf16[1,640,960]{1,2,0:T(8,128)(2,1)} %param.8) | copy-start | bytes 3686404
  98.9 16.9 %all-to-all-start.5 = ((bf16[32,24,128]{2,1,0:T(8,128)(2,1)}), bf16[32,24,128]{2,1,0:T(8,128)(2,1)S(1)}, u32[]{:S(2)}, u32[]{:S(2)}) async-start(bf16[32,24,128]{2,1,0:T(8,128)(2,1)} %broadcast_in_dim.17), calls=%async_computation.5 | async-start | bytes 393216 | tf_op jit(solution)/shard_map/all_to_all | solution.py:30
  156.7 17.5 %all-to-all-start.8 = ((bf16[16,48,128]{2,1,0:T(8,128)(2,1)}), bf16[16,48,128]{2,1,0:T(8,128)(2,1)S(1)}, u32[]{:S(2)}, u32[]{:S(2)}) async-start(bf16[16,48,128]{2,1,0:T(8,128)(2,1)} %pad_maximum_fusion.10), calls=%async_computation.8 | async-start | bytes 393216 | tf_op jit(solution)/shard_map/all_to_all | solution.py:33
  175.3 20.7 %copy-start.1 = (bf16[1,640,960]{1,2,0:T(8,128)(2,1)S(1)}, bf16[1,640,960]{1,2,0:T(8,128)(2,1)}, u32[]{:S(2)}) copy-start(bf16[1,640,960]{1,2,0:T(8,128)(2,1)} %param.10) | copy-start | bytes 3686404
  175.3 20.6 %all-to-all-start.9 = ((bf16[32,72,128]{2,1,0:T(8,128)(2,1)}), bf16[32,72,128]{2,1,0:T(8,128)(2,1)S(1)}, u32[]{:S(2)}, u32[]{:S(2)}) async-start(bf16[32,72,128]{2,1,0:T(8,128)(2,1)} %pad_maximum_fusion.4), calls=%async_computation.9 | async-start | bytes 1179648 | tf_op jit(solution)/shard_map/all_to_all | solution.py:30
  195.9 1.1 copy-start.3
  197.7 4.0 %collective-permute-start = (bf16[8,40,128]{2,1,0:T(8,128)(2,1)S(1)}, bf16[8,40,128]{2,1,0:T(8,128)(2,1)S(1)}, u32[]{:S(2)}, u32[]{:S(2)}) collective-permute-start(bf16[8,40,128]{2,1,0:T(8,128)(2,1)S(1)} %fusion.20), channel_id=1, source_target_pairs={{0,16},{16,0},{32,48},{48,32},{64,80},{80,64},{96,112},{112,96},{1... | collective-permute-start | bytes 245768 | tf_op jit(solution)/shard_map/ppermute | solution.py:124
  202.4 15.5 %all-to-all-start.10 = ((bf16[8,80,128]{2,1,0:T(8,128)(2,1)}), bf16[8,80,128]{2,1,0:T(8,128)(2,1)S(1)}, u32[]{:S(2)}, u32[]{:S(2)}) async-start(bf16[8,80,128]{2,1,0:T(8,128)(2,1)} %pad_maximum_fusion.15), calls=%async_computation.10 | async-start | bytes 327680 | tf_op jit(solution)/shard_map/all_to_all | solution.py:33
  235.4 6.1 %collective-permute-start.1 = (bf16[2,320,128]{2,1,0:T(8,128)(2,1)S(1)}, bf16[2,320,128]{2,1,0:T(8,128)(2,1)S(1)}, u32[]{:S(2)}, u32[]{:S(2)}) collective-permute-start(bf16[2,320,128]{2,1,0:T(8,128)(2,1)S(1)} %bitcast.102), channel_id=1, source_target_pairs={{0,16},{16,0},{32,48},{48,32},{64,80},{80,64},{96,112},{112,96},{1... | collective-permute-start | bytes 491528 | tf_op jit(solution)/shard_map/ppermute | solution.py:132

commit v6 on v3

v6 whole, which is shorter than its diff:
```python
import jax
import jax.numpy as jnp
from jax import lax
from jax.sharding import PartitionSpec as P

BLK = 128
WIN = 24
PIECE = 40
LO = PIECE - WIN


def body(forcing, live, lower_inv, lower_upd, upper_inv, upper_upd):
    n_leaf = lax.axis_size("leaf")
    n_front = lax.axis_size("front")
    n_z = n_leaf // 2
    half = n_z // 2
    sep_dev, n_rhs = forcing.shape[1:]
    w0, w1 = sep_dev, sep_dev // 2
    n_plane = 2 * n_front
    height = n_front * WIN
    tail = w1 % n_rhs
    head = w1 - tail
    bf, f32, i32, u32 = jnp.bfloat16, jnp.float32, jnp.int32, jnp.uint32
    leaf_id = lax.axis_index("leaf").astype(u32)
    front_id = lax.axis_index("front").astype(u32)
    z, core = leaf_id // 2, leaf_id % 2
    node, z8 = z // half, z % half

    plane = [[(2 * k + c) * n_front + f for c in range(2) for f in range(n_front)] for k in range(n_z)]
    z_all = [[2 * k + c for k in range(n_z)] for c in range(2)]
    z_half = [[2 * (h * half + k) + c for k in range(half)] for h in range(2) for c in range(2)]
    swap = [(k, k ^ 1) for k in range(n_leaf)]

    def a2a_plane(v):
        return lax.all_to_all(v, ("leaf", "front"), 0, 0, axis_index_groups=plane)

    def a2a_leaf(v, groups):
        return lax.all_to_all(v, "leaf", 0, 0, axis_index_groups=groups)

    def spread(v, n):
        return jnp.broadcast_to(v[None], (n,) + v.shape)

    def by_core(v):
        return jnp.broadcast_to(v[:, None], (2, n_front) + v.shape[1:]).reshape((n_plane,) + v.shape[1:])

    def cut(v):
        v = v.reshape(n_front, PIECE, v.shape[-1])
        return jnp.concatenate([v[:, :WIN], v[:, LO:]], 0)

    def join(v):
        low, high = v[:n_front], v[n_front:, WIN - LO :]
        return jnp.concatenate([low, high], 1).reshape(n_front * PIECE, v.shape[-1])

    def fold(v):
        return v[:n_front].astype(f32) + v[n_front:].astype(f32)

    def total(v):
        return jnp.sum(v.astype(f32), 0)

    def pick(v, k, n):
        return lax.dynamic_slice(v, (k,) + (u32(0),) * (v.ndim - 1), (n,) + v.shape[1:])

    def masked(v, keep):
        return jnp.where(keep[..., None], v, 0.0).astype(bf)

    def dot(a, b):
        return jnp.dot(a, b, preferred_element_type=f32)

    def panel(mat, h, first, last):
        return mat.reshape(2 * height, mat.shape[-1])[h * height : (h + 1) * height, first:last]

    live_a, live_b, live_root = (live[k].reshape(()) * BLK for k in ((0, slice(0, 1)), (0, slice(1, 2)), (1, slice(0, 1))))
    live_node = jnp.where(node == 0, live_a, live_b)
    here = (front_id * PIECE + core * LO).astype(i32)
    at_out = (front_id * sep_dev + (core * half + z8) * PIECE).astype(i32)
    kind = lax.iota(i32, 8)
    count = jnp.where(kind == 2, live_a, jnp.where(kind == 3, live_b, jnp.where((kind < 4) | (kind > 6), live_node, live_root)))
    block = jnp.where((kind > 1) & (kind < 5), z.astype(i32), 2 * z8.astype(i32) + ((kind == 1) | (kind == 6)).astype(i32))
    begin = jnp.where(kind == 7, at_out, here + block * sep_dev)
    keep = lax.broadcasted_iota(i32, (8, PIECE), 1) < (count - begin)[:, None]
    keep = (keep[0:2, :WIN], keep[2, :WIN], keep[3, :WIN], keep[4, :WIN], keep[5:7, :WIN], keep[7])
    scalars = (keep, core, 1 - core, 2 * z8, front_id // 2)

    got = a2a_plane(cut(forcing[0]))
    uinv1 = cut(upper_inv[0, :, w0:])
    extra = jnp.concatenate([cut(lower_inv[0, :, w0:]), uinv1[:, :, head:]], 2)
    got, extra, uinv1, scalars = lax.optimization_barrier((got, extra, uinv1[:, :, :head], scalars))
    keep, core, other_core, two_z8, half_front = scalars

    pair = fold(got).astype(bf).reshape(half, 2 * WIN, n_rhs)
    r0 = total(a2a_leaf(pair, z_half)).reshape(2, WIN, n_rhs)
    moved = a2a_plane(jnp.concatenate([by_core(masked(r0, keep[0])), extra], 2))
    rm0 = join(moved[:, :, :n_rhs])

    c_part = dot(lower_upd[0], rm0).astype(bf)
    y_part = dot(lower_inv[0, :, :w0], rm0).astype(bf)
    parts = fold(a2a_plane(cut(jnp.concatenate([c_part, y_part], 1)))).astype(bf)

    got = a2a_leaf(jnp.concatenate([parts[:, :, :n_rhs], parts[:, :, n_rhs:]], 1), z_all)
    r1 = masked(-total(got[:, :WIN]), keep[3])
    y0 = jnp.stack([masked(total(got[:half, WIN:]), keep[1]), masked(total(got[half:, WIN:]), keep[2])])
    y0 = jnp.broadcast_to(y0[:, None], (2, half, WIN, n_rhs)).reshape(n_z, WIN, n_rhs)
    r1, y0 = lax.optimization_barrier((spread(r1, n_plane), y0))
    r1 = join(a2a_plane(r1))

    blank = jnp.zeros((n_rhs - tail, n_rhs), bf)
    y1 = sum(
        dot(panel(moved, h, n_rhs, n_rhs + w1 + tail), jnp.concatenate([r1[h * w1 : (h + 1) * w1], blank], 0))
        for h in range(2)
    )
    got = a2a_leaf(jnp.concatenate([y1.astype(bf).reshape(n_front, WIN, n_rhs), y0], 1), z_all)
    y1 = masked(total(got[:, :WIN]), keep[3])
    y0 = pick(got[:, WIN:], two_z8, 2)
    got = a2a_plane(jnp.concatenate([spread(y1, n_plane), by_core(y0), uinv1], 2))
    y1 = join(got[:, :, :n_rhs])
    y0 = join(got[:, :, n_rhs : 2 * n_rhs])

    x1 = 0.0
    for h in range(2):
        v = y1[h * w1 : (h + 1) * w1]
        x1 = x1 + dot(panel(got, h, 2 * n_rhs, 2 * n_rhs + head), v[:head])
        x1 = x1 + dot(panel(moved, h, n_rhs + head, n_rhs + head + n_rhs), jnp.concatenate([blank, v[head:]], 0))
    x1 = x1.astype(bf).reshape(half, 2 * WIN, n_rhs)
    x1, term = lax.optimization_barrier((jnp.concatenate([x1, x1], 0), dot(upper_inv[0, :, :w0], y0)))
    x1 = masked(total(a2a_leaf(x1, z_all)).reshape(2, WIN, n_rhs), keep[4])
    own = jnp.broadcast_to(x1[None, None], (2, n_front // 2) + x1.shape).reshape(n_plane, WIN, n_rhs)
    got = a2a_plane(jnp.concatenate([by_core(x1), own], 1))
    x1 = join(got[:, :WIN])
    own = join(got[:, WIN:])

    term = (term - dot(upper_upd[0], x1)).reshape(2, half, PIECE, n_rhs)
    away = pick(term, other_core, 1)[0].astype(bf)
    own = pick(own.reshape(2, half, PIECE, n_rhs), core, 1)[0]
    away = lax.ppermute(away, "leaf", swap)
    term = (pick(term, core, 1)[0] + away.astype(f32)).astype(bf)
    got = a2a_leaf(jnp.concatenate([term, own], 1), z_half)

    x0 = masked(total(got[:, :PIECE]), keep[5])
    x1 = pick(got[:, PIECE:], half_front, 1)[0]
    both = a2a_leaf(spread(jnp.stack([x0, x1]), half), z_half)
    both = jnp.swapaxes(both, 0, 1).reshape(2, half * PIECE, n_rhs)
    other = lax.ppermute(both, "leaf", swap)
    both = jnp.where(core == 0, jnp.concatenate([both, other], 1), jnp.concatenate([other, both], 1))
    return both[:, None]


def solution(mesh):
    return jax.shard_map(
        body,
        mesh=mesh,
        in_specs=(
            P("leaf", "front", None),
            P(),
            P("leaf", "front", None),
            P("leaf", "front", None),
            P("leaf", "front", None),
            P("leaf", "front", None),
        ),
        out_specs=P(None, "leaf", "front", None),
        check_vma=False,
    )
```

time: 244 us -> 234 us (0.959)
  blocking collectives: 83 us -> 196 us
  waiting for transfers between devices: 78.8 us -> 5.54 us
  starting transfers between devices: 61.1 us -> 18.7 us
  other arithmetic: 8.11 us -> 2.97 us
  local copies, waits for them, and re-layouts: 7.64 us -> 4.67 us
    all_to_all x2 -> x5, blocking collectives: 32.3 us -> 89.2 us  [a2a_plane(): return lax.all_to_all(v, ('leaf', 'front'), 0, 0, axis_index_groups=plane)]
    all_to_all x3 -> x6, blocking collectives: 50.6 us -> 107 us  [a2a_leaf(): return lax.all_to_all(v, 'leaf', 0, 0, axis_index_groups=groups)]
    all_to_all x4 -> x1, waiting for transfers between devices: 45.8 us -> 3.69 us  [a2a_plane(): return lax.all_to_all(v, ('leaf', 'front'), 0, 0, axis_index_groups=plane)]
    all_to_all x3 -> x0, waiting for transfers between devices: 31 us -> none  [a2a_leaf(): return lax.all_to_all(v, 'leaf', 0, 0, axis_index_groups=groups)]
    all_to_all x3 -> x0, starting transfers between devices: 23 us -> none  [a2a_leaf(): return lax.all_to_all(v, 'leaf', 0, 0, axis_index_groups=groups)]
    all_to_all x4 -> x1, starting transfers between devices: 29.8 us -> 10.5 us  [a2a_plane(): return lax.all_to_all(v, ('leaf', 'front'), 0, 0, axis_index_groups=plane)]
  transfers between devices with their start and end apart: 9 -> 3, of which waited for: 9 -> 3; matrix products, arithmetic and copies ran while one was open for 2% -> 1% of each run, Pallas kernels for 0% -> 0%
where the time goes in v6:
time: 234 us
  blocking collectives  196 us (84%)
  starting transfers between devices  18.7 us (8%)
  waiting for transfers between devices  5.54 us (2%)
  local copies, waits for them, and re-layouts  4.67 us (2%)
  other arithmetic  2.97 us (1%)
  matrix products  2.67 us (1%)
  between operations  2.6 us (1%)
    all_to_all x6, blocking collectives, a2a_leaf(): return lax.all_to_all(v, 'leaf', 0, 0, axis_index_groups=groups)  107 us
    all_to_all x5, blocking collectives, a2a_plane(): return lax.all_to_all(v, ('leaf', 'front'), 0, 0, axis_index_groups=plane)  89.2 us
    all_to_all x1, starting transfers between devices, a2a_plane(): return lax.all_to_all(v, ('leaf', 'front'), 0, 0, axis_index_groups=plane)  10.5 us
    ppermute x1, starting transfers between devices, body(): other = lax.ppermute(both, 'leaf', swap)  5.11 us
  transfers between devices with their start and end apart: 3, of which 3 were waited for; matrix products, arithmetic and copies ran while one was open for 1% of the time, Pallas kernels for 0%

profile of v6, /device:TPU:1, one launch (start us, length us, event | category | flops | bytes accessed | tf_op | source)
XLA Modules:
  0.0 233.5 jit_solution(1419997105331753435)
XLA Ops:
  0.0 1.1 fusion.53
  1.1 0.7 pad_maximum_fusion.6
  1.8 10.5 %all-to-all-start = ((bf16[32,24,128]{2,1,0:T(8,128)(2,1)}), bf16[32,24,128]{2,1,0:T(8,128)(2,1)S(1)}, u32[]{:S(2)}, u32[]{:S(2)}) async-start(bf16[32,24,128]{2,1,0:T(8,128)(2,1)} %pad_maximum_fusion.6), calls=%async_computation | async-start | bytes 393216 | tf_op jit(solution)/shard_map/all_to_all | solution.py:35
  12.3 0.7 fusion.55
  15.0 0.1 iota_compare_fusion.1
  15.1 0.3 copy.26
  15.4 0.7 slice-done.1
  16.1 0.3 copy.27
  16.4 0.1 fusion.47
  16.5 0.1 fusion.15
  16.7 3.7 %all-to-all-done = bf16[32,24,128]{2,1,0:T(8,128)(2,1)S(1)} async-done(((bf16[32,24,128]{2,1,0:T(8,128)(2,1)}), bf16[32,24,128]{2,1,0:T(8,128)(2,1)S(1)}, u32[]{:S(2)}, u32[]{:S(2)}) %all-to-all-start) | async-done | bytes 196640 | tf_op jit(solution)/shard_map/all_to_all | solution.py:35
  20.4 20.2 %all_to_all.60 = bf16[8,48,128]{2,1,0:T(8,128)(2,1)S(1)} all-to-all(bf16[8,48,128]{2,1,0:T(8,128)(2,1)S(1)} %bitcast.112), channel_id=1, replica_groups={{0,32,64,96,128,160,192,224},{16,48,80,112,144,176,208,240},{256,288,32..., dimensions={0} | all-to-all | bytes 196608 | tf_op jit(solution)/shard_map/all_to_all | solution.py:38
  40.6 0.1 select_convert_fusion.1
  40.7 0.1 pad_maximum_fusion
  40.8 19.3 %all_to_all.61 = bf16[32,24,512]{2,1,0:T(8,128)(2,1)S(1)} all-to-all(bf16[32,24,512]{2,1,0:T(8,128)(2,1)S(1)} %pad_maximum_fusion), channel_id=1, replica_groups={{0,1,2,3,4,5,6,7,8,9,10,11,12,13,14,15,16,17,18,19,20,21,22,23,24,25,26..., dimensions={0} | all-to-all | bytes 1572864 | tf_op jit(solution)/shard_map/all_to_all | solution.py:35
  60.2 0.3 fusion.5
  60.6 0.4 fusion.4
  61.0 0.2 copy.22
  61.3 13.6 %all_to_all.62 = bf16[32,24,256]{2,1,0:T(8,128)(2,1)S(1)} all-to-all(bf16[32,24,256]{2,1,0:T(8,128)(2,1)S(1)} %pad_maximum_fusion.3), channel_id=1, replica_groups={{0,1,2,3,4,5,6,7,8,9,10,11,12,13,14,15,16,17,18,19,20,21,22,23,24,25,26..., dimensions={0} | all-to-all | bytes 786432 | tf_op jit(solution)/shard_map/all_to_all | solution.py:35
  75.1 19.6 %all_to_all.63 = bf16[16,48,128]{2,1,0:T(8,128)(2,1)S(1)} all-to-all(bf16[16,48,128]{2,1,0:T(8,128)(2,1)S(1)} %pad_maximum_fusion.7), channel_id=1, replica_groups={{0,32,64,96,128,160,192,224,256,288,320,352,384,416,448,480},{16,48,80,..., dimensions={0} | all-to-all | bytes 393216 | tf_op jit(solution)/shard_map/all_to_all | solution.py:38
  94.7 0.1 select_convert_fusion.3
  94.8 0.1 fusion.37
  94.8 0.1 fusion.38
  95.0 16.6 %all_to_all.64 = bf16[32,24,128]{2,1,0:T(8,128)(2,1)S(1)} all-to-all(bf16[32,24,128]{2,1,0:T(8,128)(2,1)S(1)} %broadcast_in_dim.151), channel_id=1, replica_groups={{0,1,2,3,4,5,6,7,8,9,10,11,12,13,14,15,16,17,18,19,20,21,22,23,24,25,26..., dimensions={0} | all-to-all | bytes 393216 | tf_op jit(solution)/shard_map/all_to_all | solution.py:35
  111.6 0.2 fusion.18
  111.9 0.2 fusion.6
  112.2 17.4 %all_to_all.65 = bf16[16,48,128]{2,1,0:T(8,128)(2,1)S(1)} all-to-all(bf16[16,48,128]{2,1,0:T(8,128)(2,1)S(1)} %pad_maximum_fusion.8), channel_id=1, replica_groups={{0,32,64,96,128,160,192,224,256,288,320,352,384,416,448,480},{16,48,80,..., dimensions={0} | all-to-all | bytes 393216 | tf_op jit(solution)/shard_map/all_to_all | solution.py:38
  129.6 0.1 select_convert_fusion.2
  129.8 21.4 %all_to_all.66 = bf16[32,24,512]{2,1,0:T(8,128)(2,1)S(1)} all-to-all(bf16[32,24,512]{2,1,0:T(8,128)(2,1)S(1)} %pad_maximum_fusion.1), channel_id=1, replica_groups={{0,1,2,3,4,5,6,7,8,9,10,11,12,13,14,15,16,17,18,19,20,21,22,23,24,25,26..., dimensions={0} | all-to-all | bytes 1572864 | tf_op jit(solution)/shard_map/all_to_all | solution.py:35
  151.3 0.2 fusion.22
  151.6 0.2 fusion.20
  151.8 0.2 fusion.3
  151.9 0.2 fusion.7
  152.2 0.7 copy-done.2
  152.8 0.3 convolution_bitcast_fusion.1
  153.2 17.3 %all_to_all.67 = bf16[16,48,128]{2,1,0:T(8,128)(2,1)S(1)} all-to-all(bf16[16,48,128]{2,1,0:T(8,128)(2,1)S(1)} %pad_maximum_fusion.9), channel_id=1, replica_groups={{0,32,64,96,128,160,192,224,256,288,320,352,384,416,448,480},{16,48,80,..., dimensions={0} | all-to-all | bytes 393216 | tf_op jit(solution)/shard_map/all_to_all | solution.py:38
  170.5 0.1 select_convert_fusion
  170.7 18.2 %all_to_all.68 = bf16[32,48,128]{2,1,0:T(8,128)(2,1)S(1)} all-to-all(bf16[32,48,128]{2,1,0:T(8,128)(2,1)S(1)} %pad_maximum_fusion.4), channel_id=1, replica_groups={{0,1,2,3,4,5,6,7,8,9,10,11,12,13,14,15,16,17,18,19,20,21,22,23,24,25,26..., dimensions={0} | all-to-all | bytes 786432 | tf_op jit(solution)/shard_map/all_to_all | solution.py:35
  189.0 0.4 fusion
  189.4 0.2 copy.23
  189.6 3.1 %collective-permute-start = (bf16[8,40,128]{2,1,0:T(8,128)(2,1)S(1)}, bf16[8,40,128]{2,1,0:T(8,128)(2,1)S(1)}, u32[]{:S(2)}, u32[]{:S(2)}) collective-permute-start(bf16[8,40,128]{2,1,0:T(8,128)(2,1)S(1)} %fusion.29), channel_id=1, source_target_pairs={{0,16},{16,0},{32,48},{48,32},{64,80},{80,64},{96,112},{112,96},{1... | collective-permute-start | bytes 245768 | tf_op jit(solution)/shard_map/ppermute | solution.py:134
  192.8 0.9 collective-permute-done
  193.7 15.3 %all_to_all.69 = bf16[8,80,128]{2,1,0:T(8,128)(2,1)S(1)} all-to-all(bf16[8,80,128]{2,1,0:T(8,128)(2,1)S(1)} %pad_maximum_fusion.14), channel_id=1, replica_groups={{0,32,64,96,128,160,192,224},{16,48,80,112,144,176,208,240},{256,288,32..., dimensions={0} | all-to-all | bytes 327680 | tf_op jit(solution)/shard_map/all_to_all | solution.py:38
  209.1 0.1 fusion.36
  209.2 17.4 %all_to_all.70 = bf16[8,2,40,128]{3,2,1,0:T(8,128)(2,1)S(1)} all-to-all(bf16[8,2,40,128]{3,2,1,0:T(8,128)(2,1)S(1)} %broadcast_in_dim.162), channel_id=1, replica_groups={{0,32,64,96,128,160,192,224},{16,48,80,112,144,176,208,240},{256,288,32..., dimensions={0} | all-to-all | bytes 327680 | tf_op jit(solution)/shard_map/all_to_all | solution.py:38
  226.6 5.1 %collective-permute-start.1 = (bf16[2,320,128]{2,1,0:T(8,128)(2,1)S(1)}, bf16[2,320,128]{2,1,0:T(8,128)(2,1)S(1)}, u32[]{:S(2)}, u32[]{:S(2)}) collective-permute-start(bf16[2,320,128]{2,1,0:T(8,128)(2,1)S(1)} %bitcast.109), channel_id=1, source_target_pairs={{0,16},{16,0},{32,48},{48,32},{64,80},{80,64},{96,112},{112,96},{1... | collective-permute-start | bytes 491528 | tf_op jit(solution)/shard_map/ppermute | solution.py:142
  231.7 1.0 collective-permute-done.1
  232.7 0.8 fusion.16
  (69 shorter events, 1.2 us)
Async XLA Ops:
  0.0 60.6 %copy-start = (bf16[1,640,640]{2,1,0:T(8,128)(2,1)S(1)}, bf16[1,640,640]{2,1,0:T(8,128)(2,1)}, u32[]{:S(2)}) copy-start(bf16[1,640,640]{2,1,0:T(8,128)(2,1)} %param.9) | copy-start | bytes 2457604
  0.0 12.3 %copy-start.4 = (s32[2,32]{1,0:T(2,128)S(1)}, s32[2,32]{1,0:T(2,128)}, u32[]{:S(2)}) copy-start(s32[2,32]{1,0:T(2,128)} %param.7) | copy-start | bytes 772
  0.0 15.1 %slice-start = ((bf16[1,640,960]{1,2,0:T(8,128)(2,1)}), bf16[1,640,320]{1,2,0:T(8,128)(2,1)S(1)}, s32[]{:S(2)}) async-start(bf16[1,640,960]{1,2,0:T(8,128)(2,1)} %param.8), calls=%async_computation.12 | async-start | bytes 819200 | tf_op jit(solution)/shard_map/slice | solution.py:86
  1.8 18.6 %all-to-all-start = ((bf16[32,24,128]{2,1,0:T(8,128)(2,1)}), bf16[32,24,128]{2,1,0:T(8,128)(2,1)S(1)}, u32[]{:S(2)}, u32[]{:S(2)}) async-start(bf16[32,24,128]{2,1,0:T(8,128)(2,1)} %pad_maximum_fusion.6), calls=%async_computation | async-start | bytes 393216 | tf_op jit(solution)/shard_map/all_to_all | solution.py:35
  15.1 1.0 slice-start.1
  40.8 19.4 %copy-start.1 = (bf16[1,640,960]{1,2,0:T(8,128)(2,1)S(1)}, bf16[1,640,960]{1,2,0:T(8,128)(2,1)}, u32[]{:S(2)}) copy-start(bf16[1,640,960]{1,2,0:T(8,128)(2,1)} %param.8) | copy-start | bytes 3686404
  151.5 1.3 copy-start.2
  170.7 18.3 %copy-start.3 = (bf16[1,640,640]{2,1,0:T(8,128)(2,1)S(1)}, bf16[1,640,640]{2,1,0:T(8,128)(2,1)}, u32[]{:S(2)}) copy-start(bf16[1,640,640]{2,1,0:T(8,128)(2,1)} %param.11) | copy-start | bytes 2457604
  189.6 4.0 %collective-permute-start = (bf16[8,40,128]{2,1,0:T(8,128)(2,1)S(1)}, bf16[8,40,128]{2,1,0:T(8,128)(2,1)S(1)}, u32[]{:S(2)}, u32[]{:S(2)}) collective-permute-start(bf16[8,40,128]{2,1,0:T(8,128)(2,1)S(1)} %fusion.29), channel_id=1, source_target_pairs={{0,16},{16,0},{32,48},{48,32},{64,80},{80,64},{96,112},{112,96},{1... | collective-permute-start | bytes 245768 | tf_op jit(solution)/shard_map/ppermute | solution.py:134
  226.6 6.1 %collective-permute-start.1 = (bf16[2,320,128]{2,1,0:T(8,128)(2,1)S(1)}, bf16[2,320,128]{2,1,0:T(8,128)(2,1)S(1)}, u32[]{:S(2)}, u32[]{:S(2)}) collective-permute-start(bf16[2,320,128]{2,1,0:T(8,128)(2,1)S(1)} %bitcast.109), channel_id=1, source_target_pairs={{0,16},{16,0},{32,48},{48,32},{64,80},{80,64},{96,112},{112,96},{1... | collective-permute-start | bytes 491528 | tf_op jit(solution)/shard_map/ppermute | solution.py:142

commit v7 on v6

--- a/solution.py
+++ b/solution.py
@@ -28,7 +28,9 @@
 
     plane = [[(2 * k + c) * n_front + f for c in range(2) for f in range(n_front)] for k in range(n_z)]
     z_all = [[2 * k + c for k in range(n_z)] for c in range(2)]
-    z_half = [[2 * (h * half + k) + c for k in range(half)] for h in range(2) for c in range(2)]
+    mid = half // 2
+    order = [mid] + [k for k in range(half) if k != mid]
+    z_half = [[2 * (h * half + k) + c for k in order] for h in range(2) for c in range(2)]
     swap = [(k, k ^ 1) for k in range(n_leaf)]
 
     def a2a_plane(v):
@@ -36,6 +38,9 @@
 
     def a2a_leaf(v, groups):
         return lax.all_to_all(v, "leaf", 0, 0, axis_index_groups=groups)
+
+    def place(k):
+        return jnp.where(k == mid, u32(0), jnp.where(k < mid, k + 1, k))
 
     def spread(v, n):
         return jnp.broadcast_to(v[None], (n,) + v.shape)
@@ -72,22 +77,23 @@
     live_a, live_b, live_root = (live[k].reshape(()) * BLK for k in ((0, slice(0, 1)), (0, slice(1, 2)), (1, slice(0, 1))))
     live_node = jnp.where(node == 0, live_a, live_b)
     here = (front_id * PIECE + core * LO).astype(i32)
-    at_out = (front_id * sep_dev + (core * half + z8) * PIECE).astype(i32)
+    at_out = (front_id * sep_dev + (core * half + place(z8)) * PIECE).astype(i32)
     kind = lax.iota(i32, 8)
     count = jnp.where(kind == 2, live_a, jnp.where(kind == 3, live_b, jnp.where((kind < 4) | (kind > 6), live_node, live_root)))
     block = jnp.where((kind > 1) & (kind < 5), z.astype(i32), 2 * z8.astype(i32) + ((kind == 1) | (kind == 6)).astype(i32))
     begin = jnp.where(kind == 7, at_out, here + block * sep_dev)
     keep = lax.broadcasted_iota(i32, (8, PIECE), 1) < (count - begin)[:, None]
     keep = (keep[0:2, :WIN], keep[2, :WIN], keep[3, :WIN], keep[4, :WIN], keep[5:7, :WIN], keep[7])
-    scalars = (keep, core, 1 - core, 2 * z8, front_id // 2)
+    scalars = (keep, core, 1 - core, 2 * z8, place(front_id // 2), core == front_id % 2)
 
     got = a2a_plane(cut(forcing[0]))
     uinv1 = cut(upper_inv[0, :, w0:])
     extra = jnp.concatenate([cut(lower_inv[0, :, w0:]), uinv1[:, :, head:]], 2)
     got, extra, uinv1, scalars = lax.optimization_barrier((got, extra, uinv1[:, :, :head], scalars))
-    keep, core, other_core, two_z8, half_front = scalars
+    keep, core, other_core, two_z8, source, mine = scalars
 
     pair = fold(got).astype(bf).reshape(half, 2 * WIN, n_rhs)
+    pair = jnp.concatenate([pair[mid : mid + 1], pair[:mid], pair[mid + 1 :]], 0)
     r0 = total(a2a_leaf(pair, z_half)).reshape(2, WIN, n_rhs)
     moved = a2a_plane(jnp.concatenate([by_core(masked(r0, keep[0])), extra], 2))
     rm0 = join(moved[:, :, :n_rhs])
@@ -121,22 +127,21 @@
         x1 = x1 + dot(panel(got, h, 2 * n_rhs, 2 * n_rhs + head), v[:head])
         x1 = x1 + dot(panel(moved, h, n_rhs + head, n_rhs + head + n_rhs), jnp.concatenate([blank, v[head:]], 0))
     x1 = x1.astype(bf).reshape(half, 2 * WIN, n_rhs)
-    x1, term = lax.optimization_barrier((jnp.concatenate([x1, x1], 0), dot(upper_inv[0, :, :w0], y0)))
+    x1, y0 = lax.optimization_barrier((jnp.concatenate([x1, x1], 0), y0))
     x1 = masked(total(a2a_leaf(x1, z_all)).reshape(2, WIN, n_rhs), keep[4])
-    own = jnp.broadcast_to(x1[None, None], (2, n_front // 2) + x1.shape).reshape(n_plane, WIN, n_rhs)
-    got = a2a_plane(jnp.concatenate([by_core(x1), own], 1))
-    x1 = join(got[:, :WIN])
-    own = join(got[:, WIN:])
+    x1, y0 = lax.optimization_barrier((a2a_plane(by_core(x1)), y0))
+    x1 = join(x1)
 
-    term = (term - dot(upper_upd[0], x1)).reshape(2, half, PIECE, n_rhs)
-    away = pick(term, other_core, 1)[0].astype(bf)
-    own = pick(own.reshape(2, half, PIECE, n_rhs), core, 1)[0]
+    term = (dot(upper_inv[0, :, :w0], y0) - dot(upper_upd[0], x1)).reshape(2, half, PIECE, n_rhs)
+    x1 = x1.reshape(2, half, PIECE, n_rhs)
+    away = jnp.concatenate([pick(term, other_core, 1)[0].astype(bf), pick(x1, other_core, 1)[0]], 1)
     away = lax.ppermute(away, "leaf", swap)
-    term = (pick(term, core, 1)[0] + away.astype(f32)).astype(bf)
+    term = (pick(term, core, 1)[0] + away[:, :PIECE].astype(f32)).astype(bf)
+    own = jnp.where(mine, pick(x1, core, 1)[0], away[:, PIECE:])
     got = a2a_leaf(jnp.concatenate([term, own], 1), z_half)
 
     x0 = masked(total(got[:, :PIECE]), keep[5])
-    x1 = pick(got[:, PIECE:], half_front, 1)[0]
+    x1 = pick(got[:, PIECE:], source, 1)[0]
     both = a2a_leaf(spread(jnp.stack([x0, x1]), half), z_half)
     both = jnp.swapaxes(both, 0, 1).reshape(2, half * PIECE, n_rhs)
     other = lax.ppermute(both, "leaf", swap)

time: 234 us -> 222 us (0.949)
  blocking collectives: 196 us -> 184 us
    all_to_all x6, blocking collectives: 107 us -> 96.1 us  [a2a_leaf(): return lax.all_to_all(v, 'leaf', 0, 0, axis_index_groups=groups)]
where the time goes in v7:
time: 222 us
  blocking collectives  184 us (83%)
  starting transfers between devices  19.3 us (9%)
  waiting for transfers between devices  5.78 us (3%)
  local copies, waits for them, and re-layouts  3.96 us (2%)
  other arithmetic  2.95 us (1%)
  matrix products  2.68 us (1%)
  between operations  2.55 us (1%)
    all_to_all x6, blocking collectives, a2a_leaf(): return lax.all_to_all(v, 'leaf', 0, 0, axis_index_groups=groups)  96.1 us
    all_to_all x5, blocking collectives, a2a_plane(): return lax.all_to_all(v, ('leaf', 'front'), 0, 0, axis_index_groups=plane)  88.3 us
    all_to_all x1, starting transfers between devices, a2a_plane(): return lax.all_to_all(v, ('leaf', 'front'), 0, 0, axis_index_groups=plane)  10.5 us
    ppermute x1, starting transfers between devices, body(): other = lax.ppermute(both, 'leaf', swap)  6.36 us
  transfers between devices with their start and end apart: 3, of which 3 were waited for; matrix products, arithmetic and copies ran while one was open for 1% of the time, Pallas kernels for 0%

profile of v7, /device:TPU:1, one launch (start us, length us, event | category | flops | bytes accessed | tf_op | source)
XLA Modules:
  0.0 221.7 jit_solution(2947599129200289992)
XLA Ops:
  0.0 1.1 fusion.52
  1.1 0.7 pad_maximum_fusion.5
  1.8 10.5 %all-to-all-start = ((bf16[32,24,128]{2,1,0:T(8,128)(2,1)}), bf16[32,24,128]{2,1,0:T(8,128)(2,1)S(1)}, u32[]{:S(2)}, u32[]{:S(2)}) async-start(bf16[32,24,128]{2,1,0:T(8,128)(2,1)} %pad_maximum_fusion.5), calls=%async_computation | async-start | bytes 393216 | tf_op jit(solution)/shard_map/all_to_all | solution.py:37
  12.3 0.7 fusion.54
  14.9 0.1 iota_compare_fusion.1
  15.0 0.3 copy.25
  15.3 0.7 slice-done.1
  16.0 0.3 copy.26
  16.3 0.1 fusion.48
  16.4 0.1 fusion.16
  16.6 3.8 %all-to-all-done = bf16[32,24,128]{2,1,0:T(8,128)(2,1)S(1)} async-done(((bf16[32,24,128]{2,1,0:T(8,128)(2,1)}), bf16[32,24,128]{2,1,0:T(8,128)(2,1)S(1)}, u32[]{:S(2)}, u32[]{:S(2)}) %all-to-all-start) | async-done | bytes 196640 | tf_op jit(solution)/shard_map/all_to_all | solution.py:37
  20.5 15.1 %all_to_all.60 = bf16[8,48,128]{2,1,0:T(8,128)(2,1)S(1)} all-to-all(bf16[8,48,128]{2,1,0:T(8,128)(2,1)S(1)} %pad_maximum_fusion.14), channel_id=1, replica_groups={{128,0,32,64,96,160,192,224},{144,16,48,80,112,176,208,240},{384,256,28..., dimensions={0} | all-to-all | bytes 196608 | tf_op jit(solution)/shard_map/all_to_all | solution.py:40
  35.6 0.1 select_convert_fusion.1
  35.7 0.1 pad_maximum_fusion
  35.8 19.9 %all_to_all.61 = bf16[32,24,512]{2,1,0:T(8,128)(2,1)S(1)} all-to-all(bf16[32,24,512]{2,1,0:T(8,128)(2,1)S(1)} %pad_maximum_fusion), channel_id=1, replica_groups={{0,1,2,3,4,5,6,7,8,9,10,11,12,13,14,15,16,17,18,19,20,21,22,23,24,25,26..., dimensions={0} | all-to-all | bytes 1572864 | tf_op jit(solution)/shard_map/all_to_all | solution.py:37
  55.8 0.3 fusion.5
  56.1 0.4 fusion.4
  56.6 0.2 copy.21
  56.8 13.6 %all_to_all.62 = bf16[32,24,256]{2,1,0:T(8,128)(2,1)S(1)} all-to-all(bf16[32,24,256]{2,1,0:T(8,128)(2,1)S(1)} %pad_maximum_fusion.3), channel_id=1, replica_groups={{0,1,2,3,4,5,6,7,8,9,10,11,12,13,14,15,16,17,18,19,20,21,22,23,24,25,26..., dimensions={0} | all-to-all | bytes 786432 | tf_op jit(solution)/shard_map/all_to_all | solution.py:37
  70.6 21.2 %all_to_all.63 = bf16[16,48,128]{2,1,0:T(8,128)(2,1)S(1)} all-to-all(bf16[16,48,128]{2,1,0:T(8,128)(2,1)S(1)} %pad_maximum_fusion.6), channel_id=1, replica_groups={{0,32,64,96,128,160,192,224,256,288,320,352,384,416,448,480},{16,48,80,..., dimensions={0} | all-to-all | bytes 393216 | tf_op jit(solution)/shard_map/all_to_all | solution.py:40
  91.8 0.1 fusion.39
  91.9 0.1 fusion.38
  92.0 0.1 select_convert_fusion.3
  92.1 16.6 %all_to_all.64 = bf16[32,24,128]{2,1,0:T(8,128)(2,1)S(1)} all-to-all(bf16[32,24,128]{2,1,0:T(8,128)(2,1)S(1)} %broadcast_in_dim.146), channel_id=1, replica_groups={{0,1,2,3,4,5,6,7,8,9,10,11,12,13,14,15,16,17,18,19,20,21,22,23,24,25,26..., dimensions={0} | all-to-all | bytes 393216 | tf_op jit(solution)/shard_map/all_to_all | solution.py:37
  108.8 0.2 fusion.19
  109.0 0.2 fusion.6
  109.3 17.4 %all_to_all.65 = bf16[16,48,128]{2,1,0:T(8,128)(2,1)S(1)} all-to-all(bf16[16,48,128]{2,1,0:T(8,128)(2,1)S(1)} %pad_maximum_fusion.7), channel_id=1, replica_groups={{0,32,64,96,128,160,192,224,256,288,320,352,384,416,448,480},{16,48,80,..., dimensions={0} | all-to-all | bytes 393216 | tf_op jit(solution)/shard_map/all_to_all | solution.py:40
  126.8 0.1 select_convert_fusion.2
  126.9 0.1 pad_maximum_fusion.1
  127.0 21.4 %all_to_all.66 = bf16[32,24,512]{2,1,0:T(8,128)(2,1)S(1)} all-to-all(bf16[32,24,512]{2,1,0:T(8,128)(2,1)S(1)} %pad_maximum_fusion.1), channel_id=1, replica_groups={{0,1,2,3,4,5,6,7,8,9,10,11,12,13,14,15,16,17,18,19,20,21,22,23,24,25,26..., dimensions={0} | all-to-all | bytes 1572864 | tf_op jit(solution)/shard_map/all_to_all | solution.py:37
  148.5 0.2 fusion.23
  148.7 0.2 fusion.21
  148.9 0.2 fusion.3
  149.1 0.2 fusion.7
  149.3 17.4 %all_to_all.67 = bf16[16,48,128]{2,1,0:T(8,128)(2,1)S(1)} all-to-all(bf16[16,48,128]{2,1,0:T(8,128)(2,1)S(1)} %pad_maximum_fusion.8), channel_id=1, replica_groups={{0,32,64,96,128,160,192,224,256,288,320,352,384,416,448,480},{16,48,80,..., dimensions={0} | all-to-all | bytes 393216 | tf_op jit(solution)/shard_map/all_to_all | solution.py:40
  166.8 0.1 select_convert_fusion
  166.9 16.7 %all_to_all.68 = bf16[32,24,128]{2,1,0:T(8,128)(2,1)S(1)} all-to-all(bf16[32,24,128]{2,1,0:T(8,128)(2,1)S(1)} %bitcast.107), channel_id=1, replica_groups={{0,1,2,3,4,5,6,7,8,9,10,11,12,13,14,15,16,17,18,19,20,21,22,23,24,25,26..., dimensions={0} | all-to-all | bytes 393216 | tf_op jit(solution)/shard_map/all_to_all | solution.py:37
  183.7 0.3 fusion.9
  184.1 0.4 fusion
  184.5 0.2 copy.22
  184.7 2.5 %collective-permute-start = (bf16[8,80,128]{2,1,0:T(8,128)(2,1)S(1)}, bf16[8,80,128]{2,1,0:T(8,128)(2,1)S(1)}, u32[]{:S(2)}, u32[]{:S(2)}) collective-permute-start(bf16[8,80,128]{2,1,0:T(8,128)(2,1)S(1)} %pad_maximum_fusion.12), channel_id=1, source_target_pairs={{0,16},{16,0},{32,48},{48,32},{64,80},{80,64},{96,112},{112,96},{1... | collective-permute-start | bytes 491528 | tf_op jit(solution)/shard_map/ppermute | solution.py:138
  187.2 1.0 collective-permute-done
  188.3 12.0 %all_to_all.69 = bf16[8,80,128]{2,1,0:T(8,128)(2,1)S(1)} all-to-all(bf16[8,80,128]{2,1,0:T(8,128)(2,1)S(1)} %pad_maximum_fusion.13), channel_id=1, replica_groups={{128,0,32,64,96,160,192,224},{144,16,48,80,112,176,208,240},{384,256,28..., dimensions={0} | all-to-all | bytes 327680 | tf_op jit(solution)/shard_map/all_to_all | solution.py:40
  200.3 0.1 fusion.37
  200.4 13.0 %all_to_all.70 = bf16[8,2,40,128]{3,2,1,0:T(8,128)(2,1)S(1)} all-to-all(bf16[8,2,40,128]{3,2,1,0:T(8,128)(2,1)S(1)} %broadcast_in_dim.155), channel_id=1, replica_groups={{128,0,32,64,96,160,192,224},{144,16,48,80,112,176,208,240},{384,256,28..., dimensions={0} | all-to-all | bytes 327680 | tf_op jit(solution)/shard_map/all_to_all | solution.py:40
  213.5 6.4 %collective-permute-start.1 = (bf16[2,320,128]{2,1,0:T(8,128)(2,1)S(1)}, bf16[2,320,128]{2,1,0:T(8,128)(2,1)S(1)}, u32[]{:S(2)}, u32[]{:S(2)}) collective-permute-start(bf16[2,320,128]{2,1,0:T(8,128)(2,1)S(1)} %bitcast.109), channel_id=1, source_target_pairs={{0,16},{16,0},{32,48},{48,32},{64,80},{80,64},{96,112},{112,96},{1... | collective-permute-start | bytes 491528 | tf_op jit(solution)/shard_map/ppermute | solution.py:147
  219.9 1.0 collective-permute-done.1
  220.9 0.8 fusion.17
  (72 shorter events, 1.1 us)
Async XLA Ops:
  0.0 56.1 %copy-start = (bf16[1,640,640]{2,1,0:T(8,128)(2,1)S(1)}, bf16[1,640,640]{2,1,0:T(8,128)(2,1)}, u32[]{:S(2)}) copy-start(bf16[1,640,640]{2,1,0:T(8,128)(2,1)} %param.9) | copy-start | bytes 2457604
  0.0 12.3 %copy-start.4 = (s32[2,32]{1,0:T(2,128)S(1)}, s32[2,32]{1,0:T(2,128)}, u32[]{:S(2)}) copy-start(s32[2,32]{1,0:T(2,128)} %param.7) | copy-start | bytes 772
  0.0 15.0 %slice-start = ((bf16[1,640,960]{1,2,0:T(8,128)(2,1)}), bf16[1,640,320]{1,2,0:T(8,128)(2,1)S(1)}, s32[]{:S(2)}) async-start(bf16[1,640,960]{1,2,0:T(8,128)(2,1)} %param.8), calls=%async_computation.12 | async-start | bytes 819200 | tf_op jit(solution)/shard_map/slice | solution.py:91
  1.8 18.6 %all-to-all-start = ((bf16[32,24,128]{2,1,0:T(8,128)(2,1)}), bf16[32,24,128]{2,1,0:T(8,128)(2,1)S(1)}, u32[]{:S(2)}, u32[]{:S(2)}) async-start(bf16[32,24,128]{2,1,0:T(8,128)(2,1)} %pad_maximum_fusion.5), calls=%async_computation | async-start | bytes 393216 | tf_op jit(solution)/shard_map/all_to_all | solution.py:37
  15.0 1.0 slice-start.1
  35.8 20.0 %copy-start.1 = (bf16[1,640,960]{1,2,0:T(8,128)(2,1)S(1)}, bf16[1,640,960]{1,2,0:T(8,128)(2,1)}, u32[]{:S(2)}) copy-start(bf16[1,640,960]{1,2,0:T(8,128)(2,1)} %param.8) | copy-start | bytes 3686404
  149.1 34.6 %copy-start.2 = (bf16[1,640,960]{1,2,0:T(8,128)(2,1)S(1)}, bf16[1,640,960]{1,2,0:T(8,128)(2,1)}, u32[]{:S(2)}) copy-start(bf16[1,640,960]{1,2,0:T(8,128)(2,1)} %param.10) | copy-start | bytes 3686404
  166.9 17.2 %copy-start.3 = (bf16[1,640,640]{2,1,0:T(8,128)(2,1)S(1)}, bf16[1,640,640]{2,1,0:T(8,128)(2,1)}, u32[]{:S(2)}) copy-start(bf16[1,640,640]{2,1,0:T(8,128)(2,1)} %param.11) | copy-start | bytes 2457604
  184.7 3.5 %collective-permute-start = (bf16[8,80,128]{2,1,0:T(8,128)(2,1)S(1)}, bf16[8,80,128]{2,1,0:T(8,128)(2,1)S(1)}, u32[]{:S(2)}, u32[]{:S(2)}) collective-permute-start(bf16[8,80,128]{2,1,0:T(8,128)(2,1)S(1)} %pad_maximum_fusion.12), channel_id=1, source_target_pairs={{0,16},{16,0},{32,48},{48,32},{64,80},{80,64},{96,112},{112,96},{1... | collective-permute-start | bytes 491528 | tf_op jit(solution)/shard_map/ppermute | solution.py:138
  213.5 7.4 %collective-permute-start.1 = (bf16[2,320,128]{2,1,0:T(8,128)(2,1)S(1)}, bf16[2,320,128]{2,1,0:T(8,128)(2,1)S(1)}, u32[]{:S(2)}, u32[]{:S(2)}) collective-permute-start(bf16[2,320,128]{2,1,0:T(8,128)(2,1)S(1)} %bitcast.109), channel_id=1, source_target_pairs={{0,16},{16,0},{32,48},{48,32},{64,80},{80,64},{96,112},{112,96},{1... | collective-permute-start | bytes 491528 | tf_op jit(solution)/shard_map/ppermute | solution.py:147

commit v8 on v7

--- a/solution.py
+++ b/solution.py
@@ -26,7 +26,7 @@
     z, core = leaf_id // 2, leaf_id % 2
     node, z8 = z // half, z % half
 
-    plane = [[(2 * k + c) * n_front + f for c in range(2) for f in range(n_front)] for k in range(n_z)]
+    plane = [[(2 * k + c) * n_front + f for c in (1, 0) for f in range(n_front)] for k in range(n_z)]
     z_all = [[2 * k + c for k in range(n_z)] for c in range(2)]
     mid = half // 2
     order = [mid] + [k for k in range(half) if k != mid]
@@ -45,7 +45,8 @@
     def spread(v, n):
         return jnp.broadcast_to(v[None], (n,) + v.shape)
 
-    def by_core(v):
+    def by_core(even, odd):
+        v = jnp.stack([odd, even])
         return jnp.broadcast_to(v[:, None], (2, n_front) + v.shape[1:]).reshape((n_plane,) + v.shape[1:])
 
     def cut(v):
@@ -55,6 +56,21 @@
     def join(v):
         low, high = v[:n_front], v[n_front:, WIN - LO :]
         return jnp.concatenate([low, high], 1).reshape(n_front * PIECE, v.shape[-1])
+
+    def join_second(v):
+        low, high = v[:n_front, :LO], v[n_front:]
+        return jnp.concatenate([low, high], 1).reshape(n_front * PIECE, v.shape[-1])
+
+    def pack(a, b, low):
+        first = jnp.concatenate([a, b[..., :LO, :]], -2)
+        return jnp.where(low, first, jnp.concatenate([a[..., WIN - LO :, :], b], -2))
+
+    def unpack(v, low):
+        return jnp.where(low, v[..., :WIN, :], jnp.concatenate([v[..., : WIN - LO, :], v[..., :LO, :]], -2))
+
+    def unpack_second(v, low):
+        first = jnp.concatenate([v[..., WIN:, :], v[..., LO:WIN, :]], -2)
+        return jnp.where(low, first, v[..., LO:, :])
 
     def fold(v):
         return v[:n_front].astype(f32) + v[n_front:].astype(f32)
@@ -76,61 +92,67 @@
 
     live_a, live_b, live_root = (live[k].reshape(()) * BLK for k in ((0, slice(0, 1)), (0, slice(1, 2)), (1, slice(0, 1))))
     live_node = jnp.where(node == 0, live_a, live_b)
-    here = (front_id * PIECE + core * LO).astype(i32)
+    here = (front_id * PIECE + (1 - core) * LO).astype(i32)
     at_out = (front_id * sep_dev + (core * half + place(z8)) * PIECE).astype(i32)
     kind = lax.iota(i32, 8)
     count = jnp.where(kind == 2, live_a, jnp.where(kind == 3, live_b, jnp.where((kind < 4) | (kind > 6), live_node, live_root)))
     block = jnp.where((kind > 1) & (kind < 5), z.astype(i32), 2 * z8.astype(i32) + ((kind == 1) | (kind == 6)).astype(i32))
     begin = jnp.where(kind == 7, at_out, here + block * sep_dev)
     keep = lax.broadcasted_iota(i32, (8, PIECE), 1) < (count - begin)[:, None]
-    keep = (keep[0:2, :WIN], keep[2, :WIN], keep[3, :WIN], keep[4, :WIN], keep[5:7, :WIN], keep[7])
-    scalars = (keep, core, 1 - core, 2 * z8, place(front_id // 2), core == front_id % 2)
+    keep = tuple(keep[k, :WIN] for k in range(7)) + (keep[7],)
+    scalars = (keep, core, 1 - core, 2 * z8, place(front_id // 2), core == front_id % 2, core == 1)
 
     got = a2a_plane(cut(forcing[0]))
     uinv1 = cut(upper_inv[0, :, w0:])
     extra = jnp.concatenate([cut(lower_inv[0, :, w0:]), uinv1[:, :, head:]], 2)
     got, extra, uinv1, scalars = lax.optimization_barrier((got, extra, uinv1[:, :, :head], scalars))
-    keep, core, other_core, two_z8, source, mine = scalars
+    keep, core, other_core, two_z8, source, mine, low = scalars
 
-    pair = fold(got).astype(bf).reshape(half, 2 * WIN, n_rhs)
+    pair = fold(got).astype(bf).reshape(half, 2, WIN, n_rhs)
+    pair = pack(pair[:, 0], pair[:, 1], low)
     pair = jnp.concatenate([pair[mid : mid + 1], pair[:mid], pair[mid + 1 :]], 0)
-    r0 = total(a2a_leaf(pair, z_half)).reshape(2, WIN, n_rhs)
-    moved = a2a_plane(jnp.concatenate([by_core(masked(r0, keep[0])), extra], 2))
-    rm0 = join(moved[:, :, :n_rhs])
+    r0 = total(a2a_leaf(pair, z_half))
+    rm0 = by_core(masked(unpack(r0, low), keep[0]), masked(unpack_second(r0, low), keep[1]))
+    moved = a2a_plane(jnp.concatenate([rm0, extra], 2))
+    rm0 = moved[:, :, :n_rhs]
+    rm0 = jnp.where(low, join_second(rm0), join(rm0))
 
     c_part = dot(lower_upd[0], rm0).astype(bf)
     y_part = dot(lower_inv[0, :, :w0], rm0).astype(bf)
     parts = fold(a2a_plane(cut(jnp.concatenate([c_part, y_part], 1)))).astype(bf)
 
-    got = a2a_leaf(jnp.concatenate([parts[:, :, :n_rhs], parts[:, :, n_rhs:]], 1), z_all)
-    r1 = masked(-total(got[:, :WIN]), keep[3])
-    y0 = jnp.stack([masked(total(got[:half, WIN:]), keep[1]), masked(total(got[half:, WIN:]), keep[2])])
+    got = a2a_leaf(pack(parts[:, :, :n_rhs], parts[:, :, n_rhs:], low), z_all)
+    sum_a, sum_b = total(got[:half]), total(got[half:])
+    r1 = masked(-unpack(sum_a + sum_b, low), keep[4])
+    y0 = jnp.stack([masked(unpack_second(sum_a, low), keep[2]), masked(unpack_second(sum_b, low), keep[3])])
     y0 = jnp.broadcast_to(y0[:, None], (2, half, WIN, n_rhs)).reshape(n_z, WIN, n_rhs)
     r1, y0 = lax.optimization_barrier((spread(r1, n_plane), y0))
     r1 = join(a2a_plane(r1))
 
     blank = jnp.zeros((n_rhs - tail, n_rhs), bf)
     y1 = sum(
-        dot(panel(moved, h, n_rhs, n_rhs + w1 + tail), jnp.concatenate([r1[h * w1 : (h + 1) * w1], blank], 0))
+        dot(panel(moved, h, n_rhs, n_rhs + w1 + tail), jnp.concatenate([r1[(1 - h) * w1 : (2 - h) * w1], blank], 0))
         for h in range(2)
     )
-    got = a2a_leaf(jnp.concatenate([y1.astype(bf).reshape(n_front, WIN, n_rhs), y0], 1), z_all)
-    y1 = masked(total(got[:, :WIN]), keep[3])
-    y0 = pick(got[:, WIN:], two_z8, 2)
-    got = a2a_plane(jnp.concatenate([spread(y1, n_plane), by_core(y0), uinv1], 2))
+    got = a2a_leaf(pack(y1.astype(bf).reshape(n_front, WIN, n_rhs), y0, low), z_all)
+    y1 = masked(unpack(total(got), low), keep[4])
+    y0 = unpack_second(pick(got, two_z8, 2), low)
+    got = a2a_plane(jnp.concatenate([spread(y1, n_plane), by_core(y0[0], y0[1]), uinv1], 2))
     y1 = join(got[:, :, :n_rhs])
-    y0 = join(got[:, :, n_rhs : 2 * n_rhs])
+    y0 = join_second(got[:, :, n_rhs : 2 * n_rhs])
 
     x1 = 0.0
     for h in range(2):
-        v = y1[h * w1 : (h + 1) * w1]
+        v = y1[(1 - h) * w1 : (2 - h) * w1]
         x1 = x1 + dot(panel(got, h, 2 * n_rhs, 2 * n_rhs + head), v[:head])
         x1 = x1 + dot(panel(moved, h, n_rhs + head, n_rhs + head + n_rhs), jnp.concatenate([blank, v[head:]], 0))
-    x1 = x1.astype(bf).reshape(half, 2 * WIN, n_rhs)
+    x1 = x1.astype(bf).reshape(half, 2, WIN, n_rhs)
+    x1 = pack(x1[:, 0], x1[:, 1], low)
     x1, y0 = lax.optimization_barrier((jnp.concatenate([x1, x1], 0), y0))
-    x1 = masked(total(a2a_leaf(x1, z_all)).reshape(2, WIN, n_rhs), keep[4])
-    x1, y0 = lax.optimization_barrier((a2a_plane(by_core(x1)), y0))
-    x1 = join(x1)
+    x1 = total(a2a_leaf(x1, z_all))
+    x1 = by_core(masked(unpack(x1, low), keep[5]), masked(unpack_second(x1, low), keep[6]))
+    x1, y0 = lax.optimization_barrier((a2a_plane(x1), y0))
+    x1 = jnp.where(low, join_second(x1), join(x1))
 
     term = (dot(upper_inv[0, :, :w0], y0) - dot(upper_upd[0], x1)).reshape(2, half, PIECE, n_rhs)
     x1 = x1.reshape(2, half, PIECE, n_rhs)
@@ -140,7 +162,7 @@
     own = jnp.where(mine, pick(x1, core, 1)[0], away[:, PIECE:])
     got = a2a_leaf(jnp.concatenate([term, own], 1), z_half)
 
-    x0 = masked(total(got[:, :PIECE]), keep[5])
+    x0 = masked(total(got[:, :PIECE]), keep[7])
     x1 = pick(got[:, PIECE:], source, 1)[0]
     both = a2a_leaf(spread(jnp.stack([x0, x1]), half), z_half)
     both = jnp.swapaxes(both, 0, 1).reshape(2, half * PIECE, n_rhs)

time: 222 us -> 218 us (0.982)
  blocking collectives: 184 us -> 147 us
  waiting for transfers between devices: 5.78 us -> 25.8 us
  starting transfers between devices: 19.3 us -> 29.9 us
    all_to_all x5 -> x4, blocking collectives: 88.3 us -> 67.9 us  [a2a_plane(): return lax.all_to_all(v, ('leaf', 'front'), 0, 0, axis_index_groups=plane)]
    all_to_all x6 -> x5, blocking collectives: 96.1 us -> 79.2 us  [a2a_leaf(): return lax.all_to_all(v, 'leaf', 0, 0, axis_index_groups=groups)]
    all_to_all x0 -> x1, waiting for transfers between devices: none -> 12.2 us  [a2a_leaf(): return lax.all_to_all(v, 'leaf', 0, 0, axis_index_groups=groups)]
    all_to_all x1 -> x2, waiting for transfers between devices: 3.78 us -> 11.5 us  [a2a_plane(): return lax.all_to_all(v, ('leaf', 'front'), 0, 0, axis_index_groups=plane)]
    all_to_all x1 -> x2, starting transfers between devices: 10.5 us -> 16.6 us  [a2a_plane(): return lax.all_to_all(v, ('leaf', 'front'), 0, 0, axis_index_groups=plane)]
    all_to_all x0 -> x1, starting transfers between devices: none -> 4.47 us  [a2a_leaf(): return lax.all_to_all(v, 'leaf', 0, 0, axis_index_groups=groups)]
  transfers between devices with their start and end apart: 3 -> 5, of which waited for: 3 -> 5; matrix products, arithmetic and copies ran while one was open for 1% -> 1% of each run, Pallas kernels for 0% -> 0%
where the time goes in v8:
time: 218 us
  blocking collectives  147 us (67%)
  starting transfers between devices  29.9 us (14%)
  waiting for transfers between devices  25.8 us (12%)
  local copies, waits for them, and re-layouts  5.42 us (2%)
  other arithmetic  3.83 us (2%)
  between operations  2.72 us (1%)
  matrix products  2.68 us (1%)
    all_to_all x5, blocking collectives, a2a_leaf(): return lax.all_to_all(v, 'leaf', 0, 0, axis_index_groups=groups)  79.2 us
    all_to_all x4, blocking collectives, a2a_plane(): return lax.all_to_all(v, ('leaf', 'front'), 0, 0, axis_index_groups=plane)  67.9 us
    all_to_all x2, starting transfers between devices, a2a_plane(): return lax.all_to_all(v, ('leaf', 'front'), 0, 0, axis_index_groups=plane)  16.6 us
    all_to_all x1, waiting for transfers between devices, a2a_leaf(): return lax.all_to_all(v, 'leaf', 0, 0, axis_index_groups=groups)  12.2 us
    all_to_all x2, waiting for transfers between devices, a2a_plane(): return lax.all_to_all(v, ('leaf', 'front'), 0, 0, axis_index_groups=plane)  11.5 us
    ppermute x1, starting transfers between devices, body(): other = lax.ppermute(both, 'leaf', swap)  6.36 us
    all_to_all x1, starting transfers between devices, a2a_leaf(): return lax.all_to_all(v, 'leaf', 0, 0, axis_index_groups=groups)  4.47 us
  transfers between devices with their start and end apart: 5, of which 5 were waited for; matrix products, arithmetic and copies ran while one was open for 1% of the time, Pallas kernels for 0%

profile of v8, /device:TPU:1, one launch (start us, length us, event | category | flops | bytes accessed | tf_op | source)
XLA Modules:
  0.0 217.5 jit_solution(10851415783214918044)
XLA Ops:
  0.0 1.1 fusion.78
  1.1 0.7 pad_maximum_fusion.5
  1.8 8.5 %all-to-all-start = ((bf16[32,24,128]{2,1,0:T(8,128)(2,1)}), bf16[32,24,128]{2,1,0:T(8,128)(2,1)S(1)}, u32[]{:S(2)}, u32[]{:S(2)}) async-start(bf16[32,24,128]{2,1,0:T(8,128)(2,1)} %pad_maximum_fusion.5), calls=%async_computation | async-start | bytes 393216 | tf_op jit(solution)/shard_map/all_to_all | solution.py:37
  10.4 0.6 fusion.84
  13.0 0.3 copy.38
  13.2 0.7 slice-done.1
  13.9 0.3 copy.39
  14.2 0.1 fusion.71
  14.4 0.1 fusion.16
  14.6 3.7 %all-to-all-done = bf16[32,24,128]{2,1,0:T(8,128)(2,1)S(1)} async-done(((bf16[32,24,128]{2,1,0:T(8,128)(2,1)}), bf16[32,24,128]{2,1,0:T(8,128)(2,1)S(1)}, u32[]{:S(2)}, u32[]{:S(2)}) %all-to-all-start) | async-done | bytes 196640 | tf_op jit(solution)/shard_map/all_to_all | solution.py:37
  18.4 16.8 %all_to_all.60 = bf16[8,40,128]{2,1,0:T(8,128)(2,1)S(1)} all-to-all(bf16[8,40,128]{2,1,0:T(8,128)(2,1)S(1)} %pad_maximum_fusion.12), channel_id=1, replica_groups={{128,0,32,64,96,160,192,224},{144,16,48,80,112,176,208,240},{384,256,28..., dimensions={0} | all-to-all | bytes 163840 | tf_op jit(solution)/shard_map/all_to_all | solution.py:40
  35.2 0.1 fusion.55
  35.4 18.5 %all_to_all.61 = bf16[32,24,512]{2,1,0:T(8,128)(2,1)S(1)} all-to-all(bf16[32,24,512]{2,1,0:T(8,128)(2,1)S(1)} %pad_maximum_fusion), channel_id=1, replica_groups={{16,17,18,19,20,21,22,23,24,25,26,27,28,29,30,31,0,1,2,3,4,5,6,7,8,9,10..., dimensions={0} | all-to-all | bytes 1572864 | tf_op jit(solution)/shard_map/all_to_all | solution.py:37
  54.1 0.3 fusion.5
  54.5 0.4 fusion.4
  54.9 0.2 copy.32
  55.2 13.4 %all_to_all.62 = bf16[32,24,256]{2,1,0:T(8,128)(2,1)S(1)} all-to-all(bf16[32,24,256]{2,1,0:T(8,128)(2,1)S(1)} %pad_maximum_fusion.3), channel_id=1, replica_groups={{16,17,18,19,20,21,22,23,24,25,26,27,28,29,30,31,0,1,2,3,4,5,6,7,8,9,10..., dimensions={0} | all-to-all | bytes 786432 | tf_op jit(solution)/shard_map/all_to_all | solution.py:37
  68.8 21.0 %all_to_all.63 = bf16[16,40,128]{2,1,0:T(8,128)(2,1)S(1)} all-to-all(bf16[16,40,128]{2,1,0:T(8,128)(2,1)S(1)} %maximum_select_fusion.2), channel_id=1, replica_groups={{0,32,64,96,128,160,192,224,256,288,320,352,384,416,448,480},{16,48,80,..., dimensions={0} | all-to-all | bytes 327680 | tf_op jit(solution)/shard_map/all_to_all | solution.py:40
  89.9 0.1 fusion.57
  90.0 0.1 fusion.50
  90.1 0.7 broadcast_in_dim.152
  90.8 8.1 %all-to-all-start.5 = ((bf16[32,24,128]{2,1,0:T(8,128)(2,1)}), bf16[32,24,128]{2,1,0:T(8,128)(2,1)S(1)}, u32[]{:S(2)}, u32[]{:S(2)}) async-start(bf16[32,24,128]{2,1,0:T(8,128)(2,1)} %broadcast_in_dim.152), calls=%async_computation.5 | async-start | bytes 393216 | tf_op jit(solution)/shard_map/all_to_all | solution.py:37
  98.9 7.9 %all-to-all-done.5 = bf16[32,24,128]{2,1,0:T(8,128)(2,1)S(1)} async-done(((bf16[32,24,128]{2,1,0:T(8,128)(2,1)}), bf16[32,24,128]{2,1,0:T(8,128)(2,1)S(1)}, u32[]{:S(2)}, u32[]{:S(2)}) %all-to-all-start.5) | async-done | bytes 196640 | tf_op jit(solution)/shard_map/all_to_all | solution.py:37
  106.8 0.2 fusion.19
  107.1 0.2 fusion.6
  107.3 0.7 maximum_select_fusion.3
  108.1 4.5 %all-to-all-start.6 = ((bf16[16,40,128]{2,1,0:T(8,128)(2,1)}), bf16[16,40,128]{2,1,0:T(8,128)(2,1)S(1)}, u32[]{:S(2)}, u32[]{:S(2)}) async-start(bf16[16,40,128]{2,1,0:T(8,128)(2,1)} %maximum_select_fusion.3), calls=%async_computation.6 | async-start | bytes 327680 | tf_op jit(solution)/shard_map/all_to_all | solution.py:40
  112.5 12.2 %all-to-all-done.6 = bf16[16,40,128]{2,1,0:T(8,128)(2,1)S(1)} async-done(((bf16[16,40,128]{2,1,0:T(8,128)(2,1)}), bf16[16,40,128]{2,1,0:T(8,128)(2,1)S(1)}, u32[]{:S(2)}, u32[]{:S(2)}) %all-to-all-start.6) | async-done | bytes 163872 | tf_op jit(solution)/shard_map/all_to_all | solution.py:40
  124.9 0.1 fusion.43
  125.1 20.5 %all_to_all.64 = bf16[32,24,512]{2,1,0:T(8,128)(2,1)S(1)} all-to-all(bf16[32,24,512]{2,1,0:T(8,128)(2,1)S(1)} %pad_maximum_fusion.1), channel_id=1, replica_groups={{16,17,18,19,20,21,22,23,24,25,26,27,28,29,30,31,0,1,2,3,4,5,6,7,8,9,10..., dimensions={0} | all-to-all | bytes 1572864 | tf_op jit(solution)/shard_map/all_to_all | solution.py:37
  145.8 0.2 fusion.23
  146.0 0.2 fusion.21
  146.2 0.2 fusion.3
  146.3 0.2 fusion.7
  146.7 16.6 %all_to_all.65 = bf16[16,40,128]{2,1,0:T(8,128)(2,1)S(1)} all-to-all(bf16[16,40,128]{2,1,0:T(8,128)(2,1)S(1)} %pad_maximum_fusion.6), channel_id=1, replica_groups={{0,32,64,96,128,160,192,224,256,288,320,352,384,416,448,480},{16,48,80,..., dimensions={0} | all-to-all | bytes 327680 | tf_op jit(solution)/shard_map/all_to_all | solution.py:40
  163.3 0.1 fusion.59
  163.4 15.5 %all_to_all.66 = bf16[32,24,128]{2,1,0:T(8,128)(2,1)S(1)} all-to-all(bf16[32,24,128]{2,1,0:T(8,128)(2,1)S(1)} %bitcast.129), channel_id=1, replica_groups={{16,17,18,19,20,21,22,23,24,25,26,27,28,29,30,31,0,1,2,3,4,5,6,7,8,9,10..., dimensions={0} | all-to-all | bytes 393216 | tf_op jit(solution)/shard_map/all_to_all | solution.py:37
  178.9 0.3 fusion.9
  179.3 0.7 copy-done.3
  180.0 0.4 fusion
  180.4 0.2 copy.35
  180.7 2.5 %collective-permute-start = (bf16[8,80,128]{2,1,0:T(8,128)(2,1)S(1)}, bf16[8,80,128]{2,1,0:T(8,128)(2,1)S(1)}, u32[]{:S(2)}, u32[]{:S(2)}) collective-permute-start(bf16[8,80,128]{2,1,0:T(8,128)(2,1)S(1)} %pad_maximum_fusion.8), channel_id=1, source_target_pairs={{0,16},{16,0},{32,48},{48,32},{64,80},{80,64},{96,112},{112,96},{1... | collective-permute-start | bytes 491528 | tf_op jit(solution)/shard_map/ppermute | solution.py:160
  183.2 1.0 collective-permute-done
  184.3 11.9 %all_to_all.67 = bf16[8,80,128]{2,1,0:T(8,128)(2,1)S(1)} all-to-all(bf16[8,80,128]{2,1,0:T(8,128)(2,1)S(1)} %pad_maximum_fusion.9), channel_id=1, replica_groups={{128,0,32,64,96,160,192,224},{144,16,48,80,112,176,208,240},{384,256,28..., dimensions={0} | all-to-all | bytes 327680 | tf_op jit(solution)/shard_map/all_to_all | solution.py:40
  196.3 13.0 %all_to_all.68 = bf16[8,2,40,128]{3,2,1,0:T(8,128)(2,1)S(1)} all-to-all(bf16[8,2,40,128]{3,2,1,0:T(8,128)(2,1)S(1)} %broadcast_in_dim.161), channel_id=1, replica_groups={{128,0,32,64,96,160,192,224},{144,16,48,80,112,176,208,240},{384,256,28..., dimensions={0} | all-to-all | bytes 327680 | tf_op jit(solution)/shard_map/all_to_all | solution.py:40
  209.3 6.4 %collective-permute-start.1 = (bf16[2,320,128]{2,1,0:T(8,128)(2,1)S(1)}, bf16[2,320,128]{2,1,0:T(8,128)(2,1)S(1)}, u32[]{:S(2)}, u32[]{:S(2)}) collective-permute-start(bf16[2,320,128]{2,1,0:T(8,128)(2,1)S(1)} %bitcast.135), channel_id=1, source_target_pairs={{0,16},{16,0},{32,48},{48,32},{64,80},{80,64},{96,112},{112,96},{1... | collective-permute-start | bytes 491528 | tf_op jit(solution)/shard_map/ppermute | solution.py:169
  215.7 1.0 collective-permute-done.1
  216.7 0.8 fusion.17
  (101 shorter events, 1.8 us)
Async XLA Ops:
  0.0 54.5 %copy-start = (bf16[1,640,640]{2,1,0:T(8,128)(2,1)S(1)}, bf16[1,640,640]{2,1,0:T(8,128)(2,1)}, u32[]{:S(2)}) copy-start(bf16[1,640,640]{2,1,0:T(8,128)(2,1)} %param.9) | copy-start | bytes 2457604
  0.0 10.4 %copy-start.4 = (s32[2,32]{1,0:T(2,128)S(1)}, s32[2,32]{1,0:T(2,128)}, u32[]{:S(2)}) copy-start(s32[2,32]{1,0:T(2,128)} %param.7) | copy-start | bytes 772
  0.0 12.9 %slice-start = ((bf16[1,640,960]{1,2,0:T(8,128)(2,1)}), bf16[1,640,320]{1,2,0:T(8,128)(2,1)S(1)}, s32[]{:S(2)}) async-start(bf16[1,640,960]{1,2,0:T(8,128)(2,1)} %param.8), calls=%async_computation.12 | async-start | bytes 819200 | tf_op jit(solution)/shard_map/slice | solution.py:107
  1.8 16.4 %all-to-all-start = ((bf16[32,24,128]{2,1,0:T(8,128)(2,1)}), bf16[32,24,128]{2,1,0:T(8,128)(2,1)S(1)}, u32[]{:S(2)}, u32[]{:S(2)}) async-start(bf16[32,24,128]{2,1,0:T(8,128)(2,1)} %pad_maximum_fusion.5), calls=%async_computation | async-start | bytes 393216 | tf_op jit(solution)/shard_map/all_to_all | solution.py:37
  12.9 1.0 slice-start.1
  35.4 18.7 %copy-start.1 = (bf16[1,640,960]{1,2,0:T(8,128)(2,1)S(1)}, bf16[1,640,960]{1,2,0:T(8,128)(2,1)}, u32[]{:S(2)}) copy-start(bf16[1,640,960]{1,2,0:T(8,128)(2,1)} %param.8) | copy-start | bytes 3686404
  90.8 16.0 %all-to-all-start.5 = ((bf16[32,24,128]{2,1,0:T(8,128)(2,1)}), bf16[32,24,128]{2,1,0:T(8,128)(2,1)S(1)}, u32[]{:S(2)}, u32[]{:S(2)}) async-start(bf16[32,24,128]{2,1,0:T(8,128)(2,1)} %broadcast_in_dim.152), calls=%async_computation.5 | async-start | bytes 393216 | tf_op jit(solution)/shard_map/all_to_all | solution.py:37
  108.1 16.7 %all-to-all-start.6 = ((bf16[16,40,128]{2,1,0:T(8,128)(2,1)}), bf16[16,40,128]{2,1,0:T(8,128)(2,1)S(1)}, u32[]{:S(2)}, u32[]{:S(2)}) async-start(bf16[16,40,128]{2,1,0:T(8,128)(2,1)} %maximum_select_fusion.3), calls=%async_computation.6 | async-start | bytes 327680 | tf_op jit(solution)/shard_map/all_to_all | solution.py:40
  146.6 32.3 %copy-start.2 = (bf16[1,640,960]{1,2,0:T(8,128)(2,1)S(1)}, bf16[1,640,960]{1,2,0:T(8,128)(2,1)}, u32[]{:S(2)}) copy-start(bf16[1,640,960]{1,2,0:T(8,128)(2,1)} %param.10) | copy-start | bytes 3686404
  178.9 1.1 copy-start.3
  180.7 3.5 %collective-permute-start = (bf16[8,80,128]{2,1,0:T(8,128)(2,1)S(1)}, bf16[8,80,128]{2,1,0:T(8,128)(2,1)S(1)}, u32[]{:S(2)}, u32[]{:S(2)}) collective-permute-start(bf16[8,80,128]{2,1,0:T(8,128)(2,1)S(1)} %pad_maximum_fusion.8), channel_id=1, source_target_pairs={{0,16},{16,0},{32,48},{48,32},{64,80},{80,64},{96,112},{112,96},{1... | collective-permute-start | bytes 491528 | tf_op jit(solution)/shard_map/ppermute | solution.py:160
  209.3 7.4 %collective-permute-start.1 = (bf16[2,320,128]{2,1,0:T(8,128)(2,1)S(1)}, bf16[2,320,128]{2,1,0:T(8,128)(2,1)S(1)}, u32[]{:S(2)}, u32[]{:S(2)}) collective-permute-start(bf16[2,320,128]{2,1,0:T(8,128)(2,1)S(1)} %bitcast.135), channel_id=1, source_target_pairs={{0,16},{16,0},{32,48},{48,32},{64,80},{80,64},{96,112},{112,96},{1... | collective-permute-start | bytes 491528 | tf_op jit(solution)/shard_map/ppermute | solution.py:169

commit v9 on v8

--- a/solution.py
+++ b/solution.py
@@ -1,5 +1,6 @@
 import jax
 import jax.numpy as jnp
+import numpy as np
 from jax import lax
 from jax.sharding import PartitionSpec as P
 
@@ -26,11 +27,14 @@
     z, core = leaf_id // 2, leaf_id % 2
     node, z8 = z // half, z % half
 
-    plane = [[(2 * k + c) * n_front + f for c in (1, 0) for f in range(n_front)] for k in range(n_z)]
-    z_all = [[2 * k + c for k in range(n_z)] for c in range(2)]
-    mid = half // 2
-    order = [mid] + [k for k in range(half) if k != mid]
-    z_half = [[2 * (h * half + k) + c for k in order] for h in range(2) for c in range(2)]
+    shift = half - 2
+    turn = shift // 2
+    fronts = [(k + shift) % n_front for k in range(n_front)]
+    planes = [(k + shift) % n_z for k in range(n_z)]
+    halves = [(k + turn) % half for k in range(half)]
+    plane = [[(2 * k + c) * n_front + f for c in (1, 0) for f in fronts] for k in range(n_z)]
+    z_all = [[2 * k + c for k in planes] for c in range(2)]
+    z_half = [[2 * (h * half + k) + c for k in halves] for h in range(2) for c in range(2)]
     swap = [(k, k ^ 1) for k in range(n_leaf)]
 
     def a2a_plane(v):
@@ -40,7 +44,7 @@
         return lax.all_to_all(v, "leaf", 0, 0, axis_index_groups=groups)
 
     def place(k):
-        return jnp.where(k == mid, u32(0), jnp.where(k < mid, k + 1, k))
+        return (k + (half - turn)) % half
 
     def spread(v, n):
         return jnp.broadcast_to(v[None], (n,) + v.shape)
@@ -61,6 +65,16 @@
         low, high = v[:n_front, :LO], v[n_front:]
         return jnp.concatenate([low, high], 1).reshape(n_front * PIECE, v.shape[-1])
 
+    def lift(a, low):
+        blank = jnp.zeros(a.shape[:-2] + (LO, n_rhs), a.dtype)
+        first = jnp.concatenate([a, blank], -2)
+        return jnp.where(low, first, jnp.concatenate([a[..., WIN - LO :, :], blank, blank[..., : WIN - LO, :]], -2))
+
+    def lift_second(b, low):
+        blank = jnp.zeros(b.shape[:-2] + (LO, n_rhs), b.dtype)
+        first = jnp.concatenate([blank, blank[..., : WIN - LO, :], b[..., :LO, :]], -2)
+        return jnp.where(low, first, jnp.concatenate([blank, b], -2))
+
     def pack(a, b, low):
         first = jnp.concatenate([a, b[..., :LO, :]], -2)
         return jnp.where(low, first, jnp.concatenate([a[..., WIN - LO :, :], b], -2))
@@ -79,7 +93,7 @@
         return jnp.sum(v.astype(f32), 0)
 
     def pick(v, k, n):
-        return lax.dynamic_slice(v, (k,) + (u32(0),) * (v.ndim - 1), (n,) + v.shape[1:])
+        return lax.dynamic_slice(v, (k,) + (np.uint32(0),) * (v.ndim - 1), (n,) + v.shape[1:])
 
     def masked(v, keep):
         return jnp.where(keep[..., None], v, 0.0).astype(bf)
@@ -92,7 +106,7 @@
 
     live_a, live_b, live_root = (live[k].reshape(()) * BLK for k in ((0, slice(0, 1)), (0, slice(1, 2)), (1, slice(0, 1))))
     live_node = jnp.where(node == 0, live_a, live_b)
-    here = (front_id * PIECE + (1 - core) * LO).astype(i32)
+    here = ((front_id + (n_front - shift)) % n_front * PIECE + (1 - core) * LO).astype(i32)
     at_out = (front_id * sep_dev + (core * half + place(z8)) * PIECE).astype(i32)
     kind = lax.iota(i32, 8)
     count = jnp.where(kind == 2, live_a, jnp.where(kind == 3, live_b, jnp.where((kind < 4) | (kind > 6), live_node, live_root)))
@@ -100,7 +114,7 @@
     begin = jnp.where(kind == 7, at_out, here + block * sep_dev)
     keep = lax.broadcasted_iota(i32, (8, PIECE), 1) < (count - begin)[:, None]
     keep = tuple(keep[k, :WIN] for k in range(7)) + (keep[7],)
-    scalars = (keep, core, 1 - core, 2 * z8, place(front_id // 2), core == front_id % 2, core == 1)
+    scalars = (keep, core, 1 - core, (2 * z8 + (n_z - shift)) % n_z, place(front_id // 2), core == front_id % 2, core == 1)
 
     got = a2a_plane(cut(forcing[0]))
     uinv1 = cut(upper_inv[0, :, w0:])
@@ -110,7 +124,6 @@
 
     pair = fold(got).astype(bf).reshape(half, 2, WIN, n_rhs)
     pair = pack(pair[:, 0], pair[:, 1], low)
-    pair = jnp.concatenate([pair[mid : mid + 1], pair[:mid], pair[mid + 1 :]], 0)
     r0 = total(a2a_leaf(pair, z_half))
     rm0 = by_core(masked(unpack(r0, low), keep[0]), masked(unpack_second(r0, low), keep[1]))
     moved = a2a_plane(jnp.concatenate([rm0, extra], 2))
@@ -122,11 +135,12 @@
     parts = fold(a2a_plane(cut(jnp.concatenate([c_part, y_part], 1)))).astype(bf)
 
     got = a2a_leaf(pack(parts[:, :, :n_rhs], parts[:, :, n_rhs:], low), z_all)
-    sum_a, sum_b = total(got[:half]), total(got[half:])
+    edge = half - shift
+    sum_a, sum_b = total(got[:edge]) + total(got[edge + half :]), total(got[edge : edge + half])
     r1 = masked(-unpack(sum_a + sum_b, low), keep[4])
-    y0 = jnp.stack([masked(unpack_second(sum_a, low), keep[2]), masked(unpack_second(sum_b, low), keep[3])])
-    y0 = jnp.broadcast_to(y0[:, None], (2, half, WIN, n_rhs)).reshape(n_z, WIN, n_rhs)
-    r1, y0 = lax.optimization_barrier((spread(r1, n_plane), y0))
+    y0_a, y0_b = masked(unpack_second(sum_a, low), keep[2]), masked(unpack_second(sum_b, low), keep[3])
+    y0 = jnp.concatenate([spread(y0_a, edge), spread(y0_b, half), spread(y0_a, shift)], 0)
+    r1, y0 = lax.optimization_barrier((spread(r1, n_plane), lift_second(y0, low)))
     r1 = join(a2a_plane(r1))
 
     blank = jnp.zeros((n_rhs - tail, n_rhs), bf)
@@ -134,9 +148,9 @@
         dot(panel(moved, h, n_rhs, n_rhs + w1 + tail), jnp.concatenate([r1[(1 - h) * w1 : (2 - h) * w1], blank], 0))
         for h in range(2)
     )
-    got = a2a_leaf(pack(y1.astype(bf).reshape(n_front, WIN, n_rhs), y0, low), z_all)
+    got = a2a_leaf(lift(y1.astype(bf).reshape(n_front, WIN, n_rhs), low) + y0, z_all)
     y1 = masked(unpack(total(got), low), keep[4])
-    y0 = unpack_second(pick(got, two_z8, 2), low)
+    y0 = unpack_second(lax.optimization_barrier(pick(got, two_z8, 2)), low)
     got = a2a_plane(jnp.concatenate([spread(y1, n_plane), by_core(y0[0], y0[1]), uinv1], 2))
     y1 = join(got[:, :, :n_rhs])
     y0 = join_second(got[:, :, n_rhs : 2 * n_rhs])
@@ -148,7 +162,7 @@
         x1 = x1 + dot(panel(moved, h, n_rhs + head, n_rhs + head + n_rhs), jnp.concatenate([blank, v[head:]], 0))
     x1 = x1.astype(bf).reshape(half, 2, WIN, n_rhs)
     x1 = pack(x1[:, 0], x1[:, 1], low)
-    x1, y0 = lax.optimization_barrier((jnp.concatenate([x1, x1], 0), y0))
+    x1, y0 = lax.optimization_barrier((jnp.concatenate([x1[turn:], x1, x1[:turn]], 0), y0))
     x1 = total(a2a_leaf(x1, z_all))
     x1 = by_core(masked(unpack(x1, low), keep[5]), masked(unpack_second(x1, low), keep[6]))
     x1, y0 = lax.optimization_barrier((a2a_plane(x1), y0))

time: 218 us -> 214 us (0.982)
  blocking collectives: 147 us -> 176 us
  waiting for transfers between devices: 25.8 us -> 3.23 us
  starting transfers between devices: 29.9 us -> 20.9 us
    all_to_all x5 -> x6, blocking collectives: 79.2 us -> 99 us  [a2a_leaf(): return lax.all_to_all(v, 'leaf', 0, 0, axis_index_groups=groups)]
    all_to_all x1 -> x0, waiting for transfers between devices: 12.2 us -> none  [a2a_leaf(): return lax.all_to_all(v, 'leaf', 0, 0, axis_index_groups=groups)]
    all_to_all x2 -> x1, waiting for transfers between devices: 11.5 us -> 1.22 us  [a2a_plane(): return lax.all_to_all(v, ('leaf', 'front'), 0, 0, axis_index_groups=plane)]
    all_to_all x4 -> x5, blocking collectives: 67.9 us -> 77 us  [a2a_plane(): return lax.all_to_all(v, ('leaf', 'front'), 0, 0, axis_index_groups=plane)]
    all_to_all x2 -> x1, starting transfers between devices: 16.6 us -> 12.1 us  [a2a_plane(): return lax.all_to_all(v, ('leaf', 'front'), 0, 0, axis_index_groups=plane)]
    all_to_all x1 -> x0, starting transfers between devices: 4.47 us -> none  [a2a_leaf(): return lax.all_to_all(v, 'leaf', 0, 0, axis_index_groups=groups)]
  transfers between devices with their start and end apart: 5 -> 3, of which waited for: 5 -> 3; matrix products, arithmetic and copies ran while one was open for 1% -> 1% of each run, Pallas kernels for 0% -> 0%
where the time goes in v9:
time: 214 us
  blocking collectives  176 us (82%)
  starting transfers between devices  20.9 us (10%)
  local copies, waits for them, and re-layouts  4.82 us (2%)
  other arithmetic  3.24 us (2%)
  waiting for transfers between devices  3.23 us (2%)
  between operations  2.68 us (1%)
  matrix products  2.67 us (1%)
    all_to_all x6, blocking collectives, a2a_leaf(): return lax.all_to_all(v, 'leaf', 0, 0, axis_index_groups=groups)  99 us
    all_to_all x5, blocking collectives, a2a_plane(): return lax.all_to_all(v, ('leaf', 'front'), 0, 0, axis_index_groups=plane)  77 us
    all_to_all x1, starting transfers between devices, a2a_plane(): return lax.all_to_all(v, ('leaf', 'front'), 0, 0, axis_index_groups=plane)  12.1 us
    ppermute x1, starting transfers between devices, body(): other = lax.ppermute(both, 'leaf', swap)  6.58 us
  transfers between devices with their start and end apart: 3, of which 3 were waited for; matrix products, arithmetic and copies ran while one was open for 1% of the time, Pallas kernels for 0%

profile of v9, /device:TPU:1, one launch (start us, length us, event | category | flops | bytes accessed | tf_op | source)
XLA Modules:
  0.0 213.6 jit_solution(14011979636103887229)
XLA Ops:
  0.0 1.1 fusion.78
  1.1 0.7 pad_maximum_fusion.5
  1.8 12.1 %all-to-all-start = ((bf16[32,24,128]{2,1,0:T(8,128)(2,1)}), bf16[32,24,128]{2,1,0:T(8,128)(2,1)S(1)}, u32[]{:S(2)}, u32[]{:S(2)}) async-start(bf16[32,24,128]{2,1,0:T(8,128)(2,1)} %pad_maximum_fusion.5), calls=%async_computation | async-start | bytes 393216 | tf_op jit(solution)/shard_map/all_to_all | solution.py:41
  13.9 0.7 fusion.84
  16.4 0.1 iota_compare_fusion.1
  16.5 0.3 copy.37
  16.7 0.7 slice-done.1
  17.5 0.3 copy.38
  17.7 0.1 fusion.71
  17.9 0.1 fusion.16
  18.1 1.2 all-to-all-done
  19.4 16.4 %all_to_all.60 = bf16[8,40,128]{2,1,0:T(8,128)(2,1)S(1)} all-to-all(bf16[8,40,128]{2,1,0:T(8,128)(2,1)S(1)} %maximum_select_fusion.6), channel_id=1, replica_groups={{96,128,160,192,224,0,32,64},{112,144,176,208,240,16,48,80},{352,384,41..., dimensions={0} | all-to-all | bytes 163840 | tf_op jit(solution)/shard_map/all_to_all | solution.py:44
  35.9 0.1 fusion.56
  36.0 0.1 pad_maximum_fusion
  36.1 19.0 %all_to_all.61 = bf16[32,24,512]{2,1,0:T(8,128)(2,1)S(1)} all-to-all(bf16[32,24,512]{2,1,0:T(8,128)(2,1)S(1)} %pad_maximum_fusion), channel_id=1, replica_groups={{22,23,24,25,26,27,28,29,30,31,16,17,18,19,20,21,6,7,8,9,10,11,12,13,14..., dimensions={0} | all-to-all | bytes 1572864 | tf_op jit(solution)/shard_map/all_to_all | solution.py:41
  55.2 0.3 fusion.5
  55.6 0.4 fusion.4
  56.0 0.2 copy.31
  56.3 13.0 %all_to_all.62 = bf16[32,24,256]{2,1,0:T(8,128)(2,1)S(1)} all-to-all(bf16[32,24,256]{2,1,0:T(8,128)(2,1)S(1)} %pad_maximum_fusion.3), channel_id=1, replica_groups={{22,23,24,25,26,27,28,29,30,31,16,17,18,19,20,21,6,7,8,9,10,11,12,13,14..., dimensions={0} | all-to-all | bytes 786432 | tf_op jit(solution)/shard_map/all_to_all | solution.py:41
  69.5 18.8 %all_to_all.63 = bf16[16,40,128]{2,1,0:T(8,128)(2,1)S(1)} all-to-all(bf16[16,40,128]{2,1,0:T(8,128)(2,1)S(1)} %maximum_select_fusion.2), channel_id=1, replica_groups={{192,224,256,288,320,352,384,416,448,480,0,32,64,96,128,160},{208,240,2..., dimensions={0} | all-to-all | bytes 327680 | tf_op jit(solution)/shard_map/all_to_all | solution.py:44
  88.4 0.1 fusion.46
  88.5 0.1 fusion.48
  88.7 0.1 fusion.51
  88.8 13.1 %all_to_all.64 = bf16[32,24,128]{2,1,0:T(8,128)(2,1)S(1)} all-to-all(bf16[32,24,128]{2,1,0:T(8,128)(2,1)S(1)} %broadcast_in_dim.164), channel_id=1, replica_groups={{22,23,24,25,26,27,28,29,30,31,16,17,18,19,20,21,6,7,8,9,10,11,12,13,14..., dimensions={0} | all-to-all | bytes 393216 | tf_op jit(solution)/shard_map/all_to_all | solution.py:41
  102.0 0.2 fusion.19
  102.2 0.2 fusion.6
  102.6 18.4 %all_to_all.65 = bf16[16,40,128]{2,1,0:T(8,128)(2,1)S(1)} all-to-all(bf16[16,40,128]{2,1,0:T(8,128)(2,1)S(1)} %fusion.25), channel_id=1, replica_groups={{192,224,256,288,320,352,384,416,448,480,0,32,64,96,128,160},{208,240,2..., dimensions={0} | all-to-all | bytes 327680 | tf_op jit(solution)/shard_map/all_to_all | solution.py:44
  121.0 0.1 fusion.44
  121.3 19.1 %all_to_all.66 = bf16[32,24,512]{2,1,0:T(8,128)(2,1)S(1)} all-to-all(bf16[32,24,512]{2,1,0:T(8,128)(2,1)S(1)} %pad_maximum_fusion.1), channel_id=1, replica_groups={{22,23,24,25,26,27,28,29,30,31,16,17,18,19,20,21,6,7,8,9,10,11,12,13,14..., dimensions={0} | all-to-all | bytes 1572864 | tf_op jit(solution)/shard_map/all_to_all | solution.py:41
  140.5 0.2 fusion.23
  140.7 0.2 fusion.21
  140.9 0.2 fusion.3
  141.1 0.2 fusion.7
  141.4 18.4 %all_to_all.67 = bf16[16,40,128]{2,1,0:T(8,128)(2,1)S(1)} all-to-all(bf16[16,40,128]{2,1,0:T(8,128)(2,1)S(1)} %pad_maximum_fusion.6), channel_id=1, replica_groups={{192,224,256,288,320,352,384,416,448,480,0,32,64,96,128,160},{208,240,2..., dimensions={0} | all-to-all | bytes 327680 | tf_op jit(solution)/shard_map/all_to_all | solution.py:44
  159.9 0.1 fusion.58
  160.0 12.8 %all_to_all.68 = bf16[32,24,128]{2,1,0:T(8,128)(2,1)S(1)} all-to-all(bf16[32,24,128]{2,1,0:T(8,128)(2,1)S(1)} %bitcast.124), channel_id=1, replica_groups={{22,23,24,25,26,27,28,29,30,31,16,17,18,19,20,21,6,7,8,9,10,11,12,13,14..., dimensions={0} | all-to-all | bytes 393216 | tf_op jit(solution)/shard_map/all_to_all | solution.py:41
  172.8 0.3 fusion.9
  173.2 0.7 copy-done.3
  173.9 0.4 fusion
  174.3 0.2 copy.34
  174.6 2.3 %collective-permute-start = (bf16[8,80,128]{2,1,0:T(8,128)(2,1)S(1)}, bf16[8,80,128]{2,1,0:T(8,128)(2,1)S(1)}, u32[]{:S(2)}, u32[]{:S(2)}) collective-permute-start(bf16[8,80,128]{2,1,0:T(8,128)(2,1)S(1)} %pad_maximum_fusion.8), channel_id=1, source_target_pairs={{0,16},{16,0},{32,48},{48,32},{64,80},{80,64},{96,112},{112,96},{1... | collective-permute-start | bytes 491528 | tf_op jit(solution)/shard_map/ppermute | solution.py:174
  176.9 1.0 collective-permute-done
  178.0 15.0 %all_to_all.69 = bf16[8,80,128]{2,1,0:T(8,128)(2,1)S(1)} all-to-all(bf16[8,80,128]{2,1,0:T(8,128)(2,1)S(1)} %pad_maximum_fusion.9), channel_id=1, replica_groups={{96,128,160,192,224,0,32,64},{112,144,176,208,240,16,48,80},{352,384,41..., dimensions={0} | all-to-all | bytes 327680 | tf_op jit(solution)/shard_map/all_to_all | solution.py:44
  193.0 0.1 fusion.38
  193.1 12.1 %all_to_all.70 = bf16[8,2,40,128]{3,2,1,0:T(8,128)(2,1)S(1)} all-to-all(bf16[8,2,40,128]{3,2,1,0:T(8,128)(2,1)S(1)} %broadcast_in_dim.175), channel_id=1, replica_groups={{96,128,160,192,224,0,32,64},{112,144,176,208,240,16,48,80},{352,384,41..., dimensions={0} | all-to-all | bytes 327680 | tf_op jit(solution)/shard_map/all_to_all | solution.py:44
  205.2 6.6 %collective-permute-start.1 = (bf16[2,320,128]{2,1,0:T(8,128)(2,1)S(1)}, bf16[2,320,128]{2,1,0:T(8,128)(2,1)S(1)}, u32[]{:S(2)}, u32[]{:S(2)}) collective-permute-start(bf16[2,320,128]{2,1,0:T(8,128)(2,1)S(1)} %bitcast.128), channel_id=1, source_target_pairs={{0,16},{16,0},{32,48},{48,32},{64,80},{80,64},{96,112},{112,96},{1... | collective-permute-start | bytes 491528 | tf_op jit(solution)/shard_map/ppermute | solution.py:183
  211.8 1.0 collective-permute-done.1
  212.8 0.8 fusion.17
  (105 shorter events, 1.6 us)
Async XLA Ops:
  0.0 55.6 %copy-start = (bf16[1,640,640]{2,1,0:T(8,128)(2,1)S(1)}, bf16[1,640,640]{2,1,0:T(8,128)(2,1)}, u32[]{:S(2)}) copy-start(bf16[1,640,640]{2,1,0:T(8,128)(2,1)} %param.9) | copy-start | bytes 2457604
  0.0 13.9 %copy-start.4 = (s32[2,32]{1,0:T(2,128)S(1)}, s32[2,32]{1,0:T(2,128)}, u32[]{:S(2)}) copy-start(s32[2,32]{1,0:T(2,128)} %param.7) | copy-start | bytes 772
  0.0 16.5 %slice-start = ((bf16[1,640,960]{1,2,0:T(8,128)(2,1)}), bf16[1,640,320]{1,2,0:T(8,128)(2,1)S(1)}, s32[]{:S(2)}) async-start(bf16[1,640,960]{1,2,0:T(8,128)(2,1)} %param.8), calls=%async_computation.12 | async-start | bytes 819200 | tf_op jit(solution)/shard_map/slice | solution.py:121
  1.8 17.5 %all-to-all-start = ((bf16[32,24,128]{2,1,0:T(8,128)(2,1)}), bf16[32,24,128]{2,1,0:T(8,128)(2,1)S(1)}, u32[]{:S(2)}, u32[]{:S(2)}) async-start(bf16[32,24,128]{2,1,0:T(8,128)(2,1)} %pad_maximum_fusion.5), calls=%async_computation | async-start | bytes 393216 | tf_op jit(solution)/shard_map/all_to_all | solution.py:41
  16.5 1.0 slice-start.1
  36.1 19.1 %copy-start.1 = (bf16[1,640,960]{1,2,0:T(8,128)(2,1)S(1)}, bf16[1,640,960]{1,2,0:T(8,128)(2,1)}, u32[]{:S(2)}) copy-start(bf16[1,640,960]{1,2,0:T(8,128)(2,1)} %param.8) | copy-start | bytes 3686404
  141.4 31.5 %copy-start.2 = (bf16[1,640,960]{1,2,0:T(8,128)(2,1)S(1)}, bf16[1,640,960]{1,2,0:T(8,128)(2,1)}, u32[]{:S(2)}) copy-start(bf16[1,640,960]{1,2,0:T(8,128)(2,1)} %param.10) | copy-start | bytes 3686404
  172.8 1.1 copy-start.3
  174.6 3.3 %collective-permute-start = (bf16[8,80,128]{2,1,0:T(8,128)(2,1)S(1)}, bf16[8,80,128]{2,1,0:T(8,128)(2,1)S(1)}, u32[]{:S(2)}, u32[]{:S(2)}) collective-permute-start(bf16[8,80,128]{2,1,0:T(8,128)(2,1)S(1)} %pad_maximum_fusion.8), channel_id=1, source_target_pairs={{0,16},{16,0},{32,48},{48,32},{64,80},{80,64},{96,112},{112,96},{1... | collective-permute-start | bytes 491528 | tf_op jit(solution)/shard_map/ppermute | solution.py:174
  205.2 7.6 %collective-permute-start.1 = (bf16[2,320,128]{2,1,0:T(8,128)(2,1)S(1)}, bf16[2,320,128]{2,1,0:T(8,128)(2,1)S(1)}, u32[]{:S(2)}, u32[]{:S(2)}) collective-permute-start(bf16[2,320,128]{2,1,0:T(8,128)(2,1)S(1)} %bitcast.128), channel_id=1, source_target_pairs={{0,16},{16,0},{32,48},{48,32},{64,80},{80,64},{96,112},{112,96},{1... | collective-permute-start | bytes 491528 | tf_op jit(solution)/shard_map/ppermute | solution.py:183

commit v10 on v9

--- a/solution.py
+++ b/solution.py
@@ -35,6 +35,9 @@
     plane = [[(2 * k + c) * n_front + f for c in (1, 0) for f in fronts] for k in range(n_z)]
     z_all = [[2 * k + c for k in planes] for c in range(2)]
     z_half = [[2 * (h * half + k) + c for k in halves] for h in range(2) for c in range(2)]
+    mid = half // 2
+    middle_first = [mid] + [k for k in range(half) if k != mid]
+    z_last = [[2 * (h * half + k) + c for k in middle_first] for h in range(2) for c in range(2)]
     swap = [(k, k ^ 1) for k in range(n_leaf)]
 
     def a2a_plane(v):
@@ -44,7 +47,7 @@
         return lax.all_to_all(v, "leaf", 0, 0, axis_index_groups=groups)
 
     def place(k):
-        return (k + (half - turn)) % half
+        return jnp.where(k == mid, u32(0), jnp.where(k < mid, k + 1, k))
 
     def spread(v, n):
         return jnp.broadcast_to(v[None], (n,) + v.shape)
@@ -130,11 +133,17 @@
     rm0 = moved[:, :, :n_rhs]
     rm0 = jnp.where(low, join_second(rm0), join(rm0))
 
-    c_part = dot(lower_upd[0], rm0).astype(bf)
-    y_part = dot(lower_inv[0, :, :w0], rm0).astype(bf)
-    parts = fold(a2a_plane(cut(jnp.concatenate([c_part, y_part], 1)))).astype(bf)
-
-    got = a2a_leaf(pack(parts[:, :, :n_rhs], parts[:, :, n_rhs:], low), z_all)
+    c_part = dot(lower_upd[0], rm0).astype(bf).reshape(n_front, PIECE, n_rhs)
+    y_part = dot(lower_inv[0, :, :w0], rm0).astype(bf).reshape(n_front, PIECE, n_rhs)
+    parts = jnp.stack(
+        [
+            jnp.concatenate([c_part[:, :WIN], y_part[:, :LO]], 1),
+            jnp.concatenate([c_part[:, WIN:], y_part[:, LO:]], 1),
+        ]
+    )
+    parts = fold(a2a_plane(parts.reshape(n_plane, PIECE, n_rhs))).astype(bf)
+
+    got = a2a_leaf(parts, z_all)
     edge = half - shift
     sum_a, sum_b = total(got[:edge]) + total(got[edge + half :]), total(got[edge : edge + half])
     r1 = masked(-unpack(sum_a + sum_b, low), keep[4])
@@ -174,11 +183,11 @@
     away = lax.ppermute(away, "leaf", swap)
     term = (pick(term, core, 1)[0] + away[:, :PIECE].astype(f32)).astype(bf)
     own = jnp.where(mine, pick(x1, core, 1)[0], away[:, PIECE:])
-    got = a2a_leaf(jnp.concatenate([term, own], 1), z_half)
+    got = a2a_leaf(jnp.concatenate([term, own], 1), z_last)
 
     x0 = masked(total(got[:, :PIECE]), keep[7])
     x1 = pick(got[:, PIECE:], source, 1)[0]
-    both = a2a_leaf(spread(jnp.stack([x0, x1]), half), z_half)
+    both = a2a_leaf(spread(jnp.stack([x0, x1]), half), z_last)
     both = jnp.swapaxes(both, 0, 1).reshape(2, half * PIECE, n_rhs)
     other = lax.ppermute(both, "leaf", swap)
     both = jnp.where(core == 0, jnp.concatenate([both, other], 1), jnp.concatenate([other, both], 1))

time: 214 us -> 212 us (level)
  no operation moved by 1% of the time
where the time goes in v10:
time: 212 us; the launch traced here: 211 us
  blocking collectives  174 us (82%)
  starting transfers between devices  20.7 us (10%)
  local copies, waits for them, and re-layouts  4.87 us (2%)
  waiting for transfers between devices  3.24 us (2%)
  other arithmetic  3.17 us (1%)
  between operations  2.73 us (1%)
  matrix products  2.67 us (1%)
    all_to_all x6, blocking collectives, a2a_leaf(): return lax.all_to_all(v, 'leaf', 0, 0, axis_index_groups=groups)  97.4 us
    all_to_all x5, blocking collectives, a2a_plane(): return lax.all_to_all(v, ('leaf', 'front'), 0, 0, axis_index_groups=plane)  76.3 us
    all_to_all x1, starting transfers between devices, a2a_plane(): return lax.all_to_all(v, ('leaf', 'front'), 0, 0, axis_index_groups=plane)  12.1 us
    ppermute x1, starting transfers between devices, body(): other = lax.ppermute(both, 'leaf', swap)  6.36 us
  transfers between devices with their start and end apart: 3, of which 3 were waited for; matrix products, arithmetic and copies ran while one was open for 1% of the time, Pallas kernels for 0%

profile of v10, /device:TPU:1, one launch (start us, length us, event | category | flops | bytes accessed | tf_op | source)
XLA Modules:
  0.0 211.1 jit_solution(12296776282157447206)
XLA Ops:
  0.0 1.1 fusion.75
  1.1 0.7 pad_maximum_fusion.4
  1.8 12.1 %all-to-all-start = ((bf16[32,24,128]{2,1,0:T(8,128)(2,1)}), bf16[32,24,128]{2,1,0:T(8,128)(2,1)S(1)}, u32[]{:S(2)}, u32[]{:S(2)}) async-start(bf16[32,24,128]{2,1,0:T(8,128)(2,1)} %pad_maximum_fusion.4), calls=%async_computation | async-start | bytes 393216 | tf_op jit(solution)/shard_map/all_to_all | solution.py:44
  13.9 0.6 fusion.81
  16.3 0.1 iota_compare_fusion.1
  16.4 0.3 copy.41
  16.7 0.7 slice-done.1
  17.4 0.3 copy.42
  17.7 0.1 fusion.71
  17.9 0.1 fusion.16
  18.0 1.2 all-to-all-done
  19.4 16.4 %all_to_all.60 = bf16[8,40,128]{2,1,0:T(8,128)(2,1)S(1)} all-to-all(bf16[8,40,128]{2,1,0:T(8,128)(2,1)S(1)} %maximum_select_fusion.5), channel_id=1, replica_groups={{96,128,160,192,224,0,32,64},{112,144,176,208,240,16,48,80},{352,384,41..., dimensions={0} | all-to-all | bytes 163840 | tf_op jit(solution)/shard_map/all_to_all | solution.py:47
  35.9 0.1 fusion.56
  36.1 19.0 %all_to_all.61 = bf16[32,24,512]{2,1,0:T(8,128)(2,1)S(1)} all-to-all(bf16[32,24,512]{2,1,0:T(8,128)(2,1)S(1)} %pad_maximum_fusion), channel_id=1, replica_groups={{22,23,24,25,26,27,28,29,30,31,16,17,18,19,20,21,6,7,8,9,10,11,12,13,14..., dimensions={0} | all-to-all | bytes 1572864 | tf_op jit(solution)/shard_map/all_to_all | solution.py:44
  55.2 0.3 fusion.5
  55.6 0.2 copy.35
  55.8 0.4 fusion.4
  56.2 0.2 copy.34
  56.5 12.3 %all_to_all.62 = bf16[32,40,128]{2,1,0:T(8,128)(2,1)S(1)} all-to-all(bf16[32,40,128]{2,1,0:T(8,128)(2,1)S(1)} %bitcast.125), channel_id=1, replica_groups={{22,23,24,25,26,27,28,29,30,31,16,17,18,19,20,21,6,7,8,9,10,11,12,13,14..., dimensions={0} | all-to-all | bytes 655360 | tf_op jit(solution)/shard_map/all_to_all | solution.py:44
  68.8 18.9 %all_to_all.63 = bf16[16,40,128]{2,1,0:T(8,128)(2,1)S(1)} all-to-all(bf16[16,40,128]{2,1,0:T(8,128)(2,1)S(1)} %add_convert_fusion), channel_id=1, replica_groups={{192,224,256,288,320,352,384,416,448,480,0,32,64,96,128,160},{208,240,2..., dimensions={0} | all-to-all | bytes 327680 | tf_op jit(solution)/shard_map/all_to_all | solution.py:47
  87.9 0.1 fusion.46
  87.9 0.1 fusion.48
  88.2 0.1 fusion.51
  88.3 13.0 %all_to_all.64 = bf16[32,24,128]{2,1,0:T(8,128)(2,1)S(1)} all-to-all(bf16[32,24,128]{2,1,0:T(8,128)(2,1)S(1)} %broadcast_in_dim.164), channel_id=1, replica_groups={{22,23,24,25,26,27,28,29,30,31,16,17,18,19,20,21,6,7,8,9,10,11,12,13,14..., dimensions={0} | all-to-all | bytes 393216 | tf_op jit(solution)/shard_map/all_to_all | solution.py:44
  101.4 0.2 fusion.19
  101.6 0.2 fusion.6
  101.9 18.4 %all_to_all.65 = bf16[16,40,128]{2,1,0:T(8,128)(2,1)S(1)} all-to-all(bf16[16,40,128]{2,1,0:T(8,128)(2,1)S(1)} %fusion.25), channel_id=1, replica_groups={{192,224,256,288,320,352,384,416,448,480,0,32,64,96,128,160},{208,240,2..., dimensions={0} | all-to-all | bytes 327680 | tf_op jit(solution)/shard_map/all_to_all | solution.py:47
  120.4 0.1 fusion.44
  120.6 19.1 %all_to_all.66 = bf16[32,24,512]{2,1,0:T(8,128)(2,1)S(1)} all-to-all(bf16[32,24,512]{2,1,0:T(8,128)(2,1)S(1)} %pad_maximum_fusion.1), channel_id=1, replica_groups={{22,23,24,25,26,27,28,29,30,31,16,17,18,19,20,21,6,7,8,9,10,11,12,13,14..., dimensions={0} | all-to-all | bytes 1572864 | tf_op jit(solution)/shard_map/all_to_all | solution.py:44
  139.9 0.2 fusion.23
  140.1 0.2 fusion.21
  140.3 0.2 fusion.3
  140.5 0.2 fusion.7
  140.8 18.4 %all_to_all.67 = bf16[16,40,128]{2,1,0:T(8,128)(2,1)S(1)} all-to-all(bf16[16,40,128]{2,1,0:T(8,128)(2,1)S(1)} %pad_maximum_fusion.5), channel_id=1, replica_groups={{192,224,256,288,320,352,384,416,448,480,0,32,64,96,128,160},{208,240,2..., dimensions={0} | all-to-all | bytes 327680 | tf_op jit(solution)/shard_map/all_to_all | solution.py:47
  159.2 0.1 fusion.58
  159.3 12.8 %all_to_all.68 = bf16[32,24,128]{2,1,0:T(8,128)(2,1)S(1)} all-to-all(bf16[32,24,128]{2,1,0:T(8,128)(2,1)S(1)} %bitcast.130), channel_id=1, replica_groups={{22,23,24,25,26,27,28,29,30,31,16,17,18,19,20,21,6,7,8,9,10,11,12,13,14..., dimensions={0} | all-to-all | bytes 393216 | tf_op jit(solution)/shard_map/all_to_all | solution.py:44
  172.2 0.3 fusion.9
  172.6 0.7 copy-done.3
  173.3 0.4 fusion
  173.7 0.2 copy.38
  173.9 2.3 %collective-permute-start = (bf16[8,80,128]{2,1,0:T(8,128)(2,1)S(1)}, bf16[8,80,128]{2,1,0:T(8,128)(2,1)S(1)}, u32[]{:S(2)}, u32[]{:S(2)}) collective-permute-start(bf16[8,80,128]{2,1,0:T(8,128)(2,1)S(1)} %pad_maximum_fusion.7), channel_id=1, source_target_pairs={{0,16},{16,0},{32,48},{48,32},{64,80},{80,64},{96,112},{112,96},{1... | collective-permute-start | bytes 491528 | tf_op jit(solution)/shard_map/ppermute | solution.py:183
  176.3 1.0 collective-permute-done
  177.3 12.4 %all_to_all.69 = bf16[8,80,128]{2,1,0:T(8,128)(2,1)S(1)} all-to-all(bf16[8,80,128]{2,1,0:T(8,128)(2,1)S(1)} %pad_maximum_fusion.8), channel_id=1, replica_groups={{128,0,32,64,96,160,192,224},{144,16,48,80,112,176,208,240},{384,256,28..., dimensions={0} | all-to-all | bytes 327680 | tf_op jit(solution)/shard_map/all_to_all | solution.py:47
  189.7 0.1 fusion.38
  189.9 13.0 %all_to_all.70 = bf16[8,2,40,128]{3,2,1,0:T(8,128)(2,1)S(1)} all-to-all(bf16[8,2,40,128]{3,2,1,0:T(8,128)(2,1)S(1)} %broadcast_in_dim.175), channel_id=1, replica_groups={{128,0,32,64,96,160,192,224},{144,16,48,80,112,176,208,240},{384,256,28..., dimensions={0} | all-to-all | bytes 327680 | tf_op jit(solution)/shard_map/all_to_all | solution.py:47
  202.9 6.4 %collective-permute-start.1 = (bf16[2,320,128]{2,1,0:T(8,128)(2,1)S(1)}, bf16[2,320,128]{2,1,0:T(8,128)(2,1)S(1)}, u32[]{:S(2)}, u32[]{:S(2)}) collective-permute-start(bf16[2,320,128]{2,1,0:T(8,128)(2,1)S(1)} %bitcast.138), channel_id=1, source_target_pairs={{0,16},{16,0},{32,48},{48,32},{64,80},{80,64},{96,112},{112,96},{1... | collective-permute-start | bytes 491528 | tf_op jit(solution)/shard_map/ppermute | solution.py:192
  209.3 1.0 collective-permute-done.1
  210.3 0.8 fusion.17
  (107 shorter events, 1.6 us)
Async XLA Ops:
  0.0 55.8 %copy-start = (bf16[1,640,640]{2,1,0:T(8,128)(2,1)S(1)}, bf16[1,640,640]{2,1,0:T(8,128)(2,1)}, u32[]{:S(2)}) copy-start(bf16[1,640,640]{2,1,0:T(8,128)(2,1)} %param.9) | copy-start | bytes 2457604
  0.0 13.9 %copy-start.4 = (s32[2,32]{1,0:T(2,128)S(1)}, s32[2,32]{1,0:T(2,128)}, u32[]{:S(2)}) copy-start(s32[2,32]{1,0:T(2,128)} %param.7) | copy-start | bytes 772
  0.0 16.4 %slice-start = ((bf16[1,640,960]{1,2,0:T(8,128)(2,1)}), bf16[1,640,320]{1,2,0:T(8,128)(2,1)S(1)}, s32[]{:S(2)}) async-start(bf16[1,640,960]{1,2,0:T(8,128)(2,1)} %param.8), calls=%async_computation.12 | async-start | bytes 819200 | tf_op jit(solution)/shard_map/slice | solution.py:124
  1.8 17.5 %all-to-all-start = ((bf16[32,24,128]{2,1,0:T(8,128)(2,1)}), bf16[32,24,128]{2,1,0:T(8,128)(2,1)S(1)}, u32[]{:S(2)}, u32[]{:S(2)}) async-start(bf16[32,24,128]{2,1,0:T(8,128)(2,1)} %pad_maximum_fusion.4), calls=%async_computation | async-start | bytes 393216 | tf_op jit(solution)/shard_map/all_to_all | solution.py:44
  16.4 1.0 slice-start.1
  36.1 19.1 %copy-start.1 = (bf16[1,640,960]{1,2,0:T(8,128)(2,1)S(1)}, bf16[1,640,960]{1,2,0:T(8,128)(2,1)}, u32[]{:S(2)}) copy-start(bf16[1,640,960]{1,2,0:T(8,128)(2,1)} %param.8) | copy-start | bytes 3686404
  140.7 31.5 %copy-start.2 = (bf16[1,640,960]{1,2,0:T(8,128)(2,1)S(1)}, bf16[1,640,960]{1,2,0:T(8,128)(2,1)}, u32[]{:S(2)}) copy-start(bf16[1,640,960]{1,2,0:T(8,128)(2,1)} %param.10) | copy-start | bytes 3686404
  172.2 1.1 copy-start.3
  173.9 3.3 %collective-permute-start = (bf16[8,80,128]{2,1,0:T(8,128)(2,1)S(1)}, bf16[8,80,128]{2,1,0:T(8,128)(2,1)S(1)}, u32[]{:S(2)}, u32[]{:S(2)}) collective-permute-start(bf16[8,80,128]{2,1,0:T(8,128)(2,1)S(1)} %pad_maximum_fusion.7), channel_id=1, source_target_pairs={{0,16},{16,0},{32,48},{48,32},{64,80},{80,64},{96,112},{112,96},{1... | collective-permute-start | bytes 491528 | tf_op jit(solution)/shard_map/ppermute | solution.py:183
  202.9 7.4 %collective-permute-start.1 = (bf16[2,320,128]{2,1,0:T(8,128)(2,1)S(1)}, bf16[2,320,128]{2,1,0:T(8,128)(2,1)S(1)}, u32[]{:S(2)}, u32[]{:S(2)}) collective-permute-start(bf16[2,320,128]{2,1,0:T(8,128)(2,1)S(1)} %bitcast.138), channel_id=1, source_target_pairs={{0,16},{16,0},{32,48},{48,32},{64,80},{80,64},{96,112},{112,96},{1... | collective-permute-start | bytes 491528 | tf_op jit(solution)/shard_map/ppermute | solution.py:192

commit v11 on v10

--- a/solution.py
+++ b/solution.py
@@ -172,12 +172,13 @@
     x1 = x1.astype(bf).reshape(half, 2, WIN, n_rhs)
     x1 = pack(x1[:, 0], x1[:, 1], low)
     x1, y0 = lax.optimization_barrier((jnp.concatenate([x1[turn:], x1, x1[:turn]], 0), y0))
-    x1 = total(a2a_leaf(x1, z_all))
+    x1, y0 = lax.optimization_barrier((total(a2a_leaf(x1, z_all)), y0))
     x1 = by_core(masked(unpack(x1, low), keep[5]), masked(unpack_second(x1, low), keep[6]))
-    x1, y0 = lax.optimization_barrier((a2a_plane(x1), y0))
+    x1, term = lax.optimization_barrier((x1, dot(upper_inv[0, :, :w0], y0)))
+    x1 = a2a_plane(x1)
     x1 = jnp.where(low, join_second(x1), join(x1))
 
-    term = (dot(upper_inv[0, :, :w0], y0) - dot(upper_upd[0], x1)).reshape(2, half, PIECE, n_rhs)
+    term = (term - dot(upper_upd[0], x1)).reshape(2, half, PIECE, n_rhs)
     x1 = x1.reshape(2, half, PIECE, n_rhs)
     away = jnp.concatenate([pick(term, other_core, 1)[0].astype(bf), pick(x1, other_core, 1)[0]], 1)
     away = lax.ppermute(away, "leaf", swap)

time: 212 us -> 211 us (level)
  no operation moved by 1% of the time
where the time goes in v11:
time: 211 us
  blocking collectives  174 us (82%)
  starting transfers between devices  20.7 us (10%)
  local copies, waits for them, and re-layouts  4.17 us (2%)
  waiting for transfers between devices  3.24 us (2%)
  other arithmetic  3.17 us (2%)
  between operations  2.74 us (1%)
  matrix products  2.67 us (1%)
    all_to_all x6, blocking collectives, a2a_leaf(): return lax.all_to_all(v, 'leaf', 0, 0, axis_index_groups=groups)  97.4 us
    all_to_all x5, blocking collectives, a2a_plane(): return lax.all_to_all(v, ('leaf', 'front'), 0, 0, axis_index_groups=plane)  76.4 us
    all_to_all x1, starting transfers between devices, a2a_plane(): return lax.all_to_all(v, ('leaf', 'front'), 0, 0, axis_index_groups=plane)  12.1 us
    ppermute x1, starting transfers between devices, body(): other = lax.ppermute(both, 'leaf', swap)  6.36 us
  transfers between devices with their start and end apart: 3, of which 3 were waited for; matrix products, arithmetic and copies ran while one was open for 1% of the time, Pallas kernels for 0%

profile of v11, /device:TPU:1, one launch (start us, length us, event | category | flops | bytes accessed | tf_op | source)
XLA Modules:
  0.0 210.6 jit_solution(8299038199177428336)
XLA Ops:
  0.0 1.1 fusion.74
  1.1 0.7 pad_maximum_fusion.4
  1.8 12.1 %all-to-all-start = ((bf16[32,24,128]{2,1,0:T(8,128)(2,1)}), bf16[32,24,128]{2,1,0:T(8,128)(2,1)S(1)}, u32[]{:S(2)}, u32[]{:S(2)}) async-start(bf16[32,24,128]{2,1,0:T(8,128)(2,1)} %pad_maximum_fusion.4), calls=%async_computation | async-start | bytes 393216 | tf_op jit(solution)/shard_map/all_to_all | solution.py:44
  13.9 0.6 fusion.80
  16.3 0.1 iota_compare_fusion.1
  16.4 0.3 copy.41
  16.7 0.7 slice-done.1
  17.4 0.3 copy.42
  17.7 0.1 fusion.70
  17.9 0.1 fusion.15
  18.0 1.2 all-to-all-done
  19.4 16.4 %all_to_all.60 = bf16[8,40,128]{2,1,0:T(8,128)(2,1)S(1)} all-to-all(bf16[8,40,128]{2,1,0:T(8,128)(2,1)S(1)} %maximum_select_fusion.5), channel_id=1, replica_groups={{96,128,160,192,224,0,32,64},{112,144,176,208,240,16,48,80},{352,384,41..., dimensions={0} | all-to-all | bytes 163840 | tf_op jit(solution)/shard_map/all_to_all | solution.py:47
  35.9 0.1 fusion.57
  36.0 0.1 pad_maximum_fusion
  36.1 19.0 %all_to_all.61 = bf16[32,24,512]{2,1,0:T(8,128)(2,1)S(1)} all-to-all(bf16[32,24,512]{2,1,0:T(8,128)(2,1)S(1)} %pad_maximum_fusion), channel_id=1, replica_groups={{22,23,24,25,26,27,28,29,30,31,16,17,18,19,20,21,6,7,8,9,10,11,12,13,14..., dimensions={0} | all-to-all | bytes 1572864 | tf_op jit(solution)/shard_map/all_to_all | solution.py:44
  55.2 0.3 fusion.5
  55.6 0.2 copy.35
  55.8 0.4 fusion.4
  56.2 0.2 copy.34
  56.5 12.3 %all_to_all.62 = bf16[32,40,128]{2,1,0:T(8,128)(2,1)S(1)} all-to-all(bf16[32,40,128]{2,1,0:T(8,128)(2,1)S(1)} %bitcast.129), channel_id=1, replica_groups={{22,23,24,25,26,27,28,29,30,31,16,17,18,19,20,21,6,7,8,9,10,11,12,13,14..., dimensions={0} | all-to-all | bytes 655360 | tf_op jit(solution)/shard_map/all_to_all | solution.py:44
  68.8 18.9 %all_to_all.63 = bf16[16,40,128]{2,1,0:T(8,128)(2,1)S(1)} all-to-all(bf16[16,40,128]{2,1,0:T(8,128)(2,1)S(1)} %add_convert_fusion), channel_id=1, replica_groups={{192,224,256,288,320,352,384,416,448,480,0,32,64,96,128,160},{208,240,2..., dimensions={0} | all-to-all | bytes 327680 | tf_op jit(solution)/shard_map/all_to_all | solution.py:47
  87.9 0.1 fusion.41
  87.9 0.1 fusion.43
  88.2 0.1 fusion.46
  88.3 13.0 %all_to_all.64 = bf16[32,24,128]{2,1,0:T(8,128)(2,1)S(1)} all-to-all(bf16[32,24,128]{2,1,0:T(8,128)(2,1)S(1)} %broadcast_in_dim.164), channel_id=1, replica_groups={{22,23,24,25,26,27,28,29,30,31,16,17,18,19,20,21,6,7,8,9,10,11,12,13,14..., dimensions={0} | all-to-all | bytes 393216 | tf_op jit(solution)/shard_map/all_to_all | solution.py:44
  101.4 0.2 fusion.18
  101.6 0.2 fusion.6
  101.9 18.4 %all_to_all.65 = bf16[16,40,128]{2,1,0:T(8,128)(2,1)S(1)} all-to-all(bf16[16,40,128]{2,1,0:T(8,128)(2,1)S(1)} %fusion.24), channel_id=1, replica_groups={{192,224,256,288,320,352,384,416,448,480,0,32,64,96,128,160},{208,240,2..., dimensions={0} | all-to-all | bytes 327680 | tf_op jit(solution)/shard_map/all_to_all | solution.py:47
  120.4 0.1 fusion.39
  120.6 19.1 %all_to_all.66 = bf16[32,24,512]{2,1,0:T(8,128)(2,1)S(1)} all-to-all(bf16[32,24,512]{2,1,0:T(8,128)(2,1)S(1)} %pad_maximum_fusion.1), channel_id=1, replica_groups={{22,23,24,25,26,27,28,29,30,31,16,17,18,19,20,21,6,7,8,9,10,11,12,13,14..., dimensions={0} | all-to-all | bytes 1572864 | tf_op jit(solution)/shard_map/all_to_all | solution.py:44
  139.9 0.2 fusion.22
  140.1 0.2 fusion.20
  140.3 0.2 fusion.3
  140.5 0.2 fusion.7
  140.8 18.4 %all_to_all.67 = bf16[16,40,128]{2,1,0:T(8,128)(2,1)S(1)} all-to-all(bf16[16,40,128]{2,1,0:T(8,128)(2,1)S(1)} %pad_maximum_fusion.5), channel_id=1, replica_groups={{192,224,256,288,320,352,384,416,448,480,0,32,64,96,128,160},{208,240,2..., dimensions={0} | all-to-all | bytes 327680 | tf_op jit(solution)/shard_map/all_to_all | solution.py:47
  159.2 0.3 convolution_bitcast_fusion.1
  159.6 0.1 fusion.56
  159.7 12.9 %all_to_all.68 = bf16[32,24,128]{2,1,0:T(8,128)(2,1)S(1)} all-to-all(bf16[32,24,128]{2,1,0:T(8,128)(2,1)S(1)} %bitcast.134), channel_id=1, replica_groups={{22,23,24,25,26,27,28,29,30,31,16,17,18,19,20,21,6,7,8,9,10,11,12,13,14..., dimensions={0} | all-to-all | bytes 393216 | tf_op jit(solution)/shard_map/all_to_all | solution.py:44
  172.8 0.4 fusion
  173.2 0.2 copy.38
  173.4 2.3 %collective-permute-start = (bf16[8,80,128]{2,1,0:T(8,128)(2,1)S(1)}, bf16[8,80,128]{2,1,0:T(8,128)(2,1)S(1)}, u32[]{:S(2)}, u32[]{:S(2)}) collective-permute-start(bf16[8,80,128]{2,1,0:T(8,128)(2,1)S(1)} %pad_maximum_fusion.7), channel_id=1, source_target_pairs={{0,16},{16,0},{32,48},{48,32},{64,80},{80,64},{96,112},{112,96},{1... | collective-permute-start | bytes 491528 | tf_op jit(solution)/shard_map/ppermute | solution.py:184
  175.7 1.0 collective-permute-done
  176.8 12.4 %all_to_all.69 = bf16[8,80,128]{2,1,0:T(8,128)(2,1)S(1)} all-to-all(bf16[8,80,128]{2,1,0:T(8,128)(2,1)S(1)} %pad_maximum_fusion.8), channel_id=1, replica_groups={{128,0,32,64,96,160,192,224},{144,16,48,80,112,176,208,240},{384,256,28..., dimensions={0} | all-to-all | bytes 327680 | tf_op jit(solution)/shard_map/all_to_all | solution.py:47
  189.2 0.1 fusion.37
  189.3 13.0 %all_to_all.70 = bf16[8,2,40,128]{3,2,1,0:T(8,128)(2,1)S(1)} all-to-all(bf16[8,2,40,128]{3,2,1,0:T(8,128)(2,1)S(1)} %broadcast_in_dim.175), channel_id=1, replica_groups={{128,0,32,64,96,160,192,224},{144,16,48,80,112,176,208,240},{384,256,28..., dimensions={0} | all-to-all | bytes 327680 | tf_op jit(solution)/shard_map/all_to_all | solution.py:47
  202.4 6.4 %collective-permute-start.1 = (bf16[2,320,128]{2,1,0:T(8,128)(2,1)S(1)}, bf16[2,320,128]{2,1,0:T(8,128)(2,1)S(1)}, u32[]{:S(2)}, u32[]{:S(2)}) collective-permute-start(bf16[2,320,128]{2,1,0:T(8,128)(2,1)S(1)} %bitcast.142), channel_id=1, source_target_pairs={{0,16},{16,0},{32,48},{48,32},{64,80},{80,64},{96,112},{112,96},{1... | collective-permute-start | bytes 491528 | tf_op jit(solution)/shard_map/ppermute | solution.py:193
  208.7 1.0 collective-permute-done.1
  209.7 0.8 fusion.16
  (107 shorter events, 1.5 us)
Async XLA Ops:
  0.0 55.8 %copy-start = (bf16[1,640,640]{2,1,0:T(8,128)(2,1)S(1)}, bf16[1,640,640]{2,1,0:T(8,128)(2,1)}, u32[]{:S(2)}) copy-start(bf16[1,640,640]{2,1,0:T(8,128)(2,1)} %param.9) | copy-start | bytes 2457604
  0.0 13.9 %copy-start.4 = (s32[2,32]{1,0:T(2,128)S(1)}, s32[2,32]{1,0:T(2,128)}, u32[]{:S(2)}) copy-start(s32[2,32]{1,0:T(2,128)} %param.7) | copy-start | bytes 772
  0.0 16.4 %slice-start = ((bf16[1,640,960]{1,2,0:T(8,128)(2,1)}), bf16[1,640,320]{1,2,0:T(8,128)(2,1)S(1)}, s32[]{:S(2)}) async-start(bf16[1,640,960]{1,2,0:T(8,128)(2,1)} %param.8), calls=%async_computation.12 | async-start | bytes 819200 | tf_op jit(solution)/shard_map/slice | solution.py:124
  1.8 17.5 %all-to-all-start = ((bf16[32,24,128]{2,1,0:T(8,128)(2,1)}), bf16[32,24,128]{2,1,0:T(8,128)(2,1)S(1)}, u32[]{:S(2)}, u32[]{:S(2)}) async-start(bf16[32,24,128]{2,1,0:T(8,128)(2,1)} %pad_maximum_fusion.4), calls=%async_computation | async-start | bytes 393216 | tf_op jit(solution)/shard_map/all_to_all | solution.py:44
  16.4 1.0 slice-start.1
  36.1 19.1 %copy-start.1 = (bf16[1,640,960]{1,2,0:T(8,128)(2,1)S(1)}, bf16[1,640,960]{1,2,0:T(8,128)(2,1)}, u32[]{:S(2)}) copy-start(bf16[1,640,960]{1,2,0:T(8,128)(2,1)} %param.8) | copy-start | bytes 3686404
  140.5 18.8 %copy-start.2 = (bf16[1,640,960]{1,2,0:T(8,128)(2,1)S(1)}, bf16[1,640,960]{1,2,0:T(8,128)(2,1)}, u32[]{:S(2)}) copy-start(bf16[1,640,960]{1,2,0:T(8,128)(2,1)} %param.10) | copy-start | bytes 3686404
  159.6 13.2 %copy-start.3 = (bf16[1,640,640]{2,1,0:T(8,128)(2,1)S(1)}, bf16[1,640,640]{2,1,0:T(8,128)(2,1)}, u32[]{:S(2)}) copy-start(bf16[1,640,640]{2,1,0:T(8,128)(2,1)} %param.11) | copy-start | bytes 2457604
  173.4 3.3 %collective-permute-start = (bf16[8,80,128]{2,1,0:T(8,128)(2,1)S(1)}, bf16[8,80,128]{2,1,0:T(8,128)(2,1)S(1)}, u32[]{:S(2)}, u32[]{:S(2)}) collective-permute-start(bf16[8,80,128]{2,1,0:T(8,128)(2,1)S(1)} %pad_maximum_fusion.7), channel_id=1, source_target_pairs={{0,16},{16,0},{32,48},{48,32},{64,80},{80,64},{96,112},{112,96},{1... | collective-permute-start | bytes 491528 | tf_op jit(solution)/shard_map/ppermute | solution.py:184
  202.4 7.4 %collective-permute-start.1 = (bf16[2,320,128]{2,1,0:T(8,128)(2,1)S(1)}, bf16[2,320,128]{2,1,0:T(8,128)(2,1)S(1)}, u32[]{:S(2)}, u32[]{:S(2)}) collective-permute-start(bf16[2,320,128]{2,1,0:T(8,128)(2,1)S(1)} %bitcast.142), channel_id=1, source_target_pairs={{0,16},{16,0},{32,48},{48,32},{64,80},{80,64},{96,112},{112,96},{1... | collective-permute-start | bytes 491528 | tf_op jit(solution)/shard_map/ppermute | solution.py:193

commit v12 on v11

--- a/solution.py
+++ b/solution.py
@@ -104,8 +104,9 @@
     def dot(a, b):
         return jnp.dot(a, b, preferred_element_type=f32)
 
-    def panel(mat, h, first, last):
-        return mat.reshape(2 * height, mat.shape[-1])[h * height : (h + 1) * height, first:last]
+    def dot_pair(mat, first, last, v):
+        m = mat.reshape(2, height, mat.shape[-1])[:, :, first:last]
+        return lax.dot_general(m, v, (((0, 2), (0, 1)), ((), ())), preferred_element_type=f32)
 
     live_a, live_b, live_root = (live[k].reshape(()) * BLK for k in ((0, slice(0, 1)), (0, slice(1, 2)), (1, slice(0, 1))))
     live_node = jnp.where(node == 0, live_a, live_b)
@@ -152,11 +153,9 @@
     r1, y0 = lax.optimization_barrier((spread(r1, n_plane), lift_second(y0, low)))
     r1 = join(a2a_plane(r1))
 
-    blank = jnp.zeros((n_rhs - tail, n_rhs), bf)
-    y1 = sum(
-        dot(panel(moved, h, n_rhs, n_rhs + w1 + tail), jnp.concatenate([r1[(1 - h) * w1 : (2 - h) * w1], blank], 0))
-        for h in range(2)
-    )
+    blank = jnp.zeros((2, n_rhs - tail, n_rhs), bf)
+    r1 = r1.reshape(2, w1, n_rhs)[::-1]
+    y1 = dot_pair(moved, n_rhs, n_rhs + w1 + tail, jnp.concatenate([r1, blank], 1))
     got = a2a_leaf(lift(y1.astype(bf).reshape(n_front, WIN, n_rhs), low) + y0, z_all)
     y1 = masked(unpack(total(got), low), keep[4])
     y0 = unpack_second(lax.optimization_barrier(pick(got, two_z8, 2)), low)
@@ -164,11 +163,9 @@
     y1 = join(got[:, :, :n_rhs])
     y0 = join_second(got[:, :, n_rhs : 2 * n_rhs])
 
-    x1 = 0.0
-    for h in range(2):
-        v = y1[(1 - h) * w1 : (2 - h) * w1]
-        x1 = x1 + dot(panel(got, h, 2 * n_rhs, 2 * n_rhs + head), v[:head])
-        x1 = x1 + dot(panel(moved, h, n_rhs + head, n_rhs + head + n_rhs), jnp.concatenate([blank, v[head:]], 0))
+    y1 = y1.reshape(2, w1, n_rhs)[::-1]
+    x1 = dot_pair(got, 2 * n_rhs, 2 * n_rhs + head, y1[:, :head])
+    x1 = x1 + dot_pair(moved, n_rhs + head, n_rhs + head + n_rhs, jnp.concatenate([blank, y1[:, head:]], 1))
     x1 = x1.astype(bf).reshape(half, 2, WIN, n_rhs)
     x1 = pack(x1[:, 0], x1[:, 1], low)
     x1, y0 = lax.optimization_barrier((jnp.concatenate([x1[turn:], x1, x1[:turn]], 0), y0))

time: 211 us -> 211 us (level)
  no operation moved by 1% of the time
where the time goes in v12:
time: 211 us; the launch traced here: 210 us
  blocking collectives  174 us (82%)
  starting transfers between devices  20.7 us (10%)
  local copies, waits for them, and re-layouts  4.22 us (2%)
  other arithmetic  3.17 us (2%)
  waiting for transfers between devices  3.16 us (1%)
  between operations  2.83 us (1%)
  matrix products  2.23 us (1%)
    all_to_all x6, blocking collectives, a2a_leaf(): return lax.all_to_all(v, 'leaf', 0, 0, axis_index_groups=groups)  97.2 us
    all_to_all x5, blocking collectives, a2a_plane(): return lax.all_to_all(v, ('leaf', 'front'), 0, 0, axis_index_groups=plane)  76.5 us
    all_to_all x1, starting transfers between devices, a2a_plane(): return lax.all_to_all(v, ('leaf', 'front'), 0, 0, axis_index_groups=plane)  12.1 us
    ppermute x1, starting transfers between devices, body(): other = lax.ppermute(both, 'leaf', swap)  6.36 us
  transfers between devices with their start and end apart: 3, of which 3 were waited for; matrix products, arithmetic and copies ran while one was open for 1% of the time, Pallas kernels for 0%

profile of v12, /device:TPU:1, one launch (start us, length us, event | category | flops | bytes accessed | tf_op | source)
XLA Modules:
  0.0 210.0 jit_solution(15989088692021693319)
XLA Ops:
  0.0 1.1 fusion.60
  1.1 0.7 pad_maximum_fusion.4
  1.8 12.1 %all-to-all-start = ((bf16[32,24,128]{2,1,0:T(8,128)(2,1)}), bf16[32,24,128]{2,1,0:T(8,128)(2,1)S(1)}, u32[]{:S(2)}, u32[]{:S(2)}) async-start(bf16[32,24,128]{2,1,0:T(8,128)(2,1)} %pad_maximum_fusion.4), calls=%async_computation | async-start | bytes 393216 | tf_op jit(solution)/shard_map/all_to_all | solution.py:44
  13.9 0.6 fusion.66
  16.4 0.1 iota_compare_fusion.1
  16.5 0.0 slice-start.1
  16.5 0.3 copy.41
  16.8 0.7 slice-done.1
  17.5 0.3 copy.42
  17.8 0.1 fusion.56
  18.0 0.1 fusion.15
  18.1 1.2 all-to-all-done
  19.4 16.4 %all_to_all.60 = bf16[8,40,128]{2,1,0:T(8,128)(2,1)S(1)} all-to-all(bf16[8,40,128]{2,1,0:T(8,128)(2,1)S(1)} %maximum_select_fusion.5), channel_id=1, replica_groups={{96,128,160,192,224,0,32,64},{112,144,176,208,240,16,48,80},{352,384,41..., dimensions={0} | all-to-all | bytes 163840 | tf_op jit(solution)/shard_map/all_to_all | solution.py:47
  35.9 0.1 fusion.45
  36.0 0.1 pad_maximum_fusion
  36.1 19.1 %all_to_all.61 = bf16[32,24,512]{2,1,0:T(8,128)(2,1)S(1)} all-to-all(bf16[32,24,512]{2,1,0:T(8,128)(2,1)S(1)} %pad_maximum_fusion), channel_id=1, replica_groups={{22,23,24,25,26,27,28,29,30,31,16,17,18,19,20,21,6,7,8,9,10,11,12,13,14..., dimensions={0} | all-to-all | bytes 1572864 | tf_op jit(solution)/shard_map/all_to_all | solution.py:44
  55.3 0.3 fusion.4
  55.7 0.2 copy.35
  55.9 0.4 fusion.3
  56.3 0.2 copy.34
  56.6 12.3 %all_to_all.62 = bf16[32,40,128]{2,1,0:T(8,128)(2,1)S(1)} all-to-all(bf16[32,40,128]{2,1,0:T(8,128)(2,1)S(1)} %bitcast.137), channel_id=1, replica_groups={{22,23,24,25,26,27,28,29,30,31,16,17,18,19,20,21,6,7,8,9,10,11,12,13,14..., dimensions={0} | all-to-all | bytes 655360 | tf_op jit(solution)/shard_map/all_to_all | solution.py:44
  68.9 18.8 %all_to_all.63 = bf16[16,40,128]{2,1,0:T(8,128)(2,1)S(1)} all-to-all(bf16[16,40,128]{2,1,0:T(8,128)(2,1)S(1)} %add_convert_fusion), channel_id=1, replica_groups={{192,224,256,288,320,352,384,416,448,480,0,32,64,96,128,160},{208,240,2..., dimensions={0} | all-to-all | bytes 327680 | tf_op jit(solution)/shard_map/all_to_all | solution.py:47
  87.9 0.1 fusion.29
  87.9 0.1 fusion.31
  88.2 0.1 fusion.34
  88.3 13.0 %all_to_all.64 = bf16[32,24,128]{2,1,0:T(8,128)(2,1)S(1)} all-to-all(bf16[32,24,128]{2,1,0:T(8,128)(2,1)S(1)} %broadcast_in_dim.164), channel_id=1, replica_groups={{22,23,24,25,26,27,28,29,30,31,16,17,18,19,20,21,6,7,8,9,10,11,12,13,14..., dimensions={0} | all-to-all | bytes 393216 | tf_op jit(solution)/shard_map/all_to_all | solution.py:44
  101.4 0.3 fusion.7
  101.7 0.1 fusion.21
  101.8 18.4 %all_to_all.65 = bf16[16,40,128]{2,1,0:T(8,128)(2,1)S(1)} all-to-all(bf16[16,40,128]{2,1,0:T(8,128)(2,1)S(1)} %fusion.21), channel_id=1, replica_groups={{192,224,256,288,320,352,384,416,448,480,0,32,64,96,128,160},{208,240,2..., dimensions={0} | all-to-all | bytes 327680 | tf_op jit(solution)/shard_map/all_to_all | solution.py:47
  120.3 0.1 fusion.27
  120.4 0.1 pad_maximum_fusion.1
  120.5 19.1 %all_to_all.66 = bf16[32,24,512]{2,1,0:T(8,128)(2,1)S(1)} all-to-all(bf16[32,24,512]{2,1,0:T(8,128)(2,1)S(1)} %pad_maximum_fusion.1), channel_id=1, replica_groups={{22,23,24,25,26,27,28,29,30,31,16,17,18,19,20,21,6,7,8,9,10,11,12,13,14..., dimensions={0} | all-to-all | bytes 1572864 | tf_op jit(solution)/shard_map/all_to_all | solution.py:44
  139.8 0.2 convolution_bitcast_fusion.4
  140.0 0.3 fusion.6
  140.4 18.2 %all_to_all.67 = bf16[16,40,128]{2,1,0:T(8,128)(2,1)S(1)} all-to-all(bf16[16,40,128]{2,1,0:T(8,128)(2,1)S(1)} %pad_maximum_fusion.7), channel_id=1, replica_groups={{192,224,256,288,320,352,384,416,448,480,0,32,64,96,128,160},{208,240,2..., dimensions={0} | all-to-all | bytes 327680 | tf_op jit(solution)/shard_map/all_to_all | solution.py:47
  158.7 0.3 convolution_bitcast_fusion.1
  159.1 0.1 fusion.44
  159.2 12.9 %all_to_all.68 = bf16[32,24,128]{2,1,0:T(8,128)(2,1)S(1)} all-to-all(bf16[32,24,128]{2,1,0:T(8,128)(2,1)S(1)} %bitcast.142), channel_id=1, replica_groups={{22,23,24,25,26,27,28,29,30,31,16,17,18,19,20,21,6,7,8,9,10,11,12,13,14..., dimensions={0} | all-to-all | bytes 393216 | tf_op jit(solution)/shard_map/all_to_all | solution.py:44
  172.2 0.4 fusion
  172.6 0.2 copy.38
  172.9 2.3 %collective-permute-start = (bf16[8,80,128]{2,1,0:T(8,128)(2,1)S(1)}, bf16[8,80,128]{2,1,0:T(8,128)(2,1)S(1)}, u32[]{:S(2)}, u32[]{:S(2)}) collective-permute-start(bf16[8,80,128]{2,1,0:T(8,128)(2,1)S(1)} %pad_maximum_fusion.9), channel_id=1, source_target_pairs={{0,16},{16,0},{32,48},{48,32},{64,80},{80,64},{96,112},{112,96},{1... | collective-permute-start | bytes 491528 | tf_op jit(solution)/shard_map/ppermute | solution.py:181
  175.2 1.0 collective-permute-done
  176.3 12.4 %all_to_all.69 = bf16[8,80,128]{2,1,0:T(8,128)(2,1)S(1)} all-to-all(bf16[8,80,128]{2,1,0:T(8,128)(2,1)S(1)} %pad_maximum_fusion.10), channel_id=1, replica_groups={{128,0,32,64,96,160,192,224},{144,16,48,80,112,176,208,240},{384,256,28..., dimensions={0} | all-to-all | bytes 327680 | tf_op jit(solution)/shard_map/all_to_all | solution.py:47
  188.7 0.1 fusion.25
  188.8 13.0 %all_to_all.70 = bf16[8,2,40,128]{3,2,1,0:T(8,128)(2,1)S(1)} all-to-all(bf16[8,2,40,128]{3,2,1,0:T(8,128)(2,1)S(1)} %broadcast_in_dim.175), channel_id=1, replica_groups={{128,0,32,64,96,160,192,224},{144,16,48,80,112,176,208,240},{384,256,28..., dimensions={0} | all-to-all | bytes 327680 | tf_op jit(solution)/shard_map/all_to_all | solution.py:47
  201.8 6.4 %collective-permute-start.1 = (bf16[2,320,128]{2,1,0:T(8,128)(2,1)S(1)}, bf16[2,320,128]{2,1,0:T(8,128)(2,1)S(1)}, u32[]{:S(2)}, u32[]{:S(2)}) collective-permute-start(bf16[2,320,128]{2,1,0:T(8,128)(2,1)S(1)} %bitcast.151), channel_id=1, source_target_pairs={{0,16},{16,0},{32,48},{48,32},{64,80},{80,64},{96,112},{112,96},{1... | collective-permute-start | bytes 491528 | tf_op jit(solution)/shard_map/ppermute | solution.py:190
  208.2 1.0 collective-permute-done.1
  209.2 0.8 fusion.18
  (107 shorter events, 1.4 us)
Async XLA Ops:
  0.0 55.9 %copy-start = (bf16[1,640,640]{2,1,0:T(8,128)(2,1)S(1)}, bf16[1,640,640]{2,1,0:T(8,128)(2,1)}, u32[]{:S(2)}) copy-start(bf16[1,640,640]{2,1,0:T(8,128)(2,1)} %param.9) | copy-start | bytes 2457604
  0.0 13.9 %copy-start.4 = (s32[2,32]{1,0:T(2,128)S(1)}, s32[2,32]{1,0:T(2,128)}, u32[]{:S(2)}) copy-start(s32[2,32]{1,0:T(2,128)} %param.7) | copy-start | bytes 772
  0.0 16.5 %slice-start = ((bf16[1,640,960]{1,2,0:T(8,128)(2,1)}), bf16[1,640,320]{1,2,0:T(8,128)(2,1)S(1)}, s32[]{:S(2)}) async-start(bf16[1,640,960]{1,2,0:T(8,128)(2,1)} %param.8), calls=%async_computation.12 | async-start | bytes 819200 | tf_op jit(solution)/shard_map/slice | solution.py:125
  1.8 17.5 %all-to-all-start = ((bf16[32,24,128]{2,1,0:T(8,128)(2,1)}), bf16[32,24,128]{2,1,0:T(8,128)(2,1)S(1)}, u32[]{:S(2)}, u32[]{:S(2)}) async-start(bf16[32,24,128]{2,1,0:T(8,128)(2,1)} %pad_maximum_fusion.4), calls=%async_computation | async-start | bytes 393216 | tf_op jit(solution)/shard_map/all_to_all | solution.py:44
  16.5 1.0 slice-start.1
  36.1 19.2 %copy-start.1 = (bf16[1,640,960]{1,2,0:T(8,128)(2,1)S(1)}, bf16[1,640,960]{1,2,0:T(8,128)(2,1)}, u32[]{:S(2)}) copy-start(bf16[1,640,960]{1,2,0:T(8,128)(2,1)} %param.8) | copy-start | bytes 3686404
  140.0 18.7 %copy-start.2 = (bf16[1,640,960]{1,2,0:T(8,128)(2,1)S(1)}, bf16[1,640,960]{1,2,0:T(8,128)(2,1)}, u32[]{:S(2)}) copy-start(bf16[1,640,960]{1,2,0:T(8,128)(2,1)} %param.10) | copy-start | bytes 3686404
  159.1 13.2 %copy-start.3 = (bf16[1,640,640]{2,1,0:T(8,128)(2,1)S(1)}, bf16[1,640,640]{2,1,0:T(8,128)(2,1)}, u32[]{:S(2)}) copy-start(bf16[1,640,640]{2,1,0:T(8,128)(2,1)} %param.11) | copy-start | bytes 2457604
  172.9 3.3 %collective-permute-start = (bf16[8,80,128]{2,1,0:T(8,128)(2,1)S(1)}, bf16[8,80,128]{2,1,0:T(8,128)(2,1)S(1)}, u32[]{:S(2)}, u32[]{:S(2)}) collective-permute-start(bf16[8,80,128]{2,1,0:T(8,128)(2,1)S(1)} %pad_maximum_fusion.9), channel_id=1, source_target_pairs={{0,16},{16,0},{32,48},{48,32},{64,80},{80,64},{96,112},{112,96},{1... | collective-permute-start | bytes 491528 | tf_op jit(solution)/shard_map/ppermute | solution.py:181
  201.8 7.4 %collective-permute-start.1 = (bf16[2,320,128]{2,1,0:T(8,128)(2,1)S(1)}, bf16[2,320,128]{2,1,0:T(8,128)(2,1)S(1)}, u32[]{:S(2)}, u32[]{:S(2)}) collective-permute-start(bf16[2,320,128]{2,1,0:T(8,128)(2,1)S(1)} %bitcast.151), channel_id=1, source_target_pairs={{0,16},{16,0},{32,48},{48,32},{64,80},{80,64},{96,112},{112,96},{1... | collective-permute-start | bytes 491528 | tf_op jit(solution)/shard_map/ppermute | solution.py:190

commit v13 on v12

--- a/solution.py
+++ b/solution.py
@@ -2,6 +2,7 @@
 import jax.numpy as jnp
 import numpy as np
 from jax import lax
+from jax.experimental.layout import Layout, with_layout_constraint
 from jax.sharding import PartitionSpec as P
 
 BLK = 128
@@ -102,7 +103,7 @@
         return jnp.where(keep[..., None], v, 0.0).astype(bf)
 
     def dot(a, b):
-        return jnp.dot(a, b, preferred_element_type=f32)
+        return with_layout_constraint(jnp.dot(a, b, preferred_element_type=f32), Layout((0, 1)))
 
     def dot_pair(mat, first, last, v):
         m = mat.reshape(2, height, mat.shape[-1])[:, :, first:last]

time: 211 us -> 210 us (level)
  no operation moved by 1% of the time
where the time goes in v13:
time: 210 us
  blocking collectives  174 us (83%)
  starting transfers between devices  20.7 us (10%)
  local copies, waits for them, and re-layouts  3.73 us (2%)
  other arithmetic  3.17 us (2%)
  waiting for transfers between devices  3.16 us (2%)
  between operations  2.83 us (1%)
  matrix products  2.44 us (1%)
    all_to_all x6, blocking collectives, a2a_leaf(): return lax.all_to_all(v, 'leaf', 0, 0, axis_index_groups=groups)  97.2 us
    all_to_all x5, blocking collectives, a2a_plane(): return lax.all_to_all(v, ('leaf', 'front'), 0, 0, axis_index_groups=plane)  76.5 us
    all_to_all x1, starting transfers between devices, a2a_plane(): return lax.all_to_all(v, ('leaf', 'front'), 0, 0, axis_index_groups=plane)  12.1 us
    ppermute x1, starting transfers between devices, body(): other = lax.ppermute(both, 'leaf', swap)  6.36 us
  transfers between devices with their start and end apart: 3, of which 3 were waited for; matrix products, arithmetic and copies ran while one was open for 1% of the time, Pallas kernels for 0%

profile of v13, /device:TPU:1, one launch (start us, length us, event | category | flops | bytes accessed | tf_op | source)
XLA Modules:
  0.0 209.8 jit_solution(18385037206020605504)
XLA Ops:
  0.0 1.1 fusion.60
  1.1 0.7 pad_maximum_fusion.4
  1.8 12.1 %all-to-all-start = ((bf16[32,24,128]{2,1,0:T(8,128)(2,1)}), bf16[32,24,128]{2,1,0:T(8,128)(2,1)S(1)}, u32[]{:S(2)}, u32[]{:S(2)}) async-start(bf16[32,24,128]{2,1,0:T(8,128)(2,1)} %pad_maximum_fusion.4), calls=%async_computation | async-start | bytes 393216 | tf_op jit(solution)/shard_map/all_to_all | solution.py:45
  13.9 0.6 fusion.66
  16.4 0.1 iota_compare_fusion.1
  16.5 0.0 slice-start.1
  16.5 0.3 copy.29
  16.8 0.7 slice-done.1
  17.5 0.3 copy.30
  17.8 0.1 fusion.56
  18.0 0.1 fusion.15
  18.1 1.2 all-to-all-done
  19.4 16.4 %all_to_all.60 = bf16[8,40,128]{2,1,0:T(8,128)(2,1)S(1)} all-to-all(bf16[8,40,128]{2,1,0:T(8,128)(2,1)S(1)} %maximum_select_fusion.5), channel_id=1, replica_groups={{96,128,160,192,224,0,32,64},{112,144,176,208,240,16,48,80},{352,384,41..., dimensions={0} | all-to-all | bytes 163840 | tf_op jit(solution)/shard_map/all_to_all | solution.py:48
  35.9 0.1 fusion.45
  36.0 0.1 pad_maximum_fusion
  36.1 0.0 copy-start.1
  36.1 19.1 %all_to_all.61 = bf16[32,24,512]{2,1,0:T(8,128)(2,1)S(1)} all-to-all(bf16[32,24,512]{2,1,0:T(8,128)(2,1)S(1)} %pad_maximum_fusion), channel_id=1, replica_groups={{22,23,24,25,26,27,28,29,30,31,16,17,18,19,20,21,6,7,8,9,10,11,12,13,14..., dimensions={0} | all-to-all | bytes 1572864 | tf_op jit(solution)/shard_map/all_to_all | solution.py:45
  55.3 0.5 fusion.3
  55.8 0.4 fusion.4
  56.3 12.3 %all_to_all.62 = bf16[32,40,128]{2,1,0:T(8,128)(2,1)S(1)} all-to-all(bf16[32,40,128]{2,1,0:T(8,128)(2,1)S(1)} %bitcast.139), channel_id=1, replica_groups={{22,23,24,25,26,27,28,29,30,31,16,17,18,19,20,21,6,7,8,9,10,11,12,13,14..., dimensions={0} | all-to-all | bytes 655360 | tf_op jit(solution)/shard_map/all_to_all | solution.py:45
  68.7 18.8 %all_to_all.63 = bf16[16,40,128]{2,1,0:T(8,128)(2,1)S(1)} all-to-all(bf16[16,40,128]{2,1,0:T(8,128)(2,1)S(1)} %add_convert_fusion), channel_id=1, replica_groups={{192,224,256,288,320,352,384,416,448,480,0,32,64,96,128,160},{208,240,2..., dimensions={0} | all-to-all | bytes 327680 | tf_op jit(solution)/shard_map/all_to_all | solution.py:48
  87.6 0.1 fusion.29
  87.7 0.1 fusion.31
  87.9 0.1 fusion.34
  88.1 13.0 %all_to_all.64 = bf16[32,24,128]{2,1,0:T(8,128)(2,1)S(1)} all-to-all(bf16[32,24,128]{2,1,0:T(8,128)(2,1)S(1)} %broadcast_in_dim.164), channel_id=1, replica_groups={{22,23,24,25,26,27,28,29,30,31,16,17,18,19,20,21,6,7,8,9,10,11,12,13,14..., dimensions={0} | all-to-all | bytes 393216 | tf_op jit(solution)/shard_map/all_to_all | solution.py:45
  101.2 0.3 fusion.7
  101.5 0.1 fusion.21
  101.6 18.4 %all_to_all.65 = bf16[16,40,128]{2,1,0:T(8,128)(2,1)S(1)} all-to-all(bf16[16,40,128]{2,1,0:T(8,128)(2,1)S(1)} %fusion.21), channel_id=1, replica_groups={{192,224,256,288,320,352,384,416,448,480,0,32,64,96,128,160},{208,240,2..., dimensions={0} | all-to-all | bytes 327680 | tf_op jit(solution)/shard_map/all_to_all | solution.py:48
  120.0 0.1 fusion.27
  120.2 0.1 pad_maximum_fusion.1
  120.3 19.1 %all_to_all.66 = bf16[32,24,512]{2,1,0:T(8,128)(2,1)S(1)} all-to-all(bf16[32,24,512]{2,1,0:T(8,128)(2,1)S(1)} %pad_maximum_fusion.1), channel_id=1, replica_groups={{22,23,24,25,26,27,28,29,30,31,16,17,18,19,20,21,6,7,8,9,10,11,12,13,14..., dimensions={0} | all-to-all | bytes 1572864 | tf_op jit(solution)/shard_map/all_to_all | solution.py:45
  139.5 0.2 convolution_bitcast_fusion.6
  139.8 0.0 copy-start.2
  139.8 0.3 fusion.6
  140.2 18.2 %all_to_all.67 = bf16[16,40,128]{2,1,0:T(8,128)(2,1)S(1)} all-to-all(bf16[16,40,128]{2,1,0:T(8,128)(2,1)S(1)} %pad_maximum_fusion.7), channel_id=1, replica_groups={{192,224,256,288,320,352,384,416,448,480,0,32,64,96,128,160},{208,240,2..., dimensions={0} | all-to-all | bytes 327680 | tf_op jit(solution)/shard_map/all_to_all | solution.py:48
  158.5 0.5 convolution_bitcast_fusion.2
  159.0 0.0 copy-start.3
  159.0 0.1 fusion.44
  159.1 12.9 %all_to_all.68 = bf16[32,24,128]{2,1,0:T(8,128)(2,1)S(1)} all-to-all(bf16[32,24,128]{2,1,0:T(8,128)(2,1)S(1)} %bitcast.144), channel_id=1, replica_groups={{22,23,24,25,26,27,28,29,30,31,16,17,18,19,20,21,6,7,8,9,10,11,12,13,14..., dimensions={0} | all-to-all | bytes 393216 | tf_op jit(solution)/shard_map/all_to_all | solution.py:45
  172.2 0.4 fusion
  172.6 2.3 %collective-permute-start = (bf16[8,80,128]{2,1,0:T(8,128)(2,1)S(1)}, bf16[8,80,128]{2,1,0:T(8,128)(2,1)S(1)}, u32[]{:S(2)}, u32[]{:S(2)}) collective-permute-start(bf16[8,80,128]{2,1,0:T(8,128)(2,1)S(1)} %pad_maximum_fusion.9), channel_id=1, source_target_pairs={{0,16},{16,0},{32,48},{48,32},{64,80},{80,64},{96,112},{112,96},{1... | collective-permute-start | bytes 491528 | tf_op jit(solution)/shard_map/ppermute | solution.py:182
  174.9 1.0 collective-permute-done
  176.0 12.4 %all_to_all.69 = bf16[8,80,128]{2,1,0:T(8,128)(2,1)S(1)} all-to-all(bf16[8,80,128]{2,1,0:T(8,128)(2,1)S(1)} %pad_maximum_fusion.10), channel_id=1, replica_groups={{128,0,32,64,96,160,192,224},{144,16,48,80,112,176,208,240},{384,256,28..., dimensions={0} | all-to-all | bytes 327680 | tf_op jit(solution)/shard_map/all_to_all | solution.py:48
  188.4 0.1 fusion.25
  188.6 13.0 %all_to_all.70 = bf16[8,2,40,128]{3,2,1,0:T(8,128)(2,1)S(1)} all-to-all(bf16[8,2,40,128]{3,2,1,0:T(8,128)(2,1)S(1)} %broadcast_in_dim.175), channel_id=1, replica_groups={{128,0,32,64,96,160,192,224},{144,16,48,80,112,176,208,240},{384,256,28..., dimensions={0} | all-to-all | bytes 327680 | tf_op jit(solution)/shard_map/all_to_all | solution.py:48
  201.6 6.4 %collective-permute-start.1 = (bf16[2,320,128]{2,1,0:T(8,128)(2,1)S(1)}, bf16[2,320,128]{2,1,0:T(8,128)(2,1)S(1)}, u32[]{:S(2)}, u32[]{:S(2)}) collective-permute-start(bf16[2,320,128]{2,1,0:T(8,128)(2,1)S(1)} %bitcast.153), channel_id=1, source_target_pairs={{0,16},{16,0},{32,48},{48,32},{64,80},{80,64},{96,112},{112,96},{1... | collective-permute-start | bytes 491528 | tf_op jit(solution)/shard_map/ppermute | solution.py:191
  208.0 1.0 collective-permute-done.1
  209.0 0.8 fusion.18
  (104 shorter events, 1.4 us)
Async XLA Ops:
  0.0 55.8 %copy-start = (bf16[1,640,640]{2,1,0:T(8,128)(2,1)S(1)}, bf16[1,640,640]{2,1,0:T(8,128)(2,1)}, u32[]{:S(2)}) copy-start(bf16[1,640,640]{2,1,0:T(8,128)(2,1)} %param.9) | copy-start | bytes 2457604
  0.0 13.9 %copy-start.4 = (s32[2,32]{1,0:T(2,128)S(1)}, s32[2,32]{1,0:T(2,128)}, u32[]{:S(2)}) copy-start(s32[2,32]{1,0:T(2,128)} %param.7) | copy-start | bytes 772
  0.0 16.5 %slice-start = ((bf16[1,640,960]{1,2,0:T(8,128)(2,1)}), bf16[1,640,320]{1,2,0:T(8,128)(2,1)S(1)}, s32[]{:S(2)}) async-start(bf16[1,640,960]{1,2,0:T(8,128)(2,1)} %param.8), calls=%async_computation.12 | async-start | bytes 819200 | tf_op jit(solution)/shard_map/slice | solution.py:126
  1.8 17.5 %all-to-all-start = ((bf16[32,24,128]{2,1,0:T(8,128)(2,1)}), bf16[32,24,128]{2,1,0:T(8,128)(2,1)S(1)}, u32[]{:S(2)}, u32[]{:S(2)}) async-start(bf16[32,24,128]{2,1,0:T(8,128)(2,1)} %pad_maximum_fusion.4), calls=%async_computation | async-start | bytes 393216 | tf_op jit(solution)/shard_map/all_to_all | solution.py:45
  16.5 1.0 slice-start.1
  36.1 19.2 %copy-start.1 = (bf16[1,640,960]{1,2,0:T(8,128)(2,1)S(1)}, bf16[1,640,960]{1,2,0:T(8,128)(2,1)}, u32[]{:S(2)}) copy-start(bf16[1,640,960]{1,2,0:T(8,128)(2,1)} %param.8) | copy-start | bytes 3686404
  139.8 18.7 %copy-start.2 = (bf16[1,640,960]{1,2,0:T(8,128)(2,1)S(1)}, bf16[1,640,960]{1,2,0:T(8,128)(2,1)}, u32[]{:S(2)}) copy-start(bf16[1,640,960]{1,2,0:T(8,128)(2,1)} %param.10) | copy-start | bytes 3686404
  159.0 13.2 %copy-start.3 = (bf16[1,640,640]{2,1,0:T(8,128)(2,1)S(1)}, bf16[1,640,640]{2,1,0:T(8,128)(2,1)}, u32[]{:S(2)}) copy-start(bf16[1,640,640]{2,1,0:T(8,128)(2,1)} %param.11) | copy-start | bytes 2457604
  172.6 3.3 %collective-permute-start = (bf16[8,80,128]{2,1,0:T(8,128)(2,1)S(1)}, bf16[8,80,128]{2,1,0:T(8,128)(2,1)S(1)}, u32[]{:S(2)}, u32[]{:S(2)}) collective-permute-start(bf16[8,80,128]{2,1,0:T(8,128)(2,1)S(1)} %pad_maximum_fusion.9), channel_id=1, source_target_pairs={{0,16},{16,0},{32,48},{48,32},{64,80},{80,64},{96,112},{112,96},{1... | collective-permute-start | bytes 491528 | tf_op jit(solution)/shard_map/ppermute | solution.py:182
  201.6 7.4 %collective-permute-start.1 = (bf16[2,320,128]{2,1,0:T(8,128)(2,1)S(1)}, bf16[2,320,128]{2,1,0:T(8,128)(2,1)S(1)}, u32[]{:S(2)}, u32[]{:S(2)}) collective-permute-start(bf16[2,320,128]{2,1,0:T(8,128)(2,1)S(1)} %bitcast.153), channel_id=1, source_target_pairs={{0,16},{16,0},{32,48},{48,32},{64,80},{80,64},{96,112},{112,96},{1... | collective-permute-start | bytes 491528 | tf_op jit(solution)/shard_map/ppermute | solution.py:191

commit v14 on v12

--- a/solution.py
+++ b/solution.py
@@ -27,7 +27,7 @@
     z, core = leaf_id // 2, leaf_id % 2
     node, z8 = z // half, z % half
 
-    shift = half - 2
+    shift = half
     turn = shift // 2
     fronts = [(k + shift) % n_front for k in range(n_front)]
     planes = [(k + shift) % n_z for k in range(n_z)]

time: 211 us -> 212 us (level)
    all_to_all x6, blocking collectives: 97.2 us -> 103 us  [a2a_leaf(): return lax.all_to_all(v, 'leaf', 0, 0, axis_index_groups=groups)]
    all_to_all x5, blocking collectives: 76.5 us -> 72.9 us  [a2a_plane(): return lax.all_to_all(v, ('leaf', 'front'), 0, 0, axis_index_groups=plane)]
where the time goes in v14:
time: 212 us; the launch traced here: 211 us
  blocking collectives  176 us (83%)
  starting transfers between devices  19.8 us (9%)
  local copies, waits for them, and re-layouts  4.26 us (2%)
  waiting for transfers between devices  3.28 us (2%)
  other arithmetic  3.17 us (1%)
  between operations  2.92 us (1%)
  matrix products  2.24 us (1%)
    all_to_all x6, blocking collectives, a2a_leaf(): return lax.all_to_all(v, 'leaf', 0, 0, axis_index_groups=groups)  103 us
    all_to_all x5, blocking collectives, a2a_plane(): return lax.all_to_all(v, ('leaf', 'front'), 0, 0, axis_index_groups=plane)  72.9 us
    all_to_all x1, starting transfers between devices, a2a_plane(): return lax.all_to_all(v, ('leaf', 'front'), 0, 0, axis_index_groups=plane)  11.2 us
    ppermute x1, starting transfers between devices, body(): other = lax.ppermute(both, 'leaf', swap)  6.36 us
  transfers between devices with their start and end apart: 3, of which 3 were waited for; matrix products, arithmetic and copies ran while one was open for 1% of the time, Pallas kernels for 0%

profile of v14, /device:TPU:1, one launch (start us, length us, event | category | flops | bytes accessed | tf_op | source)
XLA Modules:
  0.0 211.3 jit_solution(8188841610587363683)
XLA Ops:
  0.0 1.1 fusion.60
  1.1 0.7 pad_maximum_fusion.4
  1.8 11.2 %all-to-all-start = ((bf16[32,24,128]{2,1,0:T(8,128)(2,1)}), bf16[32,24,128]{2,1,0:T(8,128)(2,1)S(1)}, u32[]{:S(2)}, u32[]{:S(2)}) async-start(bf16[32,24,128]{2,1,0:T(8,128)(2,1)} %pad_maximum_fusion.4), calls=%async_computation | async-start | bytes 393216 | tf_op jit(solution)/shard_map/all_to_all | solution.py:44
  13.0 0.7 fusion.67
  15.7 0.1 iota_compare_fusion.1
  15.8 0.0 slice-start.1
  15.8 0.3 copy.41
  16.1 0.7 slice-done.1
  16.8 0.3 copy.42
  17.1 0.1 fusion.56
  17.2 0.1 fusion.15
  17.4 1.3 all-to-all-done
  18.8 15.2 %all_to_all.60 = bf16[8,40,128]{2,1,0:T(8,128)(2,1)S(1)} all-to-all(bf16[8,40,128]{2,1,0:T(8,128)(2,1)S(1)} %maximum_select_fusion.5), channel_id=1, replica_groups={{128,160,192,224,0,32,64,96},{144,176,208,240,16,48,80,112},{384,416,44..., dimensions={0} | all-to-all | bytes 163840 | tf_op jit(solution)/shard_map/all_to_all | solution.py:47
  34.0 0.1 fusion.46
  34.2 0.1 pad_maximum_fusion
  34.2 18.9 %all_to_all.61 = bf16[32,24,512]{2,1,0:T(8,128)(2,1)S(1)} all-to-all(bf16[32,24,512]{2,1,0:T(8,128)(2,1)S(1)} %pad_maximum_fusion), channel_id=1, replica_groups={{24,25,26,27,28,29,30,31,16,17,18,19,20,21,22,23,8,9,10,11,12,13,14,15,..., dimensions={0} | all-to-all | bytes 1572864 | tf_op jit(solution)/shard_map/all_to_all | solution.py:44
  53.3 0.3 fusion.4
  53.6 0.2 copy.35
  53.8 0.4 fusion.3
  54.2 0.2 copy.34
  54.5 12.8 %all_to_all.62 = bf16[32,40,128]{2,1,0:T(8,128)(2,1)S(1)} all-to-all(bf16[32,40,128]{2,1,0:T(8,128)(2,1)S(1)} %bitcast.137), channel_id=1, replica_groups={{24,25,26,27,28,29,30,31,16,17,18,19,20,21,22,23,8,9,10,11,12,13,14,15,..., dimensions={0} | all-to-all | bytes 655360 | tf_op jit(solution)/shard_map/all_to_all | solution.py:44
  67.4 21.5 %all_to_all.63 = bf16[16,40,128]{2,1,0:T(8,128)(2,1)S(1)} all-to-all(bf16[16,40,128]{2,1,0:T(8,128)(2,1)S(1)} %add_convert_fusion), channel_id=1, replica_groups={{256,288,320,352,384,416,448,480,0,32,64,96,128,160,192,224},{272,304,3..., dimensions={0} | all-to-all | bytes 327680 | tf_op jit(solution)/shard_map/all_to_all | solution.py:47
  89.0 0.1 fusion.30
  89.1 0.1 fusion.32
  89.2 0.1 fusion.35
  89.4 11.7 %all_to_all.64 = bf16[32,24,128]{2,1,0:T(8,128)(2,1)S(1)} all-to-all(bf16[32,24,128]{2,1,0:T(8,128)(2,1)S(1)} %broadcast_in_dim.158), channel_id=1, replica_groups={{24,25,26,27,28,29,30,31,16,17,18,19,20,21,22,23,8,9,10,11,12,13,14,15,..., dimensions={0} | all-to-all | bytes 393216 | tf_op jit(solution)/shard_map/all_to_all | solution.py:44
  101.2 0.3 fusion.7
  101.5 0.1 fusion.21
  101.6 19.4 %all_to_all.65 = bf16[16,40,128]{2,1,0:T(8,128)(2,1)S(1)} all-to-all(bf16[16,40,128]{2,1,0:T(8,128)(2,1)S(1)} %fusion.21), channel_id=1, replica_groups={{256,288,320,352,384,416,448,480,0,32,64,96,128,160,192,224},{272,304,3..., dimensions={0} | all-to-all | bytes 327680 | tf_op jit(solution)/shard_map/all_to_all | solution.py:47
  121.2 0.1 fusion.28
  121.3 0.1 pad_maximum_fusion.1
  121.4 17.6 %all_to_all.66 = bf16[32,24,512]{2,1,0:T(8,128)(2,1)S(1)} all-to-all(bf16[32,24,512]{2,1,0:T(8,128)(2,1)S(1)} %pad_maximum_fusion.1), channel_id=1, replica_groups={{24,25,26,27,28,29,30,31,16,17,18,19,20,21,22,23,8,9,10,11,12,13,14,15,..., dimensions={0} | all-to-all | bytes 1572864 | tf_op jit(solution)/shard_map/all_to_all | solution.py:44
  139.1 0.2 convolution_bitcast_fusion.4
  139.3 0.3 fusion.6
  139.7 19.4 %all_to_all.67 = bf16[16,40,128]{2,1,0:T(8,128)(2,1)S(1)} all-to-all(bf16[16,40,128]{2,1,0:T(8,128)(2,1)S(1)} %pad_maximum_fusion.7), channel_id=1, replica_groups={{256,288,320,352,384,416,448,480,0,32,64,96,128,160,192,224},{272,304,3..., dimensions={0} | all-to-all | bytes 327680 | tf_op jit(solution)/shard_map/all_to_all | solution.py:47
  159.2 0.3 convolution_bitcast_fusion.1
  159.6 0.1 fusion.45
  159.7 11.9 %all_to_all.68 = bf16[32,24,128]{2,1,0:T(8,128)(2,1)S(1)} all-to-all(bf16[32,24,128]{2,1,0:T(8,128)(2,1)S(1)} %bitcast.142), channel_id=1, replica_groups={{24,25,26,27,28,29,30,31,16,17,18,19,20,21,22,23,8,9,10,11,12,13,14,15,..., dimensions={0} | all-to-all | bytes 393216 | tf_op jit(solution)/shard_map/all_to_all | solution.py:44
  171.7 0.4 fusion
  172.1 0.2 copy.38
  172.3 2.3 %collective-permute-start = (bf16[8,80,128]{2,1,0:T(8,128)(2,1)S(1)}, bf16[8,80,128]{2,1,0:T(8,128)(2,1)S(1)}, u32[]{:S(2)}, u32[]{:S(2)}) collective-permute-start(bf16[8,80,128]{2,1,0:T(8,128)(2,1)S(1)} %pad_maximum_fusion.9), channel_id=1, source_target_pairs={{0,16},{16,0},{32,48},{48,32},{64,80},{80,64},{96,112},{112,96},{1... | collective-permute-start | bytes 491528 | tf_op jit(solution)/shard_map/ppermute | solution.py:181
  174.6 1.0 collective-permute-done
  175.7 14.2 %all_to_all.69 = bf16[8,80,128]{2,1,0:T(8,128)(2,1)S(1)} all-to-all(bf16[8,80,128]{2,1,0:T(8,128)(2,1)S(1)} %pad_maximum_fusion.10), channel_id=1, replica_groups={{128,0,32,64,96,160,192,224},{144,16,48,80,112,176,208,240},{384,256,28..., dimensions={0} | all-to-all | bytes 327680 | tf_op jit(solution)/shard_map/all_to_all | solution.py:47
  189.9 0.1 fusion.26
  190.1 13.0 %all_to_all.70 = bf16[8,2,40,128]{3,2,1,0:T(8,128)(2,1)S(1)} all-to-all(bf16[8,2,40,128]{3,2,1,0:T(8,128)(2,1)S(1)} %broadcast_in_dim.168), channel_id=1, replica_groups={{128,0,32,64,96,160,192,224},{144,16,48,80,112,176,208,240},{384,256,28..., dimensions={0} | all-to-all | bytes 327680 | tf_op jit(solution)/shard_map/all_to_all | solution.py:47
  203.1 6.4 %collective-permute-start.1 = (bf16[2,320,128]{2,1,0:T(8,128)(2,1)S(1)}, bf16[2,320,128]{2,1,0:T(8,128)(2,1)S(1)}, u32[]{:S(2)}, u32[]{:S(2)}) collective-permute-start(bf16[2,320,128]{2,1,0:T(8,128)(2,1)S(1)} %bitcast.151), channel_id=1, source_target_pairs={{0,16},{16,0},{32,48},{48,32},{64,80},{80,64},{96,112},{112,96},{1... | collective-permute-start | bytes 491528 | tf_op jit(solution)/shard_map/ppermute | solution.py:190
  209.5 1.0 collective-permute-done.1
  210.5 0.8 fusion.18
  (103 shorter events, 1.4 us)
Async XLA Ops:
  0.0 53.8 %copy-start = (bf16[1,640,640]{2,1,0:T(8,128)(2,1)S(1)}, bf16[1,640,640]{2,1,0:T(8,128)(2,1)}, u32[]{:S(2)}) copy-start(bf16[1,640,640]{2,1,0:T(8,128)(2,1)} %param.9) | copy-start | bytes 2457604
  0.0 13.0 %copy-start.4 = (s32[2,32]{1,0:T(2,128)S(1)}, s32[2,32]{1,0:T(2,128)}, u32[]{:S(2)}) copy-start(s32[2,32]{1,0:T(2,128)} %param.7) | copy-start | bytes 772
  0.0 15.8 %slice-start = ((bf16[1,640,960]{1,2,0:T(8,128)(2,1)}), bf16[1,640,320]{1,2,0:T(8,128)(2,1)S(1)}, s32[]{:S(2)}) async-start(bf16[1,640,960]{1,2,0:T(8,128)(2,1)} %param.8), calls=%async_computation.12 | async-start | bytes 819200 | tf_op jit(solution)/shard_map/slice | solution.py:125
  1.8 16.9 %all-to-all-start = ((bf16[32,24,128]{2,1,0:T(8,128)(2,1)}), bf16[32,24,128]{2,1,0:T(8,128)(2,1)S(1)}, u32[]{:S(2)}, u32[]{:S(2)}) async-start(bf16[32,24,128]{2,1,0:T(8,128)(2,1)} %pad_maximum_fusion.4), calls=%async_computation | async-start | bytes 393216 | tf_op jit(solution)/shard_map/all_to_all | solution.py:44
  15.8 1.0 slice-start.1
  34.2 19.0 %copy-start.1 = (bf16[1,640,960]{1,2,0:T(8,128)(2,1)S(1)}, bf16[1,640,960]{1,2,0:T(8,128)(2,1)}, u32[]{:S(2)}) copy-start(bf16[1,640,960]{1,2,0:T(8,128)(2,1)} %param.8) | copy-start | bytes 3686404
  139.3 19.9 %copy-start.2 = (bf16[1,640,960]{1,2,0:T(8,128)(2,1)S(1)}, bf16[1,640,960]{1,2,0:T(8,128)(2,1)}, u32[]{:S(2)}) copy-start(bf16[1,640,960]{1,2,0:T(8,128)(2,1)} %param.10) | copy-start | bytes 3686404
  159.6 12.1 %copy-start.3 = (bf16[1,640,640]{2,1,0:T(8,128)(2,1)S(1)}, bf16[1,640,640]{2,1,0:T(8,128)(2,1)}, u32[]{:S(2)}) copy-start(bf16[1,640,640]{2,1,0:T(8,128)(2,1)} %param.11) | copy-start | bytes 2457604
  172.3 3.3 %collective-permute-start = (bf16[8,80,128]{2,1,0:T(8,128)(2,1)S(1)}, bf16[8,80,128]{2,1,0:T(8,128)(2,1)S(1)}, u32[]{:S(2)}, u32[]{:S(2)}) collective-permute-start(bf16[8,80,128]{2,1,0:T(8,128)(2,1)S(1)} %pad_maximum_fusion.9), channel_id=1, source_target_pairs={{0,16},{16,0},{32,48},{48,32},{64,80},{80,64},{96,112},{112,96},{1... | collective-permute-start | bytes 491528 | tf_op jit(solution)/shard_map/ppermute | solution.py:181
  203.1 7.4 %collective-permute-start.1 = (bf16[2,320,128]{2,1,0:T(8,128)(2,1)S(1)}, bf16[2,320,128]{2,1,0:T(8,128)(2,1)S(1)}, u32[]{:S(2)}, u32[]{:S(2)}) collective-permute-start(bf16[2,320,128]{2,1,0:T(8,128)(2,1)S(1)} %bitcast.151), channel_id=1, source_target_pairs={{0,16},{16,0},{32,48},{48,32},{64,80},{80,64},{96,112},{112,96},{1... | collective-permute-start | bytes 491528 | tf_op jit(solution)/shard_map/ppermute | solution.py:190
